TPU v7x, 32 devices: a whole 2x2x4 slice. The times are simulated.
32 devices in a mesh: beam: 4 (over x, core), det: 2 (over y), slab: 4 (over z).
Axes of the slice: x: 2, y: 2, z: 4, core: 2. Of those that a mesh axis runs over, the one named last changes fastest.
Arguments:
- concentration: float32 [4, 32, 1024, 256], P(None, 'slab', 'beam', 'det'), may hold values from 0.1 to 1
- cross_section: float32 [4, 16], replicated, may hold values from 0.2 to 2
- line_attenuation: float32 [4], replicated, may hold values from 0.5 to 2
- energy_index: int32 [4], replicated, may hold values from 0 to 15
- fan_offset: int32 [256], replicated, may hold values from 0 to 28
- fan_weight: int32 [256, 4], replicated, may hold values from 1 to 3
- measured: float32 [4, 256, 256], P(None, None, 'det'), may hold values from 0 to 6
Outputs:
- voxel_grad: float32 [4, 32, 1024, 256], P(None, 'slab', 'beam', 'det')
- residual: float32 [4, 256, 256], P(None, ('beam', 'slab'), 'det')
All inputs are finite; a program needn't handle non-finite values.
Results may differ from a plain program's by a relative error of at most 0.00013.
Values sent between devices are 32-bit elements; how exact they have to be, the bound alone decides.
No kernel may reach another device: no remote copies, remote signals or barrier semaphores. Data moves between devices by JAX's collectives and lax.ppermute only.
A program may use at most 128 MiB of HBM per device.

v0:
```python
import jax
import jax.numpy as jnp
from jax import lax
from jax.sharding import PartitionSpec as P


def entering(value, axis, join, neutral, backward):
    count, mine = (lax.axis_size(axis), lax.axis_index(axis))
    pieces = lax.all_gather(value, axis)
    if backward:
        pieces = pieces[::-1]
        mine = count - 1 - mine
    running = jnp.full_like(value, 0) + jnp.asarray(neutral, value.dtype)

    def lap(position, running):
        longer = join(running, pieces[position])
        return jnp.where(position < mine, longer, running)

    return lax.fori_loop(0, count - 1, lap, running)


def add_pair(earlier, later):
    return earlier + later


def fan_matrix(fan_offset, fan_weight, slices):
    taps = fan_offset[:, None] + jnp.arange(fan_weight.shape[1], dtype=jnp.int32)[None, :]
    match = (taps[:, :, None] == slices[None, None, :]).astype(jnp.float32)
    return jnp.sum(fan_weight.astype(jnp.float32)[:, :, None] * match, axis=1)


def shards(
    concentration, cross_section, line_attenuation, energy_index, fan_offset, fan_weight, measured
):
    highest = lax.Precision.HIGHEST
    n_species = concentration.shape[0]
    depth_z = concentration.shape[1]
    rows_x = concentration.shape[2]
    n_beam = lax.axis_size("beam")
    n_det = lax.axis_size("det")
    n_slab = lax.axis_size("slab")
    full_x = rows_x * n_beam
    full_y = concentration.shape[3] * n_det
    onehot = (
        energy_index[:, None] == jnp.arange(cross_section.shape[1], dtype=jnp.int32)[None, :]
    ).astype(jnp.float32)
    sigma_sel = jnp.sum(cross_section[:, None, :] * onehot[None], axis=2)
    n_energy = sigma_sel.shape[1]
    emission = sigma_sel[0][:, None, None, None] * concentration[0][None]
    absorber = line_attenuation[0] * concentration[0]
    for species in range(1, n_species):
        emission = emission + sigma_sel[species][:, None, None, None] * concentration[species][None]
        absorber = absorber + line_attenuation[species] * concentration[species]
    local_depth = jnp.sum(emission, axis=2)
    upstream = entering(local_depth, "beam", add_pair, jnp.zeros_like(local_depth), False)
    path_in = jnp.cumsum(emission, axis=2) - emission + upstream[:, :, None, :]
    incident = jnp.exp(-(1.5 / full_x) * path_in)
    row_depth = jnp.sum(absorber, axis=2)
    downstream = entering(row_depth, "det", add_pair, jnp.zeros_like(row_depth), True)
    path_out = row_depth[:, :, None] - jnp.cumsum(absorber, axis=2) + downstream[:, :, None]
    escape = jnp.exp(-(1.5 / full_y) * path_out)
    fluor = emission * incident * escape[None]
    line_sums = jnp.sum(fluor, axis=2)
    slab_index = lax.axis_index("slab")
    local_slices = slab_index * depth_z + jnp.arange(depth_z, dtype=jnp.int32)
    weights_local = fan_matrix(fan_offset, fan_weight, local_slices)
    group_index = lax.axis_index(("beam", "slab"))
    share = fan_offset.shape[0] // (n_beam * n_slab)
    first_row = group_index * share
    row_total = lax.psum(line_sums, "beam")
    every_slice = lax.all_gather(row_total, "slab", axis=1, tiled=True)
    all_slices = jnp.arange(depth_z * n_slab, dtype=jnp.int32)
    weights_all = fan_matrix(fan_offset, fan_weight, all_slices)
    signal = jnp.einsum("kz,ezy->eky", weights_all, every_slice, precision=highest) / full_x
    misfit = signal - measured
    back = jnp.einsum("kz,eky->ezy", weights_local, misfit, precision=highest)
    residual = lax.dynamic_slice_in_dim(misfit, first_row, share, 1)
    heavy = back[:, :, None, :] * fluor
    heavy_rows = jnp.sum(heavy, axis=2)
    further = entering(heavy_rows, "beam", add_pair, jnp.zeros_like(heavy_rows), True)
    after_x = heavy_rows[:, :, None, :] - jnp.cumsum(heavy, axis=2) + further[:, :, None, :]
    heavy_all = jnp.sum(heavy, axis=0)
    column_sums = jnp.sum(heavy_all, axis=2)
    nearer = entering(column_sums, "det", add_pair, jnp.zeros_like(column_sums), False)
    before_y = jnp.cumsum(heavy_all, axis=2) - heavy_all + nearer[:, :, None]
    term = back[:, :, None, :] * incident * escape[None] - 1.5 / full_x * after_x
    result = []
    for species in range(n_species):
        accum = sigma_sel[species, 0] * term[0]
        for energy in range(1, n_energy):
            accum = accum + sigma_sel[species, energy] * term[energy]
        result.append(accum - line_attenuation[species] * (1.5 / full_y) * before_y)
    return (jnp.stack(result), residual)


def solution(mesh):
    in_specs = (P(None, "slab", "beam", "det"), P(), P(), P(), P(), P(), P(None, None, "det"))
    out_specs = (P(None, "slab", "beam", "det"), P(None, ("beam", "slab"), "det"))
    return jax.shard_map(shards, mesh=mesh, in_specs=in_specs, out_specs=out_specs, check_vma=False)
```

profile of v0, /device:TPU:0, one launch (start us, length us, event | category | flops | bytes accessed | tf_op | source)
XLA Modules:
  0.0 206.1 jit_solution(16518248538004318588)
XLA Ops:
  0.6 1.5 fusion.43
  2.1 6.8 %slice_bitcast_fusion.11 = (f32[8,256,128]{2,1,0:T(8,128)S(1)}, f32[8,256,128]{2,1,0:T(8,128)S(1)}, f32[8,256,128]{2,1,0:T(8,128)}, f32[8,256,128]{2,1,0:T(8,128...) fusion(f32[4,8,256,128]{3,2,1,0:T(8,128)} %param.11, ...), kind=kLoop, calls=%fused_computation.83 | loop fusion | flops 1835008 | bytes 13631504 | tf_op jit(solution)/shard_map/mul | solution.py:49
  8.9 0.6 copy.83
  9.6 0.6 copy.84
  10.2 0.6 copy.85
  10.8 0.6 copy.86
  11.6 1.2 fusion.11
  12.8 0.2 fusion.36
  13.1 2.4 %broadcast_add_fusion.1 = f32[4,8,128,2,128]{2,1,4,3,0:T(8,128)} fusion(f32[4,8,128,2,128]{2,1,4,3,0:T(8,128)S(1)} %fusion.11, f32[4,8,128,2]{2,1,3,0:T(8,128)S(1)} %slice.170), kind=kLoop, calls=%fused_computation.29 | loop fusion | flops 1048576 | bytes 8421376 | tf_op jit(solution)/shard_map/reduce_window_sum
  15.4 5.5 %copy.87 = f32[4,8,128,256]{3,1,2,0:T(8,128)} copy(f32[4,8,128,256]{2,1,3,0:T(8,128)} %bitcast.113) | data formatting | bytes 8388608 | tf_op jit(solution)/shard_map/reduce_window_sum
  21.0 0.5 copy.79
  21.4 0.5 copy.80
  21.9 1.7 copy.81
  23.6 3.0 %copy.82 = f32[8,256,128]{1,0,2:T(8,128)} copy(f32[8,256,128]{2,1,0:T(8,128)} %get-tuple-element.258) | data formatting | bytes 2097152 | tf_op jit(solution)/shard_map/mul | solution.py:52
  26.7 2.5 %fusion.12 = f32[4,8,128]{1,2,0:T(8,128)S(1)} fusion(f32[8,256,128]{1,0,2:T(8,128)} %copy.82, f32[4]{0:T(128)S(1)} %get-tuple-element.281, f32[8,256,128]{1,0,2:T(8,128)S(1)} %copy.81, f32[4]{0:T(128)S(1)} %get-tuple-element.282, f32[8,256,128]{1,0,2:T(8,128)S(1)} %copy.80, f32[4]{0:T(128)S(1)} %get-tuple-element.283, f32[8,256,128]{1,0,2:T(8,128)S(1)} %copy.79, ...), kind=kLoop, calls=%fused_computation.20 | loop fusion | flops 8384512 | bytes 4210752 | tf_op jit(solution)/shard_map/reduce_sum | solution.py:54
  29.2 6.2 %all-gather = f32[16,8,128]{2,1,0:T(8,128)S(1)} all-gather(f32[4,8,128]{2,1,0:T(8,128)S(1)} %copy.88), channel_id=2, replica_groups=mesh['beam'=4,'det'=2,'slab'=4] {'beam'}, dimensions={0}, use_global_device_ids=true | all-gather | bytes 81920 | tf_op jit(solution)/shard_map/all_gather | solution.py:9
  35.6 2.8 %copy.90 = f32[8,256,128]{1,0,2:T(8,128)} copy(f32[8,256,128]{2,1,0:T(8,128)} %get-tuple-element.259) | data formatting | bytes 2097152 | tf_op jit(solution)/shard_map/jit(cumsum)/reduce_window_sum | solution.py:60
  38.4 5.1 %add_reduce_fusion = f32[8,256]{1,0:T(8,128)S(1)} fusion(f32[]{:T(128)} %bitcast.24, f32[]{:T(128)} %bitcast.23, f32[]{:T(128)} %bitcast.22, f32[]{:T(128)} %bitcast.21, f32[4,8,256,128]{3,2,1,0:T(8,128)} %param.11), kind=kLoop, calls=%fused_computation.57 | loop fusion | flops 2095104 | bytes 4202512 | tf_op jit(solution)/shard_map/reduce_sum | solution.py:58
  43.5 4.4 %all-gather.1 = f32[16,256]{1,0:T(8,128)S(1)} all-gather(f32[8,256]{1,0:T(8,128)S(1)} %add_reduce_fusion), channel_id=3, replica_groups=mesh['beam'=4,'det'=2,'slab'=4] {'det'}, dimensions={0}, use_global_device_ids=true | all-gather | bytes 24576 | tf_op jit(solution)/shard_map/all_gather | solution.py:9
  47.9 1.5 multiply_exponential_fusion
  49.4 6.9 %fusion.41 = (f32[4,8,128]{1,2,0:T(8,128)}, f32[4,8,256,128]{2,1,3,0:T(8,128)}) fusion(f32[8,256,128]{1,0,2:T(8,128)S(1)} %multiply_exponential_fusion, f32[4,8,128]{1,2,0:T(8,128)S(1)} %copy.89, f32[4,8,128,256]{3,1,2,0:T(8,128)} %copy.87, f32[8,256,128]{1,0,2:T(8,128)} %copy.82, f32[4]{0:T(128)S(1)} %get-tuple-element.281, f32[8,256,128]{1,0,2:T(8,128)} %copy-done, ...), kind=kLoop, calls=%fused_computation.84 | loop fusion | flops 13627392 | bytes 13664320 | tf_op jit(solution)/shard_map/reduce_sum | solution.py:63
  56.3 1.0 copy.91
  57.4 10.8 %psum.7 = f32[4,8,128]{2,1,0:T(8,128)S(1)} all-reduce(f32[4,8,128]{2,1,0:T(8,128)S(1)} %copy.91), channel_id=1, replica_groups=mesh['beam'=4,'det'=2,'slab'=4] {'beam'}, use_global_device_ids=true, to_apply=%region_9.10 | all-reduce | flops 4096 | bytes 32768 | tf_op jit(solution)/shard_map/psum | solution.py:70
  68.2 13.6 %all_gather.31 = f32[4,32,128]{2,1,0:T(8,128)S(1)} all-gather(f32[4,8,128]{2,1,0:T(8,128)S(1)} %psum.7), channel_id=1, replica_groups=mesh['beam'=4,'det'=2,'slab'=4] {'slab'}, dimensions={1}, use_global_device_ids=true | all-gather | bytes 81920 | tf_op jit(solution)/shard_map/all_gather | solution.py:71
  81.8 2.0 copy.92
  83.8 2.4 %fusion.34 = f32[4,256,128]{1,2,0:T(8,128)} fusion(f32[4,256,128]{1,2,0:T(8,128)} %copy.92, f32[4,32,128]{2,1,0:T(8,128)S(1)} %all_gather.31, f32[256,32]{0,1:T(8,128)S(1)} %select_reduce_fusion), kind=kOutput, calls=%fused_computation.48 | convolution fusion | flops 50593792 | bytes 1146880 | tf_op jit(solution)/shard_map/kz,ezy->eky/dot_general | solution.py:74
  86.4 1.6 convolution_bitcast_fusion
  88.0 0.1 copy.94
  88.1 4.1 %multiply_reduce_fusion.2 = (f32[4,8,128]{1,2,0:T(8,128)}, f32[8,256,128]{1,0,2:T(8,128)}, f32[8,256]{1,0:T(8,128)S(1)}) fusion(f32[4,8,256,128]{2,1,3,0:T(8,128)} %get-tuple-element.252, f32[4,8,128]{1,2,0:T(8,128)S(1)} %copy.94), kind=kLoop, calls=%fused_computation.23 | loop fusion | flops 3926016 | bytes 5283840 | tf_op jit(solution)/shard_map/reduce_sum | solution.py:79
  92.2 1.0 copy.97
  93.2 5.7 %all-gather.2 = f32[16,8,128]{2,1,0:T(8,128)} all-gather(f32[4,8,128]{2,1,0:T(8,128)S(1)} %copy.97), channel_id=4, replica_groups=mesh['beam'=4,'det'=2,'slab'=4] {'beam'}, dimensions={0}, use_global_device_ids=true | all-gather | bytes 81920 | tf_op jit(solution)/shard_map/all_gather | solution.py:9
  98.9 0.8 rev.4
  99.9 0.8 copy.98
  100.7 1.5 copy.95
  102.2 4.8 %fusion.3 = f32[4,8,128,2,128]{2,1,4,3,0:T(8,128)S(1)} fusion(f32[4,8,128,2,128]{2,1,4,3,0:T(8,128)} %broadcast_add_fusion.1, f32[8,128,2,128]{1,0,3,2:T(8,128)} %copy.95, f32[4,8,128]{2,1,0:T(8,128)S(1)} %get-tuple-element.190, f32[4,8,128]{2,1,0:T(8,128)S(1)} %convolution_bitcast_fusion, f32[8,128,2,128]{1,0,3,2:T(8,128)} %copy-done.4, ...), kind=kOutput, calls=%fused_computation.8 | output fusion | flops 146800640 | bytes 13664320 | tf_op jit(solution)/shard_map/reduce-window.2
  107.1 0.2 fusion.35
  107.3 2.4 %broadcast_add_fusion = f32[4,8,128,2,128]{2,1,4,3,0:T(8,128)} fusion(f32[4,8,128,2,128]{2,1,4,3,0:T(8,128)S(1)} %fusion.3, f32[4,8,128,2]{2,1,3,0:T(8,128)S(1)} %slice.173), kind=kLoop, calls=%fused_computation.24 | loop fusion | flops 1048576 | bytes 8421376 | tf_op jit(solution)/shard_map/reduce_window_sum
  109.7 5.6 %copy.96 = f32[4,8,128,256]{3,1,2,0:T(8,128)} copy(f32[4,8,128,256]{2,1,3,0:T(8,128)} %bitcast.114) | data formatting | bytes 8388608 | tf_op jit(solution)/shard_map/reduce_window_sum
  115.2 7.8 %bitcast_subtract_fusion = f32[4,8,256,128]{2,1,3,0:T(8,128)} fusion(f32[4,8,128,256]{3,1,2,0:T(8,128)} %copy.96, f32[4,8,128]{1,2,0:T(8,128)} %copy.98, f32[4,8,128]{1,2,0:T(8,128)} %get-tuple-element.230, f32[4,8,128]{1,2,0:T(8,128)S(1)} %copy.94, f32[8,256,128]{1,0,2:T(8,128)S(1)} %multiply_exponential_fusion, f32[4,8,128]{1,2,0:T(8,128)} %copy-done.8, ...), kind=kLoop, calls=%fused_computation.3 | loop fusion | flops 16777216 | bytes 17891392 | tf_op jit(solution)/shard_map/sub | solution.py:86
  123.0 47.5 %fusion.44 = f32[8,256,128]{1,0,2:T(8,128)S(1)} fusion(f32[8,256,128]{1,0,2:T(8,128)S(1)} %copy-done.5), kind=kOutput, calls=%fused_computation.87 | output fusion | flops 33292288 | bytes 2097152 | tf_op jit(solution)/shard_map/jit(cumsum)/reduce_window_sum | solution.py:85
  170.5 4.4 %all-gather.3 = f32[16,256]{1,0:T(8,128)S(1)} all-gather(f32[8,256]{1,0:T(8,128)S(1)} %get-tuple-element.232), channel_id=5, replica_groups=mesh['beam'=4,'det'=2,'slab'=4] {'det'}, dimensions={0}, use_global_device_ids=true | all-gather | bytes 24576 | tf_op jit(solution)/shard_map/all_gather | solution.py:9
  174.9 0.7 fusion.42
  176.3 6.4 %multiply_subtract_fusion.3 = (f32[1,8,256,128]{2,1,3,0:T(8,128)}, f32[1,8,256,128]{2,1,3,0:T(8,128)S(1)}) fusion(f32[4,8,256,128]{2,1,3,0:T(8,128)} %bitcast_subtract_fusion, f32[]{:T(128)S(6)} %mul.558, f32[]{:T(128)} %bitcast.38, f32[]{:T(128)} %bitcast.37, f32[]{:T(128)} %bitcast.36, f32[]{:T(128)} %bitcast, f32[8,256]{1,0:T(8,128)S(1)} %slice_select_fusion, ...), kind=kLoop, calls=%fused_computation.54 | loop fusion | flops 2883584 | bytes 8396820 | tf_op jit(solution)/shard_map/sub | solution.py:92
  184.0 7.8 %multiply_subtract_fusion.2 = (f32[1,8,256,128]{2,1,3,0:T(8,128)S(1)}, f32[1,8,256,128]{2,1,3,0:T(8,128)S(1)}) fusion(f32[1,8,256,128]{2,1,3,0:T(8,128)S(1)} %get-tuple-element.250, f32[4,8,256,128]{2,1,3,0:T(8,128)} %bitcast_subtract_fusion, f32[]{:T(128)S(6)} %mul.569, f32[]{:T(128)} %bitcast.43, f32[]{:T(128)} %bitcast.42, f32[]{:T(128)} %bitcast.41, ...), kind=kLoop, calls=%fused_computation.53 | loop fusion | flops 4718592 | bytes 7340072 | tf_op jit(solution)/shard_map/sub | solution.py:92
  192.5 5.1 %multiply_subtract_fusion = f32[1,8,256,128]{2,1,3,0:T(8,128)S(1)} fusion(f32[1,8,256,128]{2,1,3,0:T(8,128)S(1)} %get-tuple-element.250, f32[4,8,256,128]{2,1,3,0:T(8,128)} %bitcast_subtract_fusion, f32[]{:T(128)S(6)} %mul.591, f32[]{:T(128)} %bitcast.51, f32[]{:T(128)} %bitcast.50, f32[]{:T(128)} %bitcast.49, f32[]{:T(128)} %bitcast.48), kind=kLoop, calls=%fused_computation.51 | loop fusion | flops 2359296 | bytes 6291476 | tf_op jit(solution)/shard_map/sub | solution.py:92
  197.6 2.2 %pad_maximum_fusion = f32[4,8,256,128]{2,1,3,0:T(8,128)} fusion(f32[1,8,256,128]{2,1,3,0:T(8,128)S(1)} %multiply_subtract_fusion, f32[1,8,256,128]{2,1,3,0:T(8,128)S(1)} %get-tuple-element.254, f32[1,8,256,128]{2,1,3,0:T(8,128)S(1)} %get-tuple-element.253, f32[1,8,256,128]{2,1,3,0:T(8,128)S(1)} %copy-done.6), kind=kLoop, calls=%fused_computation.2 | loop fusion | flops 3145728 | bytes 8388608 | tf_op jit(solution)/shard_map/stack | solution.py:93
  199.9 5.3 %copy.99 = f32[4,8,256,128]{3,2,1,0:T(8,128)} copy(f32[4,8,256,128]{2,1,3,0:T(8,128)} %pad_maximum_fusion) | data formatting | bytes 8388608
  205.3 0.7 copy.100
  (51 shorter events, 0.9 us)
Async XLA Ops:
  8.9 2.5 %copy-start.12 = (s32[4]{0:T(128)S(1)}, s32[4]{0:T(128)}, u32[]{:S(2)}) copy-start(s32[4]{0:T(128)} %param.14) | copy-start | bytes 52
  8.9 2.6 %copy-start.10 = (f32[4,16]{1,0:T(4,128)S(1)}, f32[4,16]{1,0:T(4,128)}, u32[]{:S(2)}) copy-start(f32[4,16]{1,0:T(4,128)} %param.12) | copy-start | bytes 772
  9.6 3.2 %copy-start.1 = (f32[8,128,2,128]{1,0,3,2:T(8,128)}, f32[8,128,2,128]{1,0,3,2:T(8,128)S(1)}, u32[]{:S(2)}) copy-start(f32[8,128,2,128]{1,0,3,2:T(8,128)S(1)} %copy.83) | copy-start | bytes 3145732
  10.2 2.6 %copy-start.2 = (f32[8,128,2,128]{1,0,3,2:T(8,128)}, f32[8,128,2,128]{1,0,3,2:T(8,128)S(1)}, u32[]{:S(2)}) copy-start(f32[8,128,2,128]{1,0,3,2:T(8,128)S(1)} %copy.84) | copy-start | bytes 3145732
  10.8 2.0 copy-start.3
  11.4 1.4 copy-start.4
  23.6 14.8 %copy-start = (f32[8,256,128]{1,0,2:T(8,128)}, f32[8,256,128]{1,0,2:T(8,128)S(1)}, u32[]{:S(2)}) copy-start(f32[8,256,128]{1,0,2:T(8,128)S(1)} %copy.81) | copy-start | bytes 3145732
  35.6 13.8 %copy-start.8 = (f32[4,8,128]{1,2,0:T(8,128)}, f32[4,8,128]{1,2,0:T(8,128)S(1)}, u32[]{:S(2)}) copy-start(f32[4,8,128]{1,2,0:T(8,128)S(1)} %copy.89) | copy-start | bytes 49156
  49.4 32.4 %copy-start.9 = (s32[256,4]{0,1:T(4,128)S(1)}, s32[256,4]{0,1:T(4,128)}, u32[]{:S(2)}) copy-start(s32[256,4]{0,1:T(4,128)} %param.16) | copy-start | bytes 12292
  49.4 32.4 %copy-start.11 = (s32[256]{0:T(256)S(1)}, s32[256]{0:T(256)}, u32[]{:S(2)}) copy-start(s32[256]{0:T(256)} %param.15) | copy-start | bytes 3076
  115.2 7.8 %copy-start.5 = (f32[8,256,128]{1,0,2:T(8,128)S(1)}, f32[8,256,128]{1,0,2:T(8,128)}, u32[]{:S(2)}) copy-start(f32[8,256,128]{1,0,2:T(8,128)} %get-tuple-element.231) | copy-start | bytes 3145732
  192.5 5.1 %copy-start.6 = (f32[1,8,256,128]{2,1,3,0:T(8,128)S(1)}, f32[1,8,256,128]{2,1,3,0:T(8,128)}, u32[]{:S(2)}) copy-start(f32[1,8,256,128]{2,1,3,0:T(8,128)} %get-tuple-element.249) | copy-start | bytes 3145732
  199.9 5.4 %copy-start.7 = (f32[4,256,128]{1,2,0:T(8,128)S(1)}, f32[4,256,128]{1,2,0:T(8,128)}, u32[]{:S(2)}) copy-start(f32[4,256,128]{1,2,0:T(8,128)} %fusion.34) | copy-start | bytes 1572868
where the time goes:
time: 207 us; the launch traced here: 206 us
  other arithmetic  115 us (56%)
  blocking collectives  45 us (22%)
  local copies, waits for them, and re-layouts  38.2 us (18%)
  matrix products  4.03 us (2%)
  between operations  3.56 us (2%)
    another operation x1, other arithmetic, shards(): before_y = jnp.cumsum(heavy_all, axis=2) - heavy_all + nearer[:, :, None]  47.5 us
    all_gather x4, blocking collectives, entering(): pieces = lax.all_gather(value, axis)  20.6 us
    sub x3, other arithmetic, shards(): result.append(accum - line_attenuation[species] * (1.5 / full_y) * before_y)  19.3 us
    all_gather x1, blocking collectives, shards(): every_slice = lax.all_gather(row_total, 'slab', axis=1, tiled=True)  13.6 us
    another operation x4, local copies, waits for them, and re-layouts  11.1 us
    another operation x6, other arithmetic  11.1 us
    psum x1, blocking collectives, shards(): row_total = lax.psum(line_sums, 'beam')  10.8 us
    unnamed x29, local copies, waits for them, and re-layouts  8.16 us

commit v1 on v0

v1 whole, which is shorter than its diff:
```python
import functools
import math

import jax
import jax.numpy as jnp
from jax import lax
from jax.experimental import pallas as pl
from jax.experimental.pallas import tpu as pltpu
from jax.sharding import PartitionSpec as P

VMEM, SMEM, HBM = pltpu.VMEM, pltpu.SMEM, pltpu.HBM
F32, BF16 = jnp.float32, jnp.bfloat16
LANES = 128
CHUNK = 32
STEP = 16
LN2 = math.log(2.0)
LOG2E = 1.0 / LN2


def call(body, name, out_shape, out_spaces, in_spaces, scratch=(), limit=8, cost=None):
    flops, exps, size = cost
    return pl.pallas_call(
        body,
        out_shape=out_shape,
        in_specs=[pl.BlockSpec(memory_space=s) for s in in_spaces],
        out_specs=[pl.BlockSpec(memory_space=s) for s in out_spaces],
        scratch_shapes=list(scratch),
        compiler_params=pltpu.CompilerParams(vmem_limit_bytes=limit << 20),
        cost_estimate=pl.CostEstimate(flops=flops, transcendentals=exps, bytes_accessed=size),
        name=name,
    )


def plain(*shape):
    return jax.ShapeDtypeStruct(shape, F32)


def split(value):
    high = value.astype(BF16)
    low = (value - high.astype(F32)).astype(BF16)
    return jnp.concatenate([high, low], axis=1)


def lane_sums(width, beyond):
    row = lax.broadcasted_iota(jnp.int32, (width, 2 * width), 0)
    col = lax.broadcasted_iota(jnp.int32, (width, 2 * width), 1)
    part = (row > col) if beyond else (row < col)
    ones = jnp.where(part | (col >= width), 1.0, 0.0).astype(BF16)
    return jnp.concatenate([ones, ones], axis=0)


def selected(cross_ref, index_ref):
    n_energy = index_ref.shape[0]
    columns = [index_ref[e] for e in range(n_energy)]
    return [[cross_ref[s, columns[e]] for e in range(n_energy)] for s in range(cross_ref.shape[0])]


def weighted(weights, values):
    total = weights[0] * values[0]
    for weight, value in zip(weights[1:], values[1:]):
        total = total + weight * value
    return total


def load_body(scale, line_hbm, conc_hbm, conc_ref, beyond_ref, total_ref, line_ref, line_sem, sems):
    n_species, depth, rows, width = conc_hbm.shape

    def copies(chunk):
        span = pl.ds(chunk * CHUNK, CHUNK)
        return [
            pltpu.make_async_copy(conc_hbm.at[:, z, span, :], conc_ref.at[:, span, z, :], sems.at[chunk])
            for z in range(depth)
        ]

    line_copy = pltpu.make_async_copy(line_hbm, line_ref, line_sem)
    line_copy.start()

    for chunk in range(rows // CHUNK):
        for copy in copies(chunk):
            copy.start()
    table = lane_sums(width, True)
    lane = lax.broadcasted_iota(jnp.int32, (depth, LANES), 1)
    line_copy.wait()
    line = [line_ref[s] * scale for s in range(n_species)]
    for part in range(rows // LANES):

        def step(piece, total):
            chunk = part * (LANES // CHUNK) + piece
            for copy in copies(chunk):
                copy.wait()
            absorber = []
            for q in range(CHUNK):
                x = chunk * CHUNK + q
                absorber.append(weighted(line, [conc_ref[s, x] for s in range(n_species)]))
            sums = jnp.dot(split(jnp.concatenate(absorber, axis=0)), table, preferred_element_type=F32)
            for q in range(CHUNK):
                here = sums[q * depth : (q + 1) * depth]
                beyond_ref[chunk * CHUNK + q] = here[:, :width]
                total = jnp.where(lane == piece * CHUNK + q, here[:, width : width + LANES], total)
            return total

        total_ref[:, part * LANES : (part + 1) * LANES] = lax.fori_loop(
            0, LANES // CHUNK, step, jnp.zeros((depth, LANES), F32)
        )


def local_body(scale, cross_ref, index_ref, conc_ref, beyond_ref, trans_ref, emit_ref, depth_ref):
    n_species, rows, depth, width = conc_ref.shape
    n_energy = trans_ref.shape[0]
    sigma = [[v * scale for v in row] for row in selected(cross_ref, index_ref)]

    def step(block, path):
        path = list(path)
        for q in range(STEP):
            x = block * STEP + q
            conc = [conc_ref[s, x] for s in range(n_species)]
            beyond = beyond_ref[x]
            for e in range(n_energy):
                emission = weighted([sigma[s][e] for s in range(n_species)], conc)
                trans = jnp.exp2(path[e] + beyond)
                trans_ref[e, x] = trans
                emit_ref[e, x] = emission * trans
                path[e] = path[e] + emission
        return tuple(path)

    zero = jnp.zeros((depth, width), F32)
    path = lax.fori_loop(0, rows // STEP, step, (zero,) * n_energy)
    for e in range(n_energy):
        depth_ref[e] = path[e]


def spread(source_ref, change, width, body, init):
    depth, rows = source_ref.shape
    carry = init
    for part in range(rows // LANES):
        held = change(source_ref[:, part * LANES : (part + 1) * LANES])

        def step(block, state):
            held, carry = state
            for q in range(STEP):
                column = jnp.broadcast_to(held[:, q : q + 1], (depth, width))
                carry = body(part * LANES + block * STEP + q, column, carry)
            return pltpu.roll(held, LANES - STEP, 1), carry

        _, carry = lax.fori_loop(0, LANES // STEP, step, (held, carry))
    return carry


def line_body(far_ref, emit_ref, far_out, line_ref):
    n_energy, rows, depth, width = emit_ref.shape

    def one(x, factor, sums):
        far_out[x] = factor
        return tuple(sums[e] + factor * emit_ref[e, x] for e in range(n_energy))

    zero = jnp.zeros((depth, width), F32)
    sums = spread(far_ref, jnp.exp2, width, one, (zero,) * n_energy)
    for e in range(n_energy):
        line_ref[e] = sums[e]


def ahead_body(far_ref, trans_ref, emit_ref, fluor_ref, rest_ref):
    n_energy, rows, depth, width = emit_ref.shape

    def step(block, ahead):
        ahead = list(ahead)
        for q in range(STEP):
            x = rows - 1 - (block * STEP + q)
            far = far_ref[x]
            for e in range(n_energy):
                fluor = far * emit_ref[e, x]
                fluor_ref[e, x] = fluor
                rest_ref[e, x] = far * trans_ref[e, x] + ahead[e]
                ahead[e] = ahead[e] + LN2 * fluor
        return tuple(ahead)

    zero = jnp.zeros((depth, width), F32)
    lax.fori_loop(0, rows // STEP, step, (zero,) * n_energy)


def fan_body(fan_ref, measured_ref, gram_ref, pull_ref):
    depth = pull_ref.shape[1]
    own = fan_ref[:depth, :]
    gram_ref[...] = lax.dot_general(
        own.astype(BF16), fan_ref[...].astype(BF16), (((1,), (1,)), ((), ())), preferred_element_type=F32
    )
    for e in range(pull_ref.shape[0]):
        pull_ref[e] = jnp.dot(
            own, measured_ref[e], precision=lax.Precision.HIGHEST, preferred_element_type=F32
        )


def back_body(
    scale, cross_ref, index_ref, gram_ref, pull_ref, lines_ref, up_ref, further_ref, fluor_ref,
    near_ref, total_ref, gain_ref, shift_ref,
):
    n_energy, rows, depth, width = fluor_ref.shape
    n_species = shift_ref.shape[0]
    sums = [None] * n_energy
    for r in range(lines_ref.shape[0]):
        for z in range(depth):
            place = r * depth + z
            weight = jnp.broadcast_to(gram_ref[:, place : place + 1], (depth, width))
            for e in range(n_energy):
                value = weight * lines_ref[r, e, z : z + 1, :]
                sums[e] = value if place == 0 else sums[e] + value
    back = [sums[e] * scale - pull_ref[e] for e in range(n_energy)]
    gain = [back[e] * jnp.exp2(up_ref[e]) for e in range(n_energy)]
    sigma = selected(cross_ref, index_ref)
    pushed = [LN2 * back[e] * further_ref[e] for e in range(n_energy)]
    for e in range(n_energy):
        gain_ref[e] = gain[e]
    for s in range(n_species):
        shift_ref[s] = weighted(sigma[s], pushed)
    table = lane_sums(width, False)
    lane = lax.broadcasted_iota(jnp.int32, (depth, LANES), 1)
    for part in range(rows // LANES):

        def step(piece, total):
            first = part * LANES + piece * CHUNK
            heavy = [weighted(gain, [fluor_ref[e, first + q] for e in range(n_energy)]) for q in range(CHUNK)]
            found = jnp.dot(split(jnp.concatenate(heavy, axis=0)), table, preferred_element_type=F32)
            for q in range(CHUNK):
                here = found[q * depth : (q + 1) * depth]
                near_ref[first + q] = here[:, :width]
                total = jnp.where(lane == piece * CHUNK + q, here[:, width : width + LANES], total)
            return total

        total_ref[:, part * LANES : (part + 1) * LANES] = lax.fori_loop(
            0, LANES // CHUNK, step, jnp.zeros((depth, LANES), F32)
        )


def grad_body(
    scale, cross_ref, index_ref, line_ref, nearer_ref, gain_ref, shift_ref, near_ref, rest_ref,
    out_hbm, out_ref, sems,
):
    n_energy, rows, depth, width = rest_ref.shape
    n_species = out_ref.shape[0]
    sigma = selected(cross_ref, index_ref)
    mixed = [[sigma[s][e] * gain_ref[e] for e in range(n_energy)] for s in range(n_species)]
    shift = [shift_ref[s] for s in range(n_species)]
    line = [line_ref[s] * scale for s in range(n_species)]

    def copies(chunk):
        span = pl.ds(chunk * CHUNK, CHUNK)
        return [
            pltpu.make_async_copy(out_ref.at[:, span, z, :], out_hbm.at[:, z, span, :], sems.at[chunk])
            for z in range(depth)
        ]

    for part in range(rows // LANES):

        def step(piece, held):
            chunk = part * (LANES // CHUNK) + piece
            for q in range(CHUNK):
                x = chunk * CHUNK + q
                column = jnp.broadcast_to(held[:, q : q + 1], (depth, width))
                before = near_ref[x] + column
                rest = [rest_ref[e, x] for e in range(n_energy)]
                for s in range(n_species):
                    out_ref[s, x] = weighted(mixed[s], rest) + shift[s] + line[s] * before
            for copy in copies(chunk):
                copy.start()
            return pltpu.roll(held, LANES - CHUNK, 1)

        lax.fori_loop(0, LANES // CHUNK, step, nearer_ref[:, part * LANES : (part + 1) * LANES])

    def finish(chunk, carry):
        for copy in copies(chunk):
            copy.wait()
        return carry

    lax.fori_loop(0, rows // CHUNK, finish, 0)


def signal_body(scale, fan_ref, lines_ref, measured_ref, out_ref):
    n_energy, share, width = out_ref.shape
    depth = lines_ref.shape[2]
    sums = [None] * n_energy
    for r in range(lines_ref.shape[0]):
        for z in range(depth):
            place = r * depth + z
            weight = jnp.broadcast_to(fan_ref[:, place : place + 1], (share, width))
            for e in range(n_energy):
                value = weight * lines_ref[r, e, z : z + 1, :]
                sums[e] = value if place == 0 else sums[e] + value
    for e in range(n_energy):
        out_ref[e] = sums[e] * scale - measured_ref[e]


def swap(value, axis, distance):
    return lax.ppermute(value, axis, [(i, i ^ distance) for i in range(lax.axis_size(axis))])


def beyond(value, axis, backward):
    count, mine = lax.axis_size(axis), lax.axis_index(axis)
    if count == 2:
        keep = (mine == 1) if backward else (mine == 0)
        return jnp.where(keep, swap(value, axis, 1), 0.0)
    pieces = lax.all_gather(value, axis)
    places = jnp.arange(count)
    keep = (places < mine) if backward else (places > mine)
    return jnp.sum(jnp.where(keep.reshape((-1,) + (1,) * value.ndim), pieces, 0.0), axis=0)


def fan_rows(fan_offset, fan_weight, slices):
    taps = fan_weight.shape[1]
    total = 0.0
    for j in range(taps):
        match = slices[:, None] == fan_offset[None, :] + j
        total = total + jnp.where(match, fan_weight[:, j].astype(F32)[None, :], 0.0)
    return total


def shards(conc, cross, line, index, fan_offset, fan_weight, measured):
    n_species, depth, rows, width = conc.shape
    n_energy = index.shape[0]
    n_beam, n_det, n_slab = (lax.axis_size(a) for a in ("beam", "det", "slab"))
    assert n_beam & (n_beam - 1) == 0 and n_slab & (n_slab - 1) == 0
    assert rows % LANES == 0 and width % LANES == 0 and depth % 8 == 0
    full_x, full_y = rows * n_beam, width * n_det
    scale_x = -(1.5 / full_x) * LOG2E
    scale_y = -(1.5 / full_y) * LOG2E
    voxels = depth * rows * width
    cube = VMEM((n_energy, rows, depth, width), F32)
    plane = VMEM((rows, depth, width), F32)

    conc_x, far_local, row_total = call(
        functools.partial(load_body, scale_y),
        "load",
        (VMEM((n_species, rows, depth, width), F32), plane, plain(depth, rows)),
        (VMEM, VMEM, VMEM),
        (HBM, HBM),
        [SMEM((n_species,), F32), pltpu.SemaphoreType.DMA, pltpu.SemaphoreType.DMA((rows // CHUNK,))],
        cost=(8 * voxels, 0, 16 * voxels),
    )(pltpu.with_memory_space_constraint(line, HBM), pltpu.with_memory_space_constraint(conc, HBM))

    far = beyond(row_total, "det", False)

    trans, emit, own_depth = call(
        functools.partial(local_body, scale_x),
        "local",
        (cube, cube, plain(n_energy, depth, width)),
        (VMEM, VMEM, VMEM),
        (SMEM, SMEM, VMEM, VMEM),
        cost=(40 * voxels, 4 * voxels, 1024),
    )(cross, index, conc_x, far_local)

    far_wide, own_line = call(
        line_body, "line", (plane, plain(n_energy, depth, width)), (VMEM, VMEM), (VMEM, VMEM),
        cost=(8 * voxels, 0, 1024),
    )(far, emit)

    beam = lax.axis_index("beam")
    span, sums = own_depth, own_line
    up, further = jnp.zeros_like(own_depth), jnp.zeros_like(own_line)
    distance = 1
    while distance < n_beam:
        other = swap(jnp.stack([span, sums]), "beam", distance)
        lower = (beam & distance) == 0
        first = jnp.where(lower, span, other[0])
        fade = jnp.exp2(first)
        late = fade * jnp.where(lower, other[1], sums)
        further = jnp.where(lower, further + late, fade * further)
        up = jnp.where(lower, up, up + first)
        sums = jnp.where(lower, sums, other[1]) + late
        span = span + other[0]
        distance *= 2

    fluor, rest = call(
        ahead_body, "ahead", (cube, cube), (VMEM, VMEM), (VMEM, VMEM, VMEM),
        cost=(20 * voxels, 0, 1024),
    )(far_wide, trans, emit)

    lines = sums[None]
    distance = 1
    while distance < n_slab:
        lines = jnp.concatenate([lines, swap(lines, "slab", distance)], axis=0)
        distance *= 2

    slab = lax.axis_index("slab")
    order = (slab ^ jnp.arange(n_slab, dtype=jnp.int32))[:, None] * depth
    slices = (order + jnp.arange(depth, dtype=jnp.int32)[None, :]).reshape(-1)
    fan_all = fan_rows(fan_offset, fan_weight, slices)
    gram, pull = call(
        fan_body, "fan", (plain(depth, depth * n_slab), plain(n_energy, depth, width)),
        (VMEM, VMEM), (VMEM, VMEM), cost=(4 * 2 * depth * measured.size // width * width, 0, 4 * measured.size),
    )(fan_all, measured)

    near, column_total, gain, shift = call(
        functools.partial(back_body, 1.0 / (scale_x * full_x)),
        "back",
        (plane, plain(depth, rows), plain(n_energy, depth, width), plain(n_species, depth, width)),
        (VMEM,) * 4,
        (SMEM, SMEM) + (VMEM,) * 6,
        cost=(10 * voxels, 0, 1024),
    )(cross, index, gram, pull, lines, up, further, fluor)

    nearer = beyond(column_total, "det", True)

    share = fan_offset.shape[0] // (n_beam * n_slab)
    start = lax.axis_index(("beam", "slab")) * share
    fan_own = fan_rows(
        lax.dynamic_slice_in_dim(fan_offset, start, share), lax.dynamic_slice_in_dim(fan_weight, start, share), slices
    ).T
    residual = call(
        functools.partial(signal_body, 1.0 / (scale_x * full_x)),
        "signal", (plain(n_energy, share, width),), (VMEM,), (VMEM, VMEM, VMEM),
        cost=(1 << 16, 0, 1024),
    )(fan_own, lines, lax.dynamic_slice_in_dim(measured, start, share, 1))[0]

    grad = call(
        functools.partial(grad_body, 1.0 / scale_x * scale_y * LN2),
        "grad",
        (plain(n_species, depth, rows, width),),
        (HBM,),
        (SMEM, SMEM, SMEM) + (VMEM,) * 5,
        [VMEM((n_species, rows, depth, width), F32), pltpu.SemaphoreType.DMA((rows // CHUNK,))],
        limit=16,
        cost=(40 * voxels, 0, 16 * voxels),
    )(cross, index, line, nearer, gain, shift, near, rest)[0]
    return grad, residual


def solution(mesh):
    in_specs = (P(None, "slab", "beam", "det"), P(), P(), P(), P(), P(), P(None, None, "det"))
    out_specs = (P(None, "slab", "beam", "det"), P(None, ("beam", "slab"), "det"))
    return jax.shard_map(shards, mesh=mesh, in_specs=in_specs, out_specs=out_specs, check_vma=False)
```

time: 207 us -> 50.5 us (0.24)
  other arithmetic: 115 us -> 0.41 us
  blocking collectives: 45 us -> 0 us
  local copies, waits for them, and re-layouts: 38.2 us -> 16.9 us
  Pallas kernels: 0 us -> 14.6 us
  starting transfers between devices: 0 us -> 9.36 us
  waiting for transfers between devices: 0 us -> 8.05 us
  matrix products: 4.03 us -> 0 us
  between operations: 3.56 us -> 0.81 us
    another operation x9 -> x3, other arithmetic: 62.3 us -> 0.02 us  [shards(): other = swap(jnp.stack([span, sums]), 'beam', distance)]
    all_gather x5 -> x0, blocking collectives: 34.2 us -> none  [the longest x4 20.6 us: entering(): pieces = lax.all_gather(value, axis)]
    sub x4 -> x0, other arithmetic: 27.1 us -> none  [the longest x3 19.3 us: shards(): result.append(accum - line_attenuation[species] * (1.5 / full_y) * before_y)]
    reduce_sum x7 -> x0, other arithmetic: 18.8 us -> none  [the longest x1 6.9 us: shards(): line_sums = jnp.sum(fluor, axis=2)]
    pallas_call x0 -> x8, Pallas kernels: none -> 14.6 us  [the longest x1 3.16 us: shards(): call(functools.partial(grad_body, 1.0 / scale_x * scale_y * LN2), 'grad',...]
    another operation x5 -> x0, local copies, waits for them, and re-layouts: 13.9 us -> none
    psum x1 -> x0, blocking collectives: 10.8 us -> none  [shards(): row_total = lax.psum(line_sums, 'beam')]
    mul x10 -> x0, local copies, waits for them, and re-layouts: 9.67 us -> none  [the longest x6 7.05 us: shards(): sigma_sel[species][:, None, None, None] * concentration[species][None]]
  transfers between devices with their start and end apart: 0 -> 6, of which waited for: 0 -> 4; matrix products, arithmetic and copies ran while one was open for 0% -> 1% of each run, Pallas kernels for 0% -> 10%
where the time goes in v1:
time: 50.5 us; the launch traced here: 50.2 us
  local copies, waits for them, and re-layouts  16.9 us (33%)
  Pallas kernels  14.6 us (29%)
  starting transfers between devices  9.36 us (19%)
  waiting for transfers between devices  8.05 us (16%)
  between operations  0.81 us (2%)
    unnamed x28, local copies, waits for them, and re-layouts  16.8 us
    ppermute x6, starting transfers between devices, swap(): lax.ppermute(value, axis, [(i, i ^ distance) for i in range(lax.axis_size...  9.36 us
    ppermute x6, waiting for transfers between devices, swap(): lax.ppermute(value, axis, [(i, i ^ distance) for i in range(lax.axis_size...  8.05 us
    pallas_call x1, Pallas kernels, shards(): call(functools.partial(grad_body, 1.0 / scale_x * scale_y * LN2), 'grad',...  3.16 us
    pallas_call x1, Pallas kernels, shards(): call(functools.partial(load_body, scale_y), 'load', (VMEM((n_species, row...  2.77 us
    pallas_call x1, Pallas kernels, shards(): call(functools.partial(back_body, 1.0 / (scale_x * full_x)), 'back', (pla...  2.3 us
    pallas_call x1, Pallas kernels, shards(): call(functools.partial(local_body, scale_x), 'local', (cube, cube, plain(...  2.25 us
    pallas_call x1, Pallas kernels, shards(): call(line_body, 'line', (plane, plain(n_energy, depth, width)), (VMEM, VM...  1.52 us
  transfers between devices with their start and end apart: 6, of which 4 were waited for; matrix products, arithmetic and copies ran while one was open for 1% of the time, Pallas kernels for 10%

profile of v1, /device:TPU:0, one launch (start us, length us, event | category | flops | bytes accessed | tf_op | source)
XLA Modules:
  0.0 50.2 jit_solution(14351883065445333774)
XLA Ops:
  0.6 0.0 copy-start.13
  0.6 0.0 copy-start.12
  0.7 0.0 copy-start.10
  0.7 0.0 copy-start.9
  0.7 2.8 %load.1 = (f32[4,256,8,128]{3,2,1,0:T(8,128)S(1)}, f32[256,8,128]{2,1,0:T(8,128)S(1)}, f32[8,256]{1,0:T(8,128)S(1)}) custom-call(f32[4]{0:T(128)} %line_ref.1, f32[4,8,256,128]{3,2,1,0:T(8,128)} %conc_hbm.1), custom_call_target="tpu_custom_call" | custom-call | flops 2097152 | bytes 4194304 | tf_op jit(solution)/shard_map/load/pallas_call | solution.py:329
  3.4 0.0 copy-start.2
  3.5 2.0 %copy-done.2 = f32[4,256,8,128]{3,2,1,0:T(8,128)} copy-done((f32[4,256,8,128]{3,2,1,0:T(8,128)}, f32[4,256,8,128]{3,2,1,0:T(8,128)S(1)}, u32[]{:S(2)}) %copy-start.2) | copy-done | bytes 4194328
  5.5 3.0 %collective-permute-start = (f32[8,256]{1,0:T(8,128)S(1)}, f32[8,256]{1,0:T(8,128)S(1)}, u32[]{:S(2)}, u32[]{:S(2)}) collective-permute-start(f32[8,256]{1,0:T(8,128)S(1)} %get-tuple-element.20), channel_id=1, source_target_pairs={{0,4},{4,0},{1,5},{5,1},{2,6},{6,2},{3,7},{7,3},{8,12},{12,8},{9,1... | collective-permute-start | bytes 24584 | tf_op jit(solution)/shard_map/ppermute | solution.py:293
  8.5 0.1 iota_add_fusion
  8.5 0.1 add.100
  8.6 0.0 copy-done.13
  8.6 0.0 copy-done.12
  8.6 0.1 select_add_fusion.fan_ref
  8.7 0.1 constant_dynamic-slice_fusion.1
  8.8 0.0 copy-done.10
  8.8 0.0 copy-done.9
  8.8 2.2 %copy-done.3 = f32[4,256,8,128]{3,2,1,0:T(8,128)S(1)} copy-done((f32[4,256,8,128]{3,2,1,0:T(8,128)S(1)}, f32[4,256,8,128]{3,2,1,0:T(8,128)}, u32[]{:S(2)}) %copy-start.3) | copy-done | bytes 4194328
  11.0 2.2 %local.1 = (f32[4,256,8,128]{3,2,1,0:T(8,128)S(1)}, f32[4,256,8,128]{3,2,1,0:T(8,128)S(1)}, f32[4,8,128]{2,1,0:T(8,128)S(1)}) custom-call(f32[4,16]{1,0:T(4,128)S(1)} %copy-done.9, s32[4]{0:T(128)S(1)} %copy-done.10, f32[4,256,8,128]{3,2,1,0:T(8,128)S(1)} %copy-done.3, f32[256,8,128]{2,1,0:T(8,128)S(1)} %get-tuple-element.22.beyond_ref), custom_call_target="tpu_custom_call" | custom-call | flops 10485760 | bytes 1024 | tf_op jit(solution)/shard_map/local/pallas_call | solution.py:341
  13.3 0.0 copy-start.6
  13.3 2.0 %copy-done.6 = f32[4,256,8,128]{3,2,1,0:T(8,128)} copy-done((f32[4,256,8,128]{3,2,1,0:T(8,128)}, f32[4,256,8,128]{3,2,1,0:T(8,128)S(1)}, u32[]{:S(2)}) %copy-start.6) | copy-done | bytes 4194328
  15.3 0.0 collective-permute-done
  15.3 1.5 %line.1 = (f32[256,8,128]{2,1,0:T(8,128)S(1)}, f32[4,8,128]{2,1,0:T(8,128)S(1)}) custom-call(f32[8,256]{1,0:T(8,128)S(1)} %broadcast_select_fusion.1.far_ref, f32[4,256,8,128]{3,2,1,0:T(8,128)S(1)} %get-tuple-element.23.emit_ref), custom_call_target="tpu_custom_call" | custom-call | flops 2097152 | bytes 1024 | tf_op jit(solution)/shard_map/line/pallas_call | solution.py:350
  16.8 0.0 copy-start
  16.8 1.9 %copy-done = f32[4,256,8,128]{3,2,1,0:T(8,128)} copy-done((f32[4,256,8,128]{3,2,1,0:T(8,128)}, f32[4,256,8,128]{3,2,1,0:T(8,128)S(1)}, u32[]{:S(2)}) %copy-start) | copy-done | bytes 4194328
  18.8 0.0 collective-permute-start.1
  18.8 1.2 %collective-permute-done.1 = f32[2,4,8,128]{3,2,1,0:T(8,128)S(1)} collective-permute-done((f32[2,4,8,128]{3,2,1,0:T(8,128)S(1)}, f32[2,4,8,128]{3,2,1,0:T(8,128)S(1)}, u32[]{:S(2)}, u32[]{:S(2)}) %collective-permute-start.1) | collective-permute-done | bytes 32800 | tf_op jit(solution)/shard_map/ppermute | solution.py:293
  20.0 1.6 %collective-permute-start.2 = (f32[2,4,8,128]{3,2,1,0:T(8,128)S(1)}, f32[2,4,8,128]{3,2,1,0:T(8,128)S(1)}, u32[]{:S(2)}, u32[]{:S(2)}) collective-permute-start(f32[2,4,8,128]{3,2,1,0:T(8,128)S(1)} %pad_maximum_fusion.2), channel_id=1, source_target_pairs={{0,16},{8,24},{16,0},{24,8},{1,17},{9,25},{17,1},{25,9},{2,18},{10... | collective-permute-start | bytes 98312 | tf_op jit(solution)/shard_map/ppermute | solution.py:293
  21.6 0.1 broadcast_add_fusion.5
  21.6 2.3 %collective-permute-done.2 = f32[2,4,8,128]{3,2,1,0:T(8,128)S(1)} collective-permute-done((f32[2,4,8,128]{3,2,1,0:T(8,128)S(1)}, f32[2,4,8,128]{3,2,1,0:T(8,128)S(1)}, u32[]{:S(2)}, u32[]{:S(2)}) %collective-permute-start.2) | collective-permute-done | bytes 32800 | tf_op jit(solution)/shard_map/ppermute | solution.py:293
  24.0 1.6 %collective-permute-start.3 = (f32[1,4,8,128]{3,2,1,0:T(8,128)S(1)}, f32[1,4,8,128]{3,2,1,0:T(8,128)S(1)}, u32[]{:S(2)}, u32[]{:S(2)}) collective-permute-start(f32[1,4,8,128]{3,2,1,0:T(8,128)S(1)} %get-tuple-element.41), channel_id=1, source_target_pairs={{0,1},{1,0},{2,3},{3,2},{4,5},{5,4},{6,7},{7,6},{8,9},{9,8},{10,11... | collective-permute-start | bytes 49160 | tf_op jit(solution)/shard_map/ppermute | solution.py:293
  25.7 2.2 %collective-permute-done.3 = f32[1,4,8,128]{3,2,1,0:T(8,128)S(1)} collective-permute-done((f32[1,4,8,128]{3,2,1,0:T(8,128)S(1)}, f32[1,4,8,128]{3,2,1,0:T(8,128)S(1)}, u32[]{:S(2)}, u32[]{:S(2)}) %collective-permute-start.3) | collective-permute-done | bytes 16416 | tf_op jit(solution)/shard_map/ppermute | solution.py:293
  27.9 2.6 %collective-permute-start.4 = (f32[2,4,8,128]{3,2,1,0:T(8,128)S(1)}, f32[2,4,8,128]{3,2,1,0:T(8,128)S(1)}, u32[]{:S(2)}, u32[]{:S(2)}) collective-permute-start(f32[2,4,8,128]{3,2,1,0:T(8,128)S(1)} %pad_maximum_fusion.3), channel_id=1, source_target_pairs={{0,2},{1,3},{2,0},{3,1},{4,6},{5,7},{6,4},{7,5},{8,10},{9,11},{10,... | collective-permute-start | bytes 98312 | tf_op jit(solution)/shard_map/ppermute | solution.py:293
  30.4 0.1 select_add_fusion.2.fan_ref
  30.5 0.0 copy-done.8
  30.5 0.3 fan.1
  30.9 2.2 %copy-done.1 = f32[4,256,8,128]{3,2,1,0:T(8,128)S(1)} copy-done((f32[4,256,8,128]{3,2,1,0:T(8,128)S(1)}, f32[4,256,8,128]{3,2,1,0:T(8,128)}, u32[]{:S(2)}) %copy-start.1) | copy-done | bytes 4194328
  33.1 2.2 %copy-done.7 = f32[4,256,8,128]{3,2,1,0:T(8,128)S(1)} copy-done((f32[4,256,8,128]{3,2,1,0:T(8,128)S(1)}, f32[4,256,8,128]{3,2,1,0:T(8,128)}, u32[]{:S(2)}) %copy-start.7) | copy-done | bytes 4194328
  35.2 1.5 %ahead.1 = (f32[4,256,8,128]{3,2,1,0:T(8,128)S(1)}, f32[4,256,8,128]{3,2,1,0:T(8,128)S(1)}) custom-call(f32[256,8,128]{2,1,0:T(8,128)S(1)} %get-tuple-element.26.far_ref, f32[4,256,8,128]{3,2,1,0:T(8,128)S(1)} %copy-done.7, f32[4,256,8,128]{3,2,1,0:T(8,128)S(1)} %copy-done.1), custom_call_target="tpu_custom_call" | custom-call | flops 5242880 | bytes 1024 | tf_op jit(solution)/shard_map/ahead/pallas_call | solution.py:371
  36.8 0.0 copy-start.4
  36.8 2.0 %copy-done.4 = f32[4,256,8,128]{3,2,1,0:T(8,128)} copy-done((f32[4,256,8,128]{3,2,1,0:T(8,128)}, f32[4,256,8,128]{3,2,1,0:T(8,128)S(1)}, u32[]{:S(2)}) %copy-start.4) | copy-done | bytes 4194328
  38.8 0.0 collective-permute-done.4
  38.8 2.3 %back.1 = (f32[256,8,128]{2,1,0:T(8,128)S(1)}, f32[8,256]{1,0:T(8,128)S(1)}, f32[4,8,128]{2,1,0:T(8,128)S(1)}, f32[4,8,128]{2,1,0:T(8,128)S(1)}) custom-call(f32[4,16]{1,0:T(4,128)S(1)} %copy-done.9, s32[4]{0:T(128)S(1)} %copy-done.10, f32[8,32]{1,0:T(8,128)S(1)} %get-tuple-element.18.gram_ref, f32[4,8,128]{2,1,0:T(8,128)S(1)} %get-tuple-element.19.pull_ref, ...), custom_call_target="tpu_custom_call" | custom-call | flops 2621440 | bytes 1024 | tf_op jit(solution)/shard_map/back/pallas_call | solution.py:391
  41.1 0.6 %collective-permute-start.5 = (f32[8,256]{1,0:T(8,128)S(1)}, f32[8,256]{1,0:T(8,128)S(1)}, u32[]{:S(2)}, u32[]{:S(2)}) collective-permute-start(f32[8,256]{1,0:T(8,128)S(1)} %get-tuple-element.29), channel_id=1, source_target_pairs={{0,4},{4,0},{1,5},{5,1},{2,6},{6,2},{3,7},{7,3},{8,12},{12,8},{9,1... | collective-permute-start | bytes 24584 | tf_op jit(solution)/shard_map/ppermute | solution.py:293
  41.7 0.8 %signal.1 = f32[4,16,128]{2,1,0:T(8,128)} custom-call(f32[16,32]{1,0:T(8,128)S(1)} %select_add_fusion.2.fan_ref, f32[4,4,8,128]{3,2,1,0:T(8,128)S(1)} %pad_maximum_fusion.lines_ref, f32[4,16,128]{2,1,0:T(8,128)S(1)} %constant_dynamic-slice_fusion.measured_ref), custom_call_target="tpu_custom_call" | custom-call | flops 65536 | bytes 1024 | tf_op jit(solution)/shard_map/signal/pallas_call | solution.py:407
  42.5 2.4 %collective-permute-done.5 = f32[8,256]{1,0:T(8,128)S(1)} collective-permute-done((f32[8,256]{1,0:T(8,128)S(1)}, f32[8,256]{1,0:T(8,128)S(1)}, u32[]{:S(2)}, u32[]{:S(2)}) %collective-permute-start.5) | collective-permute-done | bytes 8224 | tf_op jit(solution)/shard_map/ppermute | solution.py:293
  44.8 0.0 copy-done.11
  44.8 2.2 %copy-done.5 = f32[4,256,8,128]{3,2,1,0:T(8,128)S(1)} copy-done((f32[4,256,8,128]{3,2,1,0:T(8,128)S(1)}, f32[4,256,8,128]{3,2,1,0:T(8,128)}, u32[]{:S(2)}) %copy-start.5) | copy-done | bytes 4194328
  47.0 3.2 %grad.1 = f32[4,8,256,128]{3,2,1,0:T(8,128)} custom-call(f32[4,16]{1,0:T(4,128)S(1)} %copy-done.9, s32[4]{0:T(128)S(1)} %copy-done.10, f32[4]{0:T(128)S(1)} %copy-done.11, f32[8,256]{1,0:T(8,128)S(1)} %broadcast_select_fusion.nearer_ref, f32[4,8,128]{2,1,0:T(8,128)S(1)} %get-tuple-element.30.gain_ref, f32[4,8,128]{2,1,0:T(8,128)S(1)} %get-tuple-element.31.shift_ref, ...), custom_call_target="tpu_custom_call" | custom-call | flops 10485760 | bytes 4194304 | tf_op jit(solution)/shard_map/grad/pallas_call | solution.py:413
  (21 shorter events, 0.1 us)
Async XLA Ops:
  0.6 8.0 %copy-start.13 = (s32[256]{0:T(256)S(1)}, s32[256]{0:T(256)}, u32[]{:S(2)}) copy-start(s32[256]{0:T(256)} %param.11) | copy-start | bytes 3076
  0.6 8.0 %copy-start.12 = (s32[256,4]{0,1:T(4,128)S(1)}, s32[256,4]{0,1:T(4,128)}, u32[]{:S(2)}) copy-start(s32[256,4]{0,1:T(4,128)} %param.12) | copy-start | bytes 12292
  0.7 8.2 %copy-start.10 = (s32[4]{0:T(128)S(1)}, s32[4]{0:T(128)}, u32[]{:S(2)}) copy-start(s32[4]{0:T(128)} %index_ref.5) | copy-start | bytes 52
  0.7 8.2 %copy-start.9 = (f32[4,16]{1,0:T(4,128)S(1)}, f32[4,16]{1,0:T(4,128)}, u32[]{:S(2)}) copy-start(f32[4,16]{1,0:T(4,128)} %cross_ref.5) | copy-start | bytes 772
  3.4 2.0 %copy-start.2 = (f32[4,256,8,128]{3,2,1,0:T(8,128)}, f32[4,256,8,128]{3,2,1,0:T(8,128)S(1)}, u32[]{:S(2)}) copy-start(f32[4,256,8,128]{3,2,1,0:T(8,128)S(1)} %get-tuple-element.21.conc_ref) | copy-start | bytes 12582916
  5.5 9.8 %collective-permute-start = (f32[8,256]{1,0:T(8,128)S(1)}, f32[8,256]{1,0:T(8,128)S(1)}, u32[]{:S(2)}, u32[]{:S(2)}) collective-permute-start(f32[8,256]{1,0:T(8,128)S(1)} %get-tuple-element.20), channel_id=1, source_target_pairs={{0,4},{4,0},{1,5},{5,1},{2,6},{6,2},{3,7},{7,3},{8,12},{12,8},{9,1... | collective-permute-start | bytes 24584 | tf_op jit(solution)/shard_map/ppermute | solution.py:293
  8.8 2.2 %copy-start.3 = (f32[4,256,8,128]{3,2,1,0:T(8,128)S(1)}, f32[4,256,8,128]{3,2,1,0:T(8,128)}, u32[]{:S(2)}) copy-start(f32[4,256,8,128]{3,2,1,0:T(8,128)} %copy-done.2) | copy-start | bytes 12582916
  11.0 19.5 %copy-start.8 = (f32[4,256,128]{2,1,0:T(8,128)S(1)}, f32[4,256,128]{2,1,0:T(8,128)}, u32[]{:S(2)}) copy-start(f32[4,256,128]{2,1,0:T(8,128)} %measured_ref.1) | copy-start | bytes 1572868
  13.3 2.0 %copy-start.6 = (f32[4,256,8,128]{3,2,1,0:T(8,128)}, f32[4,256,8,128]{3,2,1,0:T(8,128)S(1)}, u32[]{:S(2)}) copy-start(f32[4,256,8,128]{3,2,1,0:T(8,128)S(1)} %get-tuple-element.27.trans_ref) | copy-start | bytes 12582916
  16.8 2.0 %copy-start = (f32[4,256,8,128]{3,2,1,0:T(8,128)}, f32[4,256,8,128]{3,2,1,0:T(8,128)S(1)}, u32[]{:S(2)}) copy-start(f32[4,256,8,128]{3,2,1,0:T(8,128)S(1)} %get-tuple-element.23.emit_ref) | copy-start | bytes 12582916
  18.8 1.2 %collective-permute-start.1 = (f32[2,4,8,128]{3,2,1,0:T(8,128)S(1)}, f32[2,4,8,128]{3,2,1,0:T(8,128)S(1)}, u32[]{:S(2)}, u32[]{:S(2)}) collective-permute-start(f32[2,4,8,128]{3,2,1,0:T(8,128)S(1)} %pad_maximum_fusion.1), channel_id=1, source_target_pairs={{0,8},{8,0},{16,24},{24,16},{1,9},{9,1},{17,25},{25,17},{2,10},{10... | collective-permute-start | bytes 98312 | tf_op jit(solution)/shard_map/ppermute | solution.py:293
  20.0 4.0 %collective-permute-start.2 = (f32[2,4,8,128]{3,2,1,0:T(8,128)S(1)}, f32[2,4,8,128]{3,2,1,0:T(8,128)S(1)}, u32[]{:S(2)}, u32[]{:S(2)}) collective-permute-start(f32[2,4,8,128]{3,2,1,0:T(8,128)S(1)} %pad_maximum_fusion.2), channel_id=1, source_target_pairs={{0,16},{8,24},{16,0},{24,8},{1,17},{9,25},{17,1},{25,9},{2,18},{10... | collective-permute-start | bytes 98312 | tf_op jit(solution)/shard_map/ppermute | solution.py:293
  24.0 3.8 %collective-permute-start.3 = (f32[1,4,8,128]{3,2,1,0:T(8,128)S(1)}, f32[1,4,8,128]{3,2,1,0:T(8,128)S(1)}, u32[]{:S(2)}, u32[]{:S(2)}) collective-permute-start(f32[1,4,8,128]{3,2,1,0:T(8,128)S(1)} %get-tuple-element.41), channel_id=1, source_target_pairs={{0,1},{1,0},{2,3},{3,2},{4,5},{5,4},{6,7},{7,6},{8,9},{9,8},{10,11... | collective-permute-start | bytes 49160 | tf_op jit(solution)/shard_map/ppermute | solution.py:293
  27.9 10.9 %collective-permute-start.4 = (f32[2,4,8,128]{3,2,1,0:T(8,128)S(1)}, f32[2,4,8,128]{3,2,1,0:T(8,128)S(1)}, u32[]{:S(2)}, u32[]{:S(2)}) collective-permute-start(f32[2,4,8,128]{3,2,1,0:T(8,128)S(1)} %pad_maximum_fusion.3), channel_id=1, source_target_pairs={{0,2},{1,3},{2,0},{3,1},{4,6},{5,7},{6,4},{7,5},{8,10},{9,11},{10,... | collective-permute-start | bytes 98312 | tf_op jit(solution)/shard_map/ppermute | solution.py:293
  30.8 2.2 %copy-start.1 = (f32[4,256,8,128]{3,2,1,0:T(8,128)S(1)}, f32[4,256,8,128]{3,2,1,0:T(8,128)}, u32[]{:S(2)}) copy-start(f32[4,256,8,128]{3,2,1,0:T(8,128)} %copy-done) | copy-start | bytes 12582916
  33.1 2.2 %copy-start.7 = (f32[4,256,8,128]{3,2,1,0:T(8,128)S(1)}, f32[4,256,8,128]{3,2,1,0:T(8,128)}, u32[]{:S(2)}) copy-start(f32[4,256,8,128]{3,2,1,0:T(8,128)} %copy-done.6) | copy-start | bytes 12582916
  36.8 2.0 %copy-start.4 = (f32[4,256,8,128]{3,2,1,0:T(8,128)}, f32[4,256,8,128]{3,2,1,0:T(8,128)S(1)}, u32[]{:S(2)}) copy-start(f32[4,256,8,128]{3,2,1,0:T(8,128)S(1)} %get-tuple-element.33.rest_ref) | copy-start | bytes 12582916
  38.8 6.0 %copy-start.11 = (f32[4]{0:T(128)S(1)}, f32[4]{0:T(128)}, u32[]{:S(2)}) copy-start(f32[4]{0:T(128)} %line_ref.1) | copy-start | bytes 52
  41.1 3.7 %collective-permute-start.5 = (f32[8,256]{1,0:T(8,128)S(1)}, f32[8,256]{1,0:T(8,128)S(1)}, u32[]{:S(2)}, u32[]{:S(2)}) collective-permute-start(f32[8,256]{1,0:T(8,128)S(1)} %get-tuple-element.29), channel_id=1, source_target_pairs={{0,4},{4,0},{1,5},{5,1},{2,6},{6,2},{3,7},{7,3},{8,12},{12,8},{9,1... | collective-permute-start | bytes 24584 | tf_op jit(solution)/shard_map/ppermute | solution.py:293
  44.8 2.2 %copy-start.5 = (f32[4,256,8,128]{3,2,1,0:T(8,128)S(1)}, f32[4,256,8,128]{3,2,1,0:T(8,128)}, u32[]{:S(2)}) copy-start(f32[4,256,8,128]{3,2,1,0:T(8,128)} %copy-done.4) | copy-start | bytes 12582916

commit v2 on v1

--- a/solution.py
+++ b/solution.py
@@ -129,6 +129,12 @@
         depth_ref[e] = path[e]
 
 
+def reached(axis, count, backward):
+    if count != 2:
+        return True
+    return lax.axis_index(axis) == (1 if backward else 0)
+
+
 def spread(source_ref, change, width, body, init):
     depth, rows = source_ref.shape
     carry = init
@@ -146,17 +152,40 @@
     return carry
 
 
-def line_body(far_ref, emit_ref, far_out, line_ref):
+def line_body(count, far_ref, emit_ref, depth_ref, far_out, pair_ref):
     n_energy, rows, depth, width = emit_ref.shape
+    keep = jnp.where(reached("det", count, False), 1.0, 0.0)
 
     def one(x, factor, sums):
         far_out[x] = factor
         return tuple(sums[e] + factor * emit_ref[e, x] for e in range(n_energy))
 
     zero = jnp.zeros((depth, width), F32)
-    sums = spread(far_ref, jnp.exp2, width, one, (zero,) * n_energy)
+    sums = spread(far_ref, lambda v: jnp.exp2(v * keep), width, one, (zero,) * n_energy)
     for e in range(n_energy):
-        line_ref[e] = sums[e]
+        pair_ref[0, e] = depth_ref[e]
+        pair_ref[1, e] = sums[e]
+
+
+def merge_body(distance, first_round, own_ref, other_ref, up_ref, further_ref, out_ref, up_out, further_out):
+    lower = (lax.axis_index("beam") & distance) == 0
+    span, sums = own_ref[0], own_ref[1]
+    first = jnp.where(lower, span, other_ref[0])
+    fade = jnp.exp2(first)
+    late = fade * jnp.where(lower, other_ref[1], sums)
+    zero = jnp.zeros_like(late)
+    if first_round:
+        further_out[...] = jnp.where(lower, late, zero)
+        up_out[...] = jnp.where(lower, zero, first)
+    else:
+        further_out[...] = jnp.where(lower, further_ref[...] + late, fade * further_ref[...])
+        up_out[...] = up_ref[...] + jnp.where(lower, zero, first)
+    total = jnp.where(lower, sums, other_ref[1]) + late
+    if out_ref.shape[0] == 2:
+        out_ref[0] = span + other_ref[0]
+        out_ref[1] = total
+    else:
+        out_ref[0] = total
 
 
 def ahead_body(far_ref, trans_ref, emit_ref, fluor_ref, rest_ref):
@@ -178,31 +207,46 @@
     lax.fori_loop(0, rows // STEP, step, (zero,) * n_energy)
 
 
-def fan_body(fan_ref, measured_ref, gram_ref, pull_ref):
-    depth = pull_ref.shape[1]
-    own = fan_ref[:depth, :]
+def fan_body(offset_ref, weight_ref, measured_ref, gram_ref, pull_ref, turned_ref):
+    depth, n_slices = gram_ref.shape
+    taps, pixels = weight_ref.shape
+    slab = lax.axis_index("slab")
+    offset = jnp.broadcast_to(offset_ref[...], (depth, pixels))
+    level = lax.broadcasted_iota(jnp.int32, (depth, pixels), 0)
+    blocks = []
+    for r in range(n_slices // depth):
+        place = level + (slab ^ r) * depth - offset
+        block = jnp.zeros((depth, pixels), F32)
+        for j in range(taps):
+            tap = jnp.broadcast_to(weight_ref[j : j + 1, :], (depth, pixels)).astype(F32)
+            block = block + jnp.where(place == j, tap, 0.0)
+        blocks.append(block)
+    every = jnp.concatenate(blocks, axis=0)
+    turned_ref[...] = every.T
     gram_ref[...] = lax.dot_general(
-        own.astype(BF16), fan_ref[...].astype(BF16), (((1,), (1,)), ((), ())), preferred_element_type=F32
+        blocks[0].astype(BF16), every.astype(BF16), (((1,), (1,)), ((), ())), preferred_element_type=F32
     )
     for e in range(pull_ref.shape[0]):
         pull_ref[e] = jnp.dot(
-            own, measured_ref[e], precision=lax.Precision.HIGHEST, preferred_element_type=F32
+            blocks[0], measured_ref[e], precision=lax.Precision.HIGHEST, preferred_element_type=F32
         )
 
 
-def back_body(
-    scale, cross_ref, index_ref, gram_ref, pull_ref, lines_ref, up_ref, further_ref, fluor_ref,
-    near_ref, total_ref, gain_ref, shift_ref,
-):
+def slices_of(refs):
+    return [(ref, i) for ref in refs for i in range(ref.shape[0])]
+
+
+def back_body(scale, cross_ref, index_ref, gram_ref, pull_ref, up_ref, further_ref, fluor_ref, *refs):
+    lines, (near_ref, total_ref, gain_ref, shift_ref) = slices_of(refs[:-4]), refs[-4:]
     n_energy, rows, depth, width = fluor_ref.shape
     n_species = shift_ref.shape[0]
     sums = [None] * n_energy
-    for r in range(lines_ref.shape[0]):
+    for r, (lines_ref, i) in enumerate(lines):
         for z in range(depth):
             place = r * depth + z
             weight = jnp.broadcast_to(gram_ref[:, place : place + 1], (depth, width))
             for e in range(n_energy):
-                value = weight * lines_ref[r, e, z : z + 1, :]
+                value = weight * lines_ref[i, e, z : z + 1, :]
                 sums[e] = value if place == 0 else sums[e] + value
     back = [sums[e] * scale - pull_ref[e] for e in range(n_energy)]
     gain = [back[e] * jnp.exp2(up_ref[e]) for e in range(n_energy)]
@@ -232,7 +276,7 @@
 
 
 def grad_body(
-    scale, cross_ref, index_ref, line_ref, nearer_ref, gain_ref, shift_ref, near_ref, rest_ref,
+    scale, count, cross_ref, index_ref, line_ref, nearer_ref, gain_ref, shift_ref, near_ref, rest_ref,
     out_hbm, out_ref, sems,
 ):
     n_energy, rows, depth, width = rest_ref.shape
@@ -241,6 +285,7 @@
     mixed = [[sigma[s][e] * gain_ref[e] for e in range(n_energy)] for s in range(n_species)]
     shift = [shift_ref[s] for s in range(n_species)]
     line = [line_ref[s] * scale for s in range(n_species)]
+    keep = jnp.where(reached("det", count, True), 1.0, 0.0)
 
     def copies(chunk):
         span = pl.ds(chunk * CHUNK, CHUNK)
@@ -264,7 +309,7 @@
                 copy.start()
             return pltpu.roll(held, LANES - CHUNK, 1)
 
-        lax.fori_loop(0, LANES // CHUNK, step, nearer_ref[:, part * LANES : (part + 1) * LANES])
+        lax.fori_loop(0, LANES // CHUNK, step, nearer_ref[:, part * LANES : (part + 1) * LANES] * keep)
 
     def finish(chunk, carry):
         for copy in copies(chunk):
@@ -274,19 +319,22 @@
     lax.fori_loop(0, rows // CHUNK, finish, 0)
 
 
-def signal_body(scale, fan_ref, lines_ref, measured_ref, out_ref):
+def signal_body(scale, fan_ref, measured_ref, *refs):
+    lines, out_ref = slices_of(refs[:-1]), refs[-1]
     n_energy, share, width = out_ref.shape
-    depth = lines_ref.shape[2]
+    depth = fan_ref.shape[1] // len(lines)
+    start = pl.multiple_of(lax.axis_index(("beam", "slab")) * share, share)
+    fan = fan_ref[pl.ds(start, share), :]
     sums = [None] * n_energy
-    for r in range(lines_ref.shape[0]):
+    for r, (lines_ref, i) in enumerate(lines):
         for z in range(depth):
             place = r * depth + z
-            weight = jnp.broadcast_to(fan_ref[:, place : place + 1], (share, width))
+            weight = jnp.broadcast_to(fan[:, place : place + 1], (share, width))
             for e in range(n_energy):
-                value = weight * lines_ref[r, e, z : z + 1, :]
+                value = weight * lines_ref[i, e, z : z + 1, :]
                 sums[e] = value if place == 0 else sums[e] + value
     for e in range(n_energy):
-        out_ref[e] = sums[e] * scale - measured_ref[e]
+        out_ref[e] = sums[e] * scale - measured_ref[e, pl.ds(start, share), :]
 
 
 def swap(value, axis, distance):
@@ -294,23 +342,14 @@
 
 
 def beyond(value, axis, backward):
-    count, mine = lax.axis_size(axis), lax.axis_index(axis)
+    count = lax.axis_size(axis)
     if count == 2:
-        keep = (mine == 1) if backward else (mine == 0)
-        return jnp.where(keep, swap(value, axis, 1), 0.0)
+        return swap(value, axis, 1)
+    mine = lax.axis_index(axis)
     pieces = lax.all_gather(value, axis)
     places = jnp.arange(count)
     keep = (places < mine) if backward else (places > mine)
     return jnp.sum(jnp.where(keep.reshape((-1,) + (1,) * value.ndim), pieces, 0.0), axis=0)
-
-
-def fan_rows(fan_offset, fan_weight, slices):
-    taps = fan_weight.shape[1]
-    total = 0.0
-    for j in range(taps):
-        match = slices[:, None] == fan_offset[None, :] + j
-        total = total + jnp.where(match, fan_weight[:, j].astype(F32)[None, :], 0.0)
-    return total
 
 
 def shards(conc, cross, line, index, fan_offset, fan_weight, measured):
@@ -347,25 +386,22 @@
         cost=(40 * voxels, 4 * voxels, 1024),
     )(cross, index, conc_x, far_local)
 
-    far_wide, own_line = call(
-        line_body, "line", (plane, plain(n_energy, depth, width)), (VMEM, VMEM), (VMEM, VMEM),
+    wide = (n_energy, depth, width)
+    far_wide, pair = call(
+        functools.partial(line_body, n_det), "line", (plane, plain(2, *wide)), (VMEM,) * 2, (VMEM,) * 3,
         cost=(8 * voxels, 0, 1024),
-    )(far, emit)
-
-    beam = lax.axis_index("beam")
-    span, sums = own_depth, own_line
-    up, further = jnp.zeros_like(own_depth), jnp.zeros_like(own_line)
+    )(far, emit, own_depth)
+
+    up = further = own_depth
     distance = 1
     while distance < n_beam:
-        other = swap(jnp.stack([span, sums]), "beam", distance)
-        lower = (beam & distance) == 0
-        first = jnp.where(lower, span, other[0])
-        fade = jnp.exp2(first)
-        late = fade * jnp.where(lower, other[1], sums)
-        further = jnp.where(lower, further + late, fade * further)
-        up = jnp.where(lower, up, up + first)
-        sums = jnp.where(lower, sums, other[1]) + late
-        span = span + other[0]
+        other = swap(pair, "beam", distance)
+        kept = 1 if 2 * distance == n_beam else 2
+        pair, up, further = call(
+            functools.partial(merge_body, distance, distance == 1),
+            "merge", (plain(kept, *wide), plain(*wide), plain(*wide)), (VMEM,) * 3, (VMEM,) * 4,
+            cost=(1 << 14, 1 << 12, 1024),
+        )(pair, other, up, further)
         distance *= 2
 
     fluor, rest = call(
@@ -373,45 +409,38 @@
         cost=(20 * voxels, 0, 1024),
     )(far_wide, trans, emit)
 
-    lines = sums[None]
+    lines = [pair]
     distance = 1
     while distance < n_slab:
-        lines = jnp.concatenate([lines, swap(lines, "slab", distance)], axis=0)
+        whole = lines[0] if distance == 1 else jnp.concatenate(lines, axis=0)
+        lines.append(swap(whole, "slab", distance))
         distance *= 2
 
-    slab = lax.axis_index("slab")
-    order = (slab ^ jnp.arange(n_slab, dtype=jnp.int32))[:, None] * depth
-    slices = (order + jnp.arange(depth, dtype=jnp.int32)[None, :]).reshape(-1)
-    fan_all = fan_rows(fan_offset, fan_weight, slices)
-    gram, pull = call(
-        fan_body, "fan", (plain(depth, depth * n_slab), plain(n_energy, depth, width)),
-        (VMEM, VMEM), (VMEM, VMEM), cost=(4 * 2 * depth * measured.size // width * width, 0, 4 * measured.size),
-    )(fan_all, measured)
+    pixels = fan_offset.shape[0]
+    gram, pull, fan_turned = call(
+        fan_body, "fan", (plain(depth, depth * n_slab), plain(*wide), plain(pixels, depth * n_slab)),
+        (VMEM,) * 3, (VMEM,) * 3, cost=(8 * depth * measured.size, 0, 4 * measured.size),
+    )(fan_offset[None, :], fan_weight.T, measured)
 
     near, column_total, gain, shift = call(
         functools.partial(back_body, 1.0 / (scale_x * full_x)),
         "back",
-        (plane, plain(depth, rows), plain(n_energy, depth, width), plain(n_species, depth, width)),
+        (plane, plain(depth, rows), plain(*wide), plain(n_species, depth, width)),
         (VMEM,) * 4,
-        (SMEM, SMEM) + (VMEM,) * 6,
+        (SMEM, SMEM) + (VMEM,) * (5 + len(lines)),
         cost=(10 * voxels, 0, 1024),
-    )(cross, index, gram, pull, lines, up, further, fluor)
+    )(cross, index, gram, pull, up, further, fluor, *lines)
 
     nearer = beyond(column_total, "det", True)
 
-    share = fan_offset.shape[0] // (n_beam * n_slab)
-    start = lax.axis_index(("beam", "slab")) * share
-    fan_own = fan_rows(
-        lax.dynamic_slice_in_dim(fan_offset, start, share), lax.dynamic_slice_in_dim(fan_weight, start, share), slices
-    ).T
     residual = call(
         functools.partial(signal_body, 1.0 / (scale_x * full_x)),
-        "signal", (plain(n_energy, share, width),), (VMEM,), (VMEM, VMEM, VMEM),
+        "signal", (plain(n_energy, pixels // (n_beam * n_slab), width),), (VMEM,), (VMEM,) * (2 + len(lines)),
         cost=(1 << 16, 0, 1024),
-    )(fan_own, lines, lax.dynamic_slice_in_dim(measured, start, share, 1))[0]
+    )(fan_turned, measured, *lines)[0]
 
     grad = call(
-        functools.partial(grad_body, 1.0 / scale_x * scale_y * LN2),
+        functools.partial(grad_body, scale_y * LN2 / scale_x, n_det),
         "grad",
         (plain(n_species, depth, rows, width),),
         (HBM,),

time: 50.5 us -> 33.6 us (0.67)
  local copies, waits for them, and re-layouts: 16.9 us -> 0.03 us
  starting transfers between devices: 9.36 us -> 10.3 us
    unnamed x28 -> x12, local copies, waits for them, and re-layouts: 16.8 us -> 0.03 us
    ppermute x6, starting transfers between devices: 9.36 us -> 10.3 us  [swap(): lax.ppermute(value, axis, [(i, i ^ distance) for i in range(lax.axis_size...]
    pallas_call x3 -> x5, Pallas kernels: 4.99 us -> 5.08 us  [the longest x1 3.17 us: shards(): call(functools.partial(grad_body, scale_y * LN2 / scale_x, n_det), 'grad'...]
  transfers between devices with their start and end apart: 6 -> 6, of which waited for: 4 -> 5; matrix products, arithmetic and copies ran while one was open for 1% -> 0% of each run, Pallas kernels for 10% -> 15%
where the time goes in v2:
time: 33.6 us; the launch traced here: 33.4 us
  Pallas kernels  14.7 us (44%)
  starting transfers between devices  10.3 us (31%)
  waiting for transfers between devices  7.63 us (23%)
  between operations  0.73 us (2%)
    ppermute x6, starting transfers between devices, swap(): lax.ppermute(value, axis, [(i, i ^ distance) for i in range(lax.axis_size...  10.3 us
    ppermute x6, waiting for transfers between devices, swap(): lax.ppermute(value, axis, [(i, i ^ distance) for i in range(lax.axis_size...  7.63 us
    pallas_call x1, Pallas kernels, shards(): call(functools.partial(grad_body, scale_y * LN2 / scale_x, n_det), 'grad'...  3.17 us
    pallas_call x1, Pallas kernels, shards(): call(functools.partial(load_body, scale_y), 'load', (VMEM((n_species, row...  2.76 us
    pallas_call x1, Pallas kernels, shards(): call(functools.partial(back_body, 1.0 / (scale_x * full_x)), 'back', (pla...  2.3 us
    pallas_call x1, Pallas kernels, shards(): call(functools.partial(local_body, scale_x), 'local', (cube, cube, plain(...  2.25 us
    pallas_call x1, Pallas kernels, shards(): call(functools.partial(line_body, n_det), 'line', (plane, plain(2, *wide)...  1.53 us
    pallas_call x1, Pallas kernels, shards(): call(ahead_body, 'ahead', (cube, cube), (VMEM, VMEM), (VMEM, VMEM, VMEM),...  1.52 us
  transfers between devices with their start and end apart: 6, of which 5 were waited for; matrix products, arithmetic and copies ran while one was open for 0% of the time, Pallas kernels for 15%

profile of v2, /device:TPU:0, one launch (start us, length us, event | category | flops | bytes accessed | tf_op | source)
XLA Modules:
  0.0 33.4 jit_solution(16221406981458299543)
XLA Ops:
  0.6 0.0 copy-start.2
  0.6 0.0 copy-start.1
  0.6 2.8 %load.1 = (f32[4,256,8,128]{3,2,1,0:T(8,128)S(1)}, f32[256,8,128]{2,1,0:T(8,128)S(1)}, f32[8,256]{1,0:T(8,128)S(1)}) custom-call(f32[4]{0:T(128)} %line_ref.1, f32[4,8,256,128]{3,2,1,0:T(8,128)} %conc_hbm.1), custom_call_target="tpu_custom_call" | custom-call | flops 2097152 | bytes 4194304 | tf_op jit(solution)/shard_map/load/pallas_call | solution.py:368
  3.4 3.1 %collective-permute-start = (f32[8,256]{1,0:T(8,128)S(1)}, f32[8,256]{1,0:T(8,128)S(1)}, u32[]{:S(2)}, u32[]{:S(2)}) collective-permute-start(f32[8,256]{1,0:T(8,128)S(1)} %get-tuple-element.27), channel_id=1, source_target_pairs={{0,4},{4,0},{1,5},{5,1},{2,6},{6,2},{3,7},{7,3},{8,12},{12,8},{9,1... | collective-permute-start | bytes 24584 | tf_op jit(solution)/shard_map/ppermute | solution.py:341
  6.5 0.0 copy-done.2
  6.5 0.0 copy-done.1
  6.5 0.0 copy-start
  6.5 0.0 copy-start.3
  6.5 0.0 copy-start.5
  6.5 2.3 %local.1 = (f32[4,256,8,128]{3,2,1,0:T(8,128)S(1)}, f32[4,256,8,128]{3,2,1,0:T(8,128)S(1)}, f32[4,8,128]{2,1,0:T(8,128)S(1)}) custom-call(f32[4,16]{1,0:T(4,128)S(1)} %copy-done.1, s32[4]{0:T(128)S(1)} %copy-done.2, f32[4,256,8,128]{3,2,1,0:T(8,128)S(1)} %get-tuple-element.28.conc_ref, f32[256,8,128]{2,1,0:T(8,128)S(1)} %get-tuple-element.29.beyond_ref), custom_call_target="tpu_custom_call" | custom-call | flops 10485760 | bytes 1024 | tf_op jit(solution)/shard_map/local/pallas_call | solution.py:380
  8.8 0.0 collective-permute-done.far_ref
  8.8 1.5 %line.1 = (f32[256,8,128]{2,1,0:T(8,128)S(1)}, f32[2,4,8,128]{3,2,1,0:T(8,128)S(1)}) custom-call(f32[8,256]{1,0:T(8,128)S(1)} %collective-permute-done.far_ref, f32[4,256,8,128]{3,2,1,0:T(8,128)S(1)} %get-tuple-element.30.emit_ref, f32[4,8,128]{2,1,0:T(8,128)S(1)} %get-tuple-element.31.depth_ref.up_ref.further_ref), custom_call_target="tpu_custom_call" | custom-call | flops 2097152 | bytes 1024 | tf_op jit(solution)/shard_map/line/pallas_call | solution.py:390
  10.3 0.1 collective-permute-start.1
  10.4 1.2 %collective-permute-done.1.other_ref = f32[2,4,8,128]{3,2,1,0:T(8,128)S(1)} collective-permute-done((f32[2,4,8,128]{3,2,1,0:T(8,128)S(1)}, f32[2,4,8,128]{3,2,1,0:T(8,128)S(1)}, u32[]{:S(2)}, u32[]{:S(2)}) %collective-permute-start.1) | collective-permute-done | bytes 32800 | tf_op jit(solution)/shard_map/ppermute | solution.py:341
  11.6 1.6 %collective-permute-start.2 = (f32[2,4,8,128]{3,2,1,0:T(8,128)S(1)}, f32[2,4,8,128]{3,2,1,0:T(8,128)S(1)}, u32[]{:S(2)}, u32[]{:S(2)}) collective-permute-start(f32[2,4,8,128]{3,2,1,0:T(8,128)S(1)} %get-tuple-element.33.own_ref), channel_id=1, source_target_pairs={{0,16},{8,24},{16,0},{24,8},{1,17},{9,25},{17,1},{25,9},{2,18},{10... | collective-permute-start | bytes 98312 | tf_op jit(solution)/shard_map/ppermute | solution.py:341
  13.2 2.4 %collective-permute-done.2.other_ref = f32[2,4,8,128]{3,2,1,0:T(8,128)S(1)} collective-permute-done((f32[2,4,8,128]{3,2,1,0:T(8,128)S(1)}, f32[2,4,8,128]{3,2,1,0:T(8,128)S(1)}, u32[]{:S(2)}, u32[]{:S(2)}) %collective-permute-start.2) | collective-permute-done | bytes 32800 | tf_op jit(solution)/shard_map/ppermute | solution.py:341
  15.6 1.6 %collective-permute-start.3 = (f32[1,4,8,128]{3,2,1,0:T(8,128)S(1)}, f32[1,4,8,128]{3,2,1,0:T(8,128)S(1)}, u32[]{:S(2)}, u32[]{:S(2)}) collective-permute-start(f32[1,4,8,128]{3,2,1,0:T(8,128)S(1)} %get-tuple-element.41.refs_0_), channel_id=1, source_target_pairs={{0,1},{1,0},{2,3},{3,2},{4,5},{5,4},{6,7},{7,6},{8,9},{9,8},{10,11... | collective-permute-start | bytes 49160 | tf_op jit(solution)/shard_map/ppermute | solution.py:341
  17.2 2.2 %collective-permute-done.3.refs_1_ = f32[1,4,8,128]{3,2,1,0:T(8,128)S(1)} collective-permute-done((f32[1,4,8,128]{3,2,1,0:T(8,128)S(1)}, f32[1,4,8,128]{3,2,1,0:T(8,128)S(1)}, u32[]{:S(2)}, u32[]{:S(2)}) %collective-permute-start.3) | collective-permute-done | bytes 16416 | tf_op jit(solution)/shard_map/ppermute | solution.py:341
  19.4 2.6 %collective-permute-start.4 = (f32[2,4,8,128]{3,2,1,0:T(8,128)S(1)}, f32[2,4,8,128]{3,2,1,0:T(8,128)S(1)}, u32[]{:S(2)}, u32[]{:S(2)}) collective-permute-start(f32[2,4,8,128]{3,2,1,0:T(8,128)S(1)} %pad_maximum_fusion), channel_id=1, source_target_pairs={{0,2},{1,3},{2,0},{3,1},{4,6},{5,7},{6,4},{7,5},{8,10},{9,11},{10,... | collective-permute-start | bytes 98312 | tf_op jit(solution)/shard_map/ppermute | solution.py:341
  22.0 0.0 copy-done
  22.0 0.0 copy-done.3
  22.0 0.0 copy-done.5
  22.0 0.3 %fan.1 = (f32[8,32]{1,0:T(8,128)S(1)}, f32[4,8,128]{2,1,0:T(8,128)S(1)}, f32[256,32]{1,0:T(8,128)S(1)}) custom-call(s32[1,256]{1,0:T(1,128)S(1)} %bitcast.3, s32[4,256]{1,0:T(4,128)S(1)} %bitcast.2, f32[4,256,128]{2,1,0:T(8,128)S(1)} %copy-done), custom_call_target="tpu_custom_call" | custom-call | flops 8388608 | bytes 524288 | tf_op jit(solution)/shard_map/fan/pallas_call | solution.py:420
  22.4 1.5 %ahead.1 = (f32[4,256,8,128]{3,2,1,0:T(8,128)S(1)}, f32[4,256,8,128]{3,2,1,0:T(8,128)S(1)}) custom-call(f32[256,8,128]{2,1,0:T(8,128)S(1)} %get-tuple-element.38.far_ref, f32[4,256,8,128]{3,2,1,0:T(8,128)S(1)} %get-tuple-element.39.trans_ref, f32[4,256,8,128]{3,2,1,0:T(8,128)S(1)} %get-tuple-element.30.emit_ref), custom_call_target="tpu_custom_call" | custom-call | flops 5242880 | bytes 1024 | tf_op jit(solution)/shard_map/ahead/pallas_call | solution.py:407
  23.9 0.0 copy-start.4
  23.9 0.3 %collective-permute-done.4.refs_2_ = f32[2,4,8,128]{3,2,1,0:T(8,128)S(1)} collective-permute-done((f32[2,4,8,128]{3,2,1,0:T(8,128)S(1)}, f32[2,4,8,128]{3,2,1,0:T(8,128)S(1)}, u32[]{:S(2)}, u32[]{:S(2)}) %collective-permute-start.4) | collective-permute-done | bytes 32800 | tf_op jit(solution)/shard_map/ppermute | solution.py:341
  24.2 2.3 %back.1 = (f32[256,8,128]{2,1,0:T(8,128)S(1)}, f32[8,256]{1,0:T(8,128)S(1)}, f32[4,8,128]{2,1,0:T(8,128)S(1)}, f32[4,8,128]{2,1,0:T(8,128)S(1)}) custom-call(f32[4,16]{1,0:T(4,128)S(1)} %copy-done.1, s32[4]{0:T(128)S(1)} %copy-done.2, f32[8,32]{1,0:T(8,128)S(1)} %get-tuple-element.25.gram_ref, f32[4,8,128]{2,1,0:T(8,128)S(1)} %get-tuple-element.26.pull_ref, ...), custom_call_target="tpu_custom_call" | custom-call | flops 2621440 | bytes 1024 | tf_op jit(solution)/shard_map/back/pallas_call | solution.py:425
  26.5 1.4 %collective-permute-start.5 = (f32[8,256]{1,0:T(8,128)S(1)}, f32[8,256]{1,0:T(8,128)S(1)}, u32[]{:S(2)}, u32[]{:S(2)}) collective-permute-start(f32[8,256]{1,0:T(8,128)S(1)} %get-tuple-element.42), channel_id=1, source_target_pairs={{0,4},{4,0},{1,5},{5,1},{2,6},{6,2},{3,7},{7,3},{8,12},{12,8},{9,1... | collective-permute-start | bytes 24584 | tf_op jit(solution)/shard_map/ppermute | solution.py:341
  27.9 0.8 %signal.1 = f32[4,16,128]{2,1,0:T(8,128)} custom-call(f32[256,32]{1,0:T(8,128)S(1)} %get-tuple-element.47.fan_ref, f32[4,256,128]{2,1,0:T(8,128)S(1)} %copy-done, f32[1,4,8,128]{3,2,1,0:T(8,128)S(1)} %get-tuple-element.41.refs_0_, f32[1,4,8,128]{3,2,1,0:T(8,128)S(1)} %collective-permute-done.3.refs_1_, f32[2,4,8,128]{3,2,1,0:T(8,128)S(1)} %collective-permute-done.4.refs_2_), custom_call_target="tpu_custom_call" | custom-call | flops 65536 | bytes 1024 | tf_op jit(solution)/shard_map/signal/pallas_call | solution.py:436
  28.7 1.5 %collective-permute-done.5.nearer_ref = f32[8,256]{1,0:T(8,128)S(1)} collective-permute-done((f32[8,256]{1,0:T(8,128)S(1)}, f32[8,256]{1,0:T(8,128)S(1)}, u32[]{:S(2)}, u32[]{:S(2)}) %collective-permute-start.5) | collective-permute-done | bytes 8224 | tf_op jit(solution)/shard_map/ppermute | solution.py:341
  30.3 0.0 copy-done.4
  30.3 3.2 %grad.1 = f32[4,8,256,128]{3,2,1,0:T(8,128)} custom-call(f32[4,16]{1,0:T(4,128)S(1)} %copy-done.1, s32[4]{0:T(128)S(1)} %copy-done.2, f32[4]{0:T(128)S(1)} %copy-done.4, f32[8,256]{1,0:T(8,128)S(1)} %collective-permute-done.5.nearer_ref, f32[4,8,128]{2,1,0:T(8,128)S(1)} %get-tuple-element.43.gain_ref, f32[4,8,128]{2,1,0:T(8,128)S(1)} %get-tuple-element.44.shift_ref, ...), custom_call_target="tpu_custom_call" | custom-call | flops 10485760 | bytes 4194304 | tf_op jit(solution)/shard_map/grad/pallas_call | solution.py:442
  (3 shorter events, 0.0 us)
Async XLA Ops:
  0.6 5.9 %copy-start.2 = (s32[4]{0:T(128)S(1)}, s32[4]{0:T(128)}, u32[]{:S(2)}) copy-start(s32[4]{0:T(128)} %index_ref.5) | copy-start | bytes 52
  0.6 5.8 %copy-start.1 = (f32[4,16]{1,0:T(4,128)S(1)}, f32[4,16]{1,0:T(4,128)}, u32[]{:S(2)}) copy-start(f32[4,16]{1,0:T(4,128)} %cross_ref.5) | copy-start | bytes 772
  3.4 5.4 %collective-permute-start = (f32[8,256]{1,0:T(8,128)S(1)}, f32[8,256]{1,0:T(8,128)S(1)}, u32[]{:S(2)}, u32[]{:S(2)}) collective-permute-start(f32[8,256]{1,0:T(8,128)S(1)} %get-tuple-element.27), channel_id=1, source_target_pairs={{0,4},{4,0},{1,5},{5,1},{2,6},{6,2},{3,7},{7,3},{8,12},{12,8},{9,1... | collective-permute-start | bytes 24584 | tf_op jit(solution)/shard_map/ppermute | solution.py:341
  6.5 15.5 %copy-start = (f32[4,256,128]{2,1,0:T(8,128)S(1)}, f32[4,256,128]{2,1,0:T(8,128)}, u32[]{:S(2)}) copy-start(f32[4,256,128]{2,1,0:T(8,128)} %measured_ref.3) | copy-start | bytes 1572868
  6.5 15.5 %copy-start.3 = (s32[256,4]{0,1:T(4,128)S(1)}, s32[256,4]{0,1:T(4,128)}, u32[]{:S(2)}) copy-start(s32[256,4]{0,1:T(4,128)} %param.12) | copy-start | bytes 12292
  6.5 15.5 %copy-start.5 = (s32[256]{0:T(256)S(1)}, s32[256]{0:T(256)}, u32[]{:S(2)}) copy-start(s32[256]{0:T(256)} %param.11) | copy-start | bytes 3076
  10.3 1.3 %collective-permute-start.1 = (f32[2,4,8,128]{3,2,1,0:T(8,128)S(1)}, f32[2,4,8,128]{3,2,1,0:T(8,128)S(1)}, u32[]{:S(2)}, u32[]{:S(2)}) collective-permute-start(f32[2,4,8,128]{3,2,1,0:T(8,128)S(1)} %get-tuple-element.32.own_ref), channel_id=1, source_target_pairs={{0,8},{8,0},{16,24},{24,16},{1,9},{9,1},{17,25},{25,17},{2,10},{10... | collective-permute-start | bytes 98312 | tf_op jit(solution)/shard_map/ppermute | solution.py:341
  11.6 4.0 %collective-permute-start.2 = (f32[2,4,8,128]{3,2,1,0:T(8,128)S(1)}, f32[2,4,8,128]{3,2,1,0:T(8,128)S(1)}, u32[]{:S(2)}, u32[]{:S(2)}) collective-permute-start(f32[2,4,8,128]{3,2,1,0:T(8,128)S(1)} %get-tuple-element.33.own_ref), channel_id=1, source_target_pairs={{0,16},{8,24},{16,0},{24,8},{1,17},{9,25},{17,1},{25,9},{2,18},{10... | collective-permute-start | bytes 98312 | tf_op jit(solution)/shard_map/ppermute | solution.py:341
  15.6 3.8 %collective-permute-start.3 = (f32[1,4,8,128]{3,2,1,0:T(8,128)S(1)}, f32[1,4,8,128]{3,2,1,0:T(8,128)S(1)}, u32[]{:S(2)}, u32[]{:S(2)}) collective-permute-start(f32[1,4,8,128]{3,2,1,0:T(8,128)S(1)} %get-tuple-element.41.refs_0_), channel_id=1, source_target_pairs={{0,1},{1,0},{2,3},{3,2},{4,5},{5,4},{6,7},{7,6},{8,9},{9,8},{10,11... | collective-permute-start | bytes 49160 | tf_op jit(solution)/shard_map/ppermute | solution.py:341
  19.4 4.8 %collective-permute-start.4 = (f32[2,4,8,128]{3,2,1,0:T(8,128)S(1)}, f32[2,4,8,128]{3,2,1,0:T(8,128)S(1)}, u32[]{:S(2)}, u32[]{:S(2)}) collective-permute-start(f32[2,4,8,128]{3,2,1,0:T(8,128)S(1)} %pad_maximum_fusion), channel_id=1, source_target_pairs={{0,2},{1,3},{2,0},{3,1},{4,6},{5,7},{6,4},{7,5},{8,10},{9,11},{10,... | collective-permute-start | bytes 98312 | tf_op jit(solution)/shard_map/ppermute | solution.py:341
  23.9 6.4 %copy-start.4 = (f32[4]{0:T(128)S(1)}, f32[4]{0:T(128)}, u32[]{:S(2)}) copy-start(f32[4]{0:T(128)} %line_ref.1) | copy-start | bytes 52
  26.5 3.7 %collective-permute-start.5 = (f32[8,256]{1,0:T(8,128)S(1)}, f32[8,256]{1,0:T(8,128)S(1)}, u32[]{:S(2)}, u32[]{:S(2)}) collective-permute-start(f32[8,256]{1,0:T(8,128)S(1)} %get-tuple-element.42), channel_id=1, source_target_pairs={{0,4},{4,0},{1,5},{5,1},{2,6},{6,2},{3,7},{7,3},{8,12},{12,8},{9,1... | collective-permute-start | bytes 24584 | tf_op jit(solution)/shard_map/ppermute | solution.py:341

commit v3 on v2

--- a/solution.py
+++ b/solution.py
@@ -135,36 +135,26 @@
     return lax.axis_index(axis) == (1 if backward else 0)
 
 
-def spread(source_ref, change, width, body, init):
+def columns(source_ref, change, width):
     depth, rows = source_ref.shape
-    carry = init
     for part in range(rows // LANES):
         held = change(source_ref[:, part * LANES : (part + 1) * LANES])
-
-        def step(block, state):
-            held, carry = state
-            for q in range(STEP):
-                column = jnp.broadcast_to(held[:, q : q + 1], (depth, width))
-                carry = body(part * LANES + block * STEP + q, column, carry)
-            return pltpu.roll(held, LANES - STEP, 1), carry
-
-        _, carry = lax.fori_loop(0, LANES // STEP, step, (held, carry))
-    return carry
+        for q in range(LANES):
+            yield part * LANES + q, jnp.broadcast_to(held[:, q : q + 1], (depth, width))
 
 
 def line_body(count, far_ref, emit_ref, depth_ref, far_out, pair_ref):
     n_energy, rows, depth, width = emit_ref.shape
     keep = jnp.where(reached("det", count, False), 1.0, 0.0)
-
-    def one(x, factor, sums):
+    sums = [[None, None] for _ in range(n_energy)]
+    for x, factor in columns(far_ref, lambda v: jnp.exp2(v * keep), width):
         far_out[x] = factor
-        return tuple(sums[e] + factor * emit_ref[e, x] for e in range(n_energy))
-
-    zero = jnp.zeros((depth, width), F32)
-    sums = spread(far_ref, lambda v: jnp.exp2(v * keep), width, one, (zero,) * n_energy)
+        for e in range(n_energy):
+            value = factor * emit_ref[e, x]
+            sums[e][x % 2] = value if x < 2 else sums[e][x % 2] + value
     for e in range(n_energy):
         pair_ref[0, e] = depth_ref[e]
-        pair_ref[1, e] = sums[e]
+        pair_ref[1, e] = sums[e][0] + sums[e][1]
 
 
 def merge_body(distance, first_round, own_ref, other_ref, up_ref, further_ref, out_ref, up_out, further_out):
@@ -236,18 +226,24 @@
     return [(ref, i) for ref in refs for i in range(ref.shape[0])]
 
 
+def weigh(weights, lines, depth, n_energy, width):
+    height = weights.shape[0]
+    sums = [[None, None] for _ in range(n_energy)]
+    for r, (lines_ref, i) in enumerate(lines):
+        for z in range(depth):
+            place = r * depth + z
+            weight = jnp.broadcast_to(weights[:, place : place + 1], (height, width))
+            for e in range(n_energy):
+                value = weight * lines_ref[i, e, z : z + 1, :]
+                sums[e][z % 2] = value if place < 2 else sums[e][z % 2] + value
+    return [a + b for a, b in sums]
+
+
 def back_body(scale, cross_ref, index_ref, gram_ref, pull_ref, up_ref, further_ref, fluor_ref, *refs):
     lines, (near_ref, total_ref, gain_ref, shift_ref) = slices_of(refs[:-4]), refs[-4:]
     n_energy, rows, depth, width = fluor_ref.shape
     n_species = shift_ref.shape[0]
-    sums = [None] * n_energy
-    for r, (lines_ref, i) in enumerate(lines):
-        for z in range(depth):
-            place = r * depth + z
-            weight = jnp.broadcast_to(gram_ref[:, place : place + 1], (depth, width))
-            for e in range(n_energy):
-                value = weight * lines_ref[i, e, z : z + 1, :]
-                sums[e] = value if place == 0 else sums[e] + value
+    sums = weigh(gram_ref[...], lines, depth, n_energy, width)
     back = [sums[e] * scale - pull_ref[e] for e in range(n_energy)]
     gain = [back[e] * jnp.exp2(up_ref[e]) for e in range(n_energy)]
     sigma = selected(cross_ref, index_ref)
@@ -259,8 +255,8 @@
     table = lane_sums(width, False)
     lane = lax.broadcasted_iota(jnp.int32, (depth, LANES), 1)
     for part in range(rows // LANES):
-
-        def step(piece, total):
+        total = jnp.zeros((depth, LANES), F32)
+        for piece in range(LANES // CHUNK):
             first = part * LANES + piece * CHUNK
             heavy = [weighted(gain, [fluor_ref[e, first + q] for e in range(n_energy)]) for q in range(CHUNK)]
             found = jnp.dot(split(jnp.concatenate(heavy, axis=0)), table, preferred_element_type=F32)
@@ -268,73 +264,65 @@
                 here = found[q * depth : (q + 1) * depth]
                 near_ref[first + q] = here[:, :width]
                 total = jnp.where(lane == piece * CHUNK + q, here[:, width : width + LANES], total)
-            return total
-
-        total_ref[:, part * LANES : (part + 1) * LANES] = lax.fori_loop(
-            0, LANES // CHUNK, step, jnp.zeros((depth, LANES), F32)
-        )
-
-
-def grad_body(
-    scale, count, cross_ref, index_ref, line_ref, nearer_ref, gain_ref, shift_ref, near_ref, rest_ref,
-    out_hbm, out_ref, sems,
-):
+        total_ref[:, part * LANES : (part + 1) * LANES] = total
+
+
+def mix_body(scale, cross_ref, index_ref, line_ref, gain_ref, shift_ref, near_ref, rest_ref, out_ref):
     n_energy, rows, depth, width = rest_ref.shape
     n_species = out_ref.shape[0]
     sigma = selected(cross_ref, index_ref)
-    mixed = [[sigma[s][e] * gain_ref[e] for e in range(n_energy)] for s in range(n_species)]
-    shift = [shift_ref[s] for s in range(n_species)]
     line = [line_ref[s] * scale for s in range(n_species)]
+
+    def step(block, carry):
+        for s in range(n_species):
+            mixed = [sigma[s][e] * gain_ref[e] for e in range(n_energy)]
+            shift = shift_ref[s]
+            for q in range(STEP):
+                x = block * STEP + q
+                rest = weighted(mixed, [rest_ref[e, x] for e in range(n_energy)])
+                out_ref[s, x] = rest + (shift + line[s] * near_ref[x])
+        return carry
+
+    lax.fori_loop(0, rows // STEP, step, 0)
+
+
+def finish_body(
+    scale, scale_line, count, line_ref, nearer_ref, mix_ref, fan_ref, measured_ref, *refs
+):
+    lines, (grad_hbm, residual_hbm, grad_ref, residual_ref, sems, residual_sem) = slices_of(refs[:-6]), refs[-6:]
+    n_species, rows, depth, width = mix_ref.shape
+    n_energy, share, _ = residual_ref.shape
+    line = [line_ref[s] * scale_line for s in range(n_species)]
     keep = jnp.where(reached("det", count, True), 1.0, 0.0)
 
     def copies(chunk):
         span = pl.ds(chunk * CHUNK, CHUNK)
         return [
-            pltpu.make_async_copy(out_ref.at[:, span, z, :], out_hbm.at[:, z, span, :], sems.at[chunk])
+            pltpu.make_async_copy(grad_ref.at[:, span, z, :], grad_hbm.at[:, z, span, :], sems.at[chunk])
             for z in range(depth)
         ]
 
-    for part in range(rows // LANES):
-
-        def step(piece, held):
-            chunk = part * (LANES // CHUNK) + piece
-            for q in range(CHUNK):
-                x = chunk * CHUNK + q
-                column = jnp.broadcast_to(held[:, q : q + 1], (depth, width))
-                before = near_ref[x] + column
-                rest = [rest_ref[e, x] for e in range(n_energy)]
-                for s in range(n_species):
-                    out_ref[s, x] = weighted(mixed[s], rest) + shift[s] + line[s] * before
-            for copy in copies(chunk):
+    for x, column in columns(nearer_ref, lambda v: v * keep, width):
+        for s in range(n_species):
+            grad_ref[s, x] = mix_ref[s, x] + line[s] * column
+        if x % CHUNK == CHUNK - 1:
+            for copy in copies(x // CHUNK):
                 copy.start()
-            return pltpu.roll(held, LANES - CHUNK, 1)
-
-        lax.fori_loop(0, LANES // CHUNK, step, nearer_ref[:, part * LANES : (part + 1) * LANES] * keep)
+
+    start = pl.multiple_of(lax.axis_index(("beam", "slab")) * share, share)
+    sums = weigh(fan_ref[pl.ds(start, share), :], lines, depth, n_energy, width)
+    for e in range(n_energy):
+        residual_ref[e] = sums[e] * scale - measured_ref[e, pl.ds(start, share), :]
+    copy = pltpu.make_async_copy(residual_ref, residual_hbm, residual_sem)
+    copy.start()
 
     def finish(chunk, carry):
-        for copy in copies(chunk):
-            copy.wait()
+        for done in copies(chunk):
+            done.wait()
         return carry
 
     lax.fori_loop(0, rows // CHUNK, finish, 0)
-
-
-def signal_body(scale, fan_ref, measured_ref, *refs):
-    lines, out_ref = slices_of(refs[:-1]), refs[-1]
-    n_energy, share, width = out_ref.shape
-    depth = fan_ref.shape[1] // len(lines)
-    start = pl.multiple_of(lax.axis_index(("beam", "slab")) * share, share)
-    fan = fan_ref[pl.ds(start, share), :]
-    sums = [None] * n_energy
-    for r, (lines_ref, i) in enumerate(lines):
-        for z in range(depth):
-            place = r * depth + z
-            weight = jnp.broadcast_to(fan[:, place : place + 1], (share, width))
-            for e in range(n_energy):
-                value = weight * lines_ref[i, e, z : z + 1, :]
-                sums[e] = value if place == 0 else sums[e] + value
-    for e in range(n_energy):
-        out_ref[e] = sums[e] * scale - measured_ref[e, pl.ds(start, share), :]
+    copy.wait()
 
 
 def swap(value, axis, distance):
@@ -392,22 +380,24 @@
         cost=(8 * voxels, 0, 1024),
     )(far, emit, own_depth)
 
+    fluor, rest = call(
+        ahead_body, "ahead", (cube, cube), (VMEM, VMEM), (VMEM, VMEM, VMEM),
+        cost=(20 * voxels, 0, 1024),
+    )(far_wide, trans, emit)
+
     up = further = own_depth
     distance = 1
     while distance < n_beam:
         other = swap(pair, "beam", distance)
         kept = 1 if 2 * distance == n_beam else 2
+        if kept == 1:
+            other, fluor, rest = lax.optimization_barrier((other, fluor, rest))
         pair, up, further = call(
             functools.partial(merge_body, distance, distance == 1),
             "merge", (plain(kept, *wide), plain(*wide), plain(*wide)), (VMEM,) * 3, (VMEM,) * 4,
             cost=(1 << 14, 1 << 12, 1024),
         )(pair, other, up, further)
         distance *= 2
-
-    fluor, rest = call(
-        ahead_body, "ahead", (cube, cube), (VMEM, VMEM), (VMEM, VMEM, VMEM),
-        cost=(20 * voxels, 0, 1024),
-    )(far_wide, trans, emit)
 
     lines = [pair]
     distance = 1
@@ -433,23 +423,30 @@
 
     nearer = beyond(column_total, "det", True)
 
-    residual = call(
-        functools.partial(signal_body, 1.0 / (scale_x * full_x)),
-        "signal", (plain(n_energy, pixels // (n_beam * n_slab), width),), (VMEM,), (VMEM,) * (2 + len(lines)),
-        cost=(1 << 16, 0, 1024),
-    )(fan_turned, measured, *lines)[0]
-
-    grad = call(
-        functools.partial(grad_body, scale_y * LN2 / scale_x, n_det),
-        "grad",
-        (plain(n_species, depth, rows, width),),
-        (HBM,),
-        (SMEM, SMEM, SMEM) + (VMEM,) * 5,
-        [VMEM((n_species, rows, depth, width), F32), pltpu.SemaphoreType.DMA((rows // CHUNK,))],
-        limit=16,
-        cost=(40 * voxels, 0, 16 * voxels),
-    )(cross, index, line, nearer, gain, shift, near, rest)[0]
-    return grad, residual
+    scale_line = scale_y * LN2 / scale_x
+    mixed = call(
+        functools.partial(mix_body, scale_line), "mix", (VMEM(conc_x.shape, F32),), (VMEM,), (SMEM,) * 3 + (VMEM,) * 4,
+        cost=(40 * voxels, 0, 1024),
+    )(cross, index, line, gain, shift, near, rest)[0]
+
+    share = pixels // (n_beam * n_slab)
+    return tuple(
+        call(
+            functools.partial(finish_body, 1.0 / (scale_x * full_x), scale_line, n_det),
+            "finish",
+            (plain(*conc.shape), plain(n_energy, share, width)),
+            (HBM, HBM),
+            (SMEM,) + (VMEM,) * (4 + len(lines)),
+            [
+                VMEM(conc_x.shape, F32),
+                VMEM((n_energy, share, width), F32),
+                pltpu.SemaphoreType.DMA((rows // CHUNK,)),
+                pltpu.SemaphoreType.DMA,
+            ],
+            limit=16,
+            cost=(10 * voxels, 0, 16 * voxels),
+        )(line, nearer, mixed, fan_turned, measured, *lines)
+    )
 
 
 def solution(mesh):

time: 33.6 us -> 31.3 us (0.932)
  waiting for transfers between devices: 7.63 us -> 6.13 us
  Pallas kernels: 14.7 us -> 13.9 us
    ppermute x6, waiting for transfers between devices: 7.63 us -> 6.13 us  [swap(): lax.ppermute(value, axis, [(i, i ^ distance) for i in range(lax.axis_size...]
    pallas_call x2, Pallas kernels: 3.96 us -> 5.21 us  [the longest x1 2.78 us: shards(): call(functools.partial(finish_body, 1.0 / (scale_x * full_x), scale_line,...]
    pallas_call x1, Pallas kernels: 2.3 us -> 1.23 us  [shards(): call(functools.partial(back_body, 1.0 / (scale_x * full_x)), 'back', (pla...]
    pallas_call x1, Pallas kernels: 1.53 us -> 0.56 us  [shards(): call(functools.partial(line_body, n_det), 'line', (plane, plain(2, *wide)...]
  transfers between devices with their start and end apart: 6 -> 6, of which waited for: 5 -> 4; matrix products, arithmetic and copies ran while one was open for 0% -> 0% of each run, Pallas kernels for 15% -> 21%
where the time goes in v3:
time: 31.3 us; the launch traced here: 31.1 us
  Pallas kernels  13.9 us (44%)
  starting transfers between devices  10.4 us (33%)
  waiting for transfers between devices  6.13 us (20%)
  between operations  0.73 us (2%)
    ppermute x6, starting transfers between devices, swap(): lax.ppermute(value, axis, [(i, i ^ distance) for i in range(lax.axis_size...  10.4 us
    ppermute x6, waiting for transfers between devices, swap(): lax.ppermute(value, axis, [(i, i ^ distance) for i in range(lax.axis_size...  6.13 us
    pallas_call x1, Pallas kernels, shards(): call(functools.partial(finish_body, 1.0 / (scale_x * full_x), scale_line,...  2.78 us
    pallas_call x1, Pallas kernels, shards(): call(functools.partial(load_body, scale_y), 'load', (VMEM((n_species, row...  2.76 us
    pallas_call x1, Pallas kernels, shards(): call(functools.partial(mix_body, scale_line), 'mix', (VMEM(conc_x.shape,...  2.43 us
    pallas_call x1, Pallas kernels, shards(): call(functools.partial(local_body, scale_x), 'local', (cube, cube, plain(...  2.25 us
    pallas_call x1, Pallas kernels, shards(): call(ahead_body, 'ahead', (cube, cube), (VMEM, VMEM), (VMEM, VMEM, VMEM),...  1.51 us
    pallas_call x1, Pallas kernels, shards(): call(functools.partial(back_body, 1.0 / (scale_x * full_x)), 'back', (pla...  1.23 us
  transfers between devices with their start and end apart: 6, of which 4 were waited for; matrix products, arithmetic and copies ran while one was open for 0% of the time, Pallas kernels for 21%

profile of v3, /device:TPU:0, one launch (start us, length us, event | category | flops | bytes accessed | tf_op | source)
XLA Modules:
  0.0 31.1 jit_solution(5010961939645815598)
XLA Ops:
  0.6 0.0 copy-start.2
  0.6 0.0 copy-start.1
  0.6 2.8 %load.1 = (f32[4,256,8,128]{3,2,1,0:T(8,128)S(1)}, f32[256,8,128]{2,1,0:T(8,128)S(1)}, f32[8,256]{1,0:T(8,128)S(1)}) custom-call(f32[4]{0:T(128)} %line_ref.3, f32[4,8,256,128]{3,2,1,0:T(8,128)} %conc_hbm.1), custom_call_target="tpu_custom_call" | custom-call | flops 2097152 | bytes 4194304 | tf_op jit(solution)/shard_map/load/pallas_call | solution.py:356
  3.4 3.1 %collective-permute-start = (f32[8,256]{1,0:T(8,128)S(1)}, f32[8,256]{1,0:T(8,128)S(1)}, u32[]{:S(2)}, u32[]{:S(2)}) collective-permute-start(f32[8,256]{1,0:T(8,128)S(1)} %get-tuple-element.30), channel_id=1, source_target_pairs={{0,4},{4,0},{1,5},{5,1},{2,6},{6,2},{3,7},{7,3},{8,12},{12,8},{9,1... | collective-permute-start | bytes 24584 | tf_op jit(solution)/shard_map/ppermute | solution.py:329
  6.5 0.0 copy-done.2
  6.5 0.0 copy-done.1
  6.5 2.2 %local.1 = (f32[4,256,8,128]{3,2,1,0:T(8,128)S(1)}, f32[4,256,8,128]{3,2,1,0:T(8,128)S(1)}, f32[4,8,128]{2,1,0:T(8,128)S(1)}) custom-call(f32[4,16]{1,0:T(4,128)S(1)} %copy-done.1, s32[4]{0:T(128)S(1)} %copy-done.2, f32[4,256,8,128]{3,2,1,0:T(8,128)S(1)} %get-tuple-element.31.conc_ref, f32[256,8,128]{2,1,0:T(8,128)S(1)} %get-tuple-element.32.beyond_ref), custom_call_target="tpu_custom_call" | custom-call | flops 10485760 | bytes 1024 | tf_op jit(solution)/shard_map/local/pallas_call | solution.py:368
  8.7 0.0 collective-permute-done.far_ref
  8.8 0.6 %line.1 = (f32[256,8,128]{2,1,0:T(8,128)S(1)}, f32[2,4,8,128]{3,2,1,0:T(8,128)S(1)}) custom-call(f32[8,256]{1,0:T(8,128)S(1)} %collective-permute-done.far_ref, f32[4,256,8,128]{3,2,1,0:T(8,128)S(1)} %get-tuple-element.33.emit_ref, f32[4,8,128]{2,1,0:T(8,128)S(1)} %get-tuple-element.34.depth_ref.up_ref.further_ref), custom_call_target="tpu_custom_call" | custom-call | flops 2097152 | bytes 1024 | tf_op jit(solution)/shard_map/line/pallas_call | solution.py:378
  9.3 0.1 collective-permute-start.1
  9.4 1.2 %collective-permute-done.1.other_ref = f32[2,4,8,128]{3,2,1,0:T(8,128)S(1)} collective-permute-done((f32[2,4,8,128]{3,2,1,0:T(8,128)S(1)}, f32[2,4,8,128]{3,2,1,0:T(8,128)S(1)}, u32[]{:S(2)}, u32[]{:S(2)}) %collective-permute-start.1) | collective-permute-done | bytes 32800 | tf_op jit(solution)/shard_map/ppermute | solution.py:329
  10.6 1.6 %collective-permute-start.2 = (f32[2,4,8,128]{3,2,1,0:T(8,128)S(1)}, f32[2,4,8,128]{3,2,1,0:T(8,128)S(1)}, u32[]{:S(2)}, u32[]{:S(2)}) collective-permute-start(f32[2,4,8,128]{3,2,1,0:T(8,128)S(1)} %get-tuple-element.36.own_ref), channel_id=1, source_target_pairs={{0,16},{8,24},{16,0},{24,8},{1,17},{9,25},{17,1},{25,9},{2,18},{10... | collective-permute-start | bytes 98312 | tf_op jit(solution)/shard_map/ppermute | solution.py:329
  12.2 0.0 copy-start
  12.2 0.0 copy-start.4
  12.2 0.0 copy-start.5
  12.2 1.5 %ahead.1 = (f32[4,256,8,128]{3,2,1,0:T(8,128)S(1)}, f32[4,256,8,128]{3,2,1,0:T(8,128)S(1)}) custom-call(f32[256,8,128]{2,1,0:T(8,128)S(1)} %get-tuple-element.37.far_ref, f32[4,256,8,128]{3,2,1,0:T(8,128)S(1)} %get-tuple-element.38.trans_ref, f32[4,256,8,128]{3,2,1,0:T(8,128)S(1)} %get-tuple-element.33.emit_ref), custom_call_target="tpu_custom_call" | custom-call | flops 5242880 | bytes 1024 | tf_op jit(solution)/shard_map/ahead/pallas_call | solution.py:383
  13.7 0.0 copy-start.3
  13.7 0.9 %collective-permute-done.2.other_ref = f32[2,4,8,128]{3,2,1,0:T(8,128)S(1)} collective-permute-done((f32[2,4,8,128]{3,2,1,0:T(8,128)S(1)}, f32[2,4,8,128]{3,2,1,0:T(8,128)S(1)}, u32[]{:S(2)}, u32[]{:S(2)}) %collective-permute-start.2) | collective-permute-done | bytes 32800 | tf_op jit(solution)/shard_map/ppermute | solution.py:329
  14.6 1.6 %collective-permute-start.3 = (f32[1,4,8,128]{3,2,1,0:T(8,128)S(1)}, f32[1,4,8,128]{3,2,1,0:T(8,128)S(1)}, u32[]{:S(2)}, u32[]{:S(2)}) collective-permute-start(f32[1,4,8,128]{3,2,1,0:T(8,128)S(1)} %get-tuple-element.47.refs_0_), channel_id=1, source_target_pairs={{0,1},{1,0},{2,3},{3,2},{4,5},{5,4},{6,7},{7,6},{8,9},{9,8},{10,11... | collective-permute-start | bytes 49160 | tf_op jit(solution)/shard_map/ppermute | solution.py:329
  16.3 2.2 %collective-permute-done.3.refs_1_ = f32[1,4,8,128]{3,2,1,0:T(8,128)S(1)} collective-permute-done((f32[1,4,8,128]{3,2,1,0:T(8,128)S(1)}, f32[1,4,8,128]{3,2,1,0:T(8,128)S(1)}, u32[]{:S(2)}, u32[]{:S(2)}) %collective-permute-start.3) | collective-permute-done | bytes 16416 | tf_op jit(solution)/shard_map/ppermute | solution.py:329
  18.4 2.6 %collective-permute-start.4 = (f32[2,4,8,128]{3,2,1,0:T(8,128)S(1)}, f32[2,4,8,128]{3,2,1,0:T(8,128)S(1)}, u32[]{:S(2)}, u32[]{:S(2)}) collective-permute-start(f32[2,4,8,128]{3,2,1,0:T(8,128)S(1)} %pad_maximum_fusion), channel_id=1, source_target_pairs={{0,2},{1,3},{2,0},{3,1},{4,6},{5,7},{6,4},{7,5},{8,10},{9,11},{10,... | collective-permute-start | bytes 98312 | tf_op jit(solution)/shard_map/ppermute | solution.py:329
  21.0 0.0 copy-done
  21.0 0.0 copy-done.4
  21.0 0.0 copy-done.5
  21.0 0.3 %fan.1 = (f32[8,32]{1,0:T(8,128)S(1)}, f32[4,8,128]{2,1,0:T(8,128)S(1)}, f32[256,32]{1,0:T(8,128)S(1)}) custom-call(s32[1,256]{1,0:T(1,128)S(1)} %bitcast.3, s32[4,256]{1,0:T(4,128)S(1)} %bitcast.2, f32[4,256,128]{2,1,0:T(8,128)S(1)} %copy-done), custom_call_target="tpu_custom_call" | custom-call | flops 8388608 | bytes 524288 | tf_op jit(solution)/shard_map/fan/pallas_call | solution.py:410
  21.4 1.9 %collective-permute-done.4.refs_2_ = f32[2,4,8,128]{3,2,1,0:T(8,128)S(1)} collective-permute-done((f32[2,4,8,128]{3,2,1,0:T(8,128)S(1)}, f32[2,4,8,128]{3,2,1,0:T(8,128)S(1)}, u32[]{:S(2)}, u32[]{:S(2)}) %collective-permute-start.4) | collective-permute-done | bytes 32800 | tf_op jit(solution)/shard_map/ppermute | solution.py:329
  23.2 1.2 %back.1 = (f32[256,8,128]{2,1,0:T(8,128)S(1)}, f32[8,256]{1,0:T(8,128)S(1)}, f32[4,8,128]{2,1,0:T(8,128)S(1)}, f32[4,8,128]{2,1,0:T(8,128)S(1)}) custom-call(f32[4,16]{1,0:T(4,128)S(1)} %copy-done.1, s32[4]{0:T(128)S(1)} %copy-done.2, f32[8,32]{1,0:T(8,128)S(1)} %get-tuple-element.28.gram_ref, f32[4,8,128]{2,1,0:T(8,128)S(1)} %get-tuple-element.29.pull_ref, ...), custom_call_target="tpu_custom_call" | custom-call | flops 2621440 | bytes 1024 | tf_op jit(solution)/shard_map/back/pallas_call | solution.py:415
  24.5 1.4 %collective-permute-start.5 = (f32[8,256]{1,0:T(8,128)S(1)}, f32[8,256]{1,0:T(8,128)S(1)}, u32[]{:S(2)}, u32[]{:S(2)}) collective-permute-start(f32[8,256]{1,0:T(8,128)S(1)} %get-tuple-element.48), channel_id=1, source_target_pairs={{0,4},{4,0},{1,5},{5,1},{2,6},{6,2},{3,7},{7,3},{8,12},{12,8},{9,1... | collective-permute-start | bytes 24584 | tf_op jit(solution)/shard_map/ppermute | solution.py:329
  25.9 0.0 copy-done.3
  25.9 2.4 %mix.1.mix_ref = f32[4,256,8,128]{3,2,1,0:T(8,128)S(1)} custom-call(f32[4,16]{1,0:T(4,128)S(1)} %copy-done.1, s32[4]{0:T(128)S(1)} %copy-done.2, f32[4]{0:T(128)S(1)} %copy-done.3, f32[4,8,128]{2,1,0:T(8,128)S(1)} %get-tuple-element.49.gain_ref, f32[4,8,128]{2,1,0:T(8,128)S(1)} %get-tuple-element.50.shift_ref, ...), custom_call_target="tpu_custom_call" | custom-call | flops 10485760 | bytes 1024 | tf_op jit(solution)/shard_map/mix/pallas_call | solution.py:427
  28.3 0.0 collective-permute-done.5.nearer_ref
  28.4 2.8 %finish.1 = (f32[4,8,256,128]{3,2,1,0:T(8,128)}, f32[4,16,128]{2,1,0:T(8,128)}) custom-call(f32[4]{0:T(128)S(1)} %copy-done.3, f32[8,256]{1,0:T(8,128)S(1)} %collective-permute-done.5.nearer_ref, f32[4,256,8,128]{3,2,1,0:T(8,128)S(1)} %mix.1.mix_ref, f32[256,32]{1,0:T(8,128)S(1)} %get-tuple-element.53.fan_ref, f32[4,256,128]{2,1,0:T(8,128)S(1)} %copy-done, ...), custom_call_target="tpu_custom_call" | custom-call | flops 2621440 | bytes 4194304 | tf_op jit(solution)/shard_map/finish/pallas_call | solution.py:434
  (3 shorter events, 0.0 us)
Async XLA Ops:
  0.6 5.9 %copy-start.2 = (s32[4]{0:T(128)S(1)}, s32[4]{0:T(128)}, u32[]{:S(2)}) copy-start(s32[4]{0:T(128)} %index_ref.5) | copy-start | bytes 52
  0.6 5.8 %copy-start.1 = (f32[4,16]{1,0:T(4,128)S(1)}, f32[4,16]{1,0:T(4,128)}, u32[]{:S(2)}) copy-start(f32[4,16]{1,0:T(4,128)} %cross_ref.5) | copy-start | bytes 772
  3.4 5.3 %collective-permute-start = (f32[8,256]{1,0:T(8,128)S(1)}, f32[8,256]{1,0:T(8,128)S(1)}, u32[]{:S(2)}, u32[]{:S(2)}) collective-permute-start(f32[8,256]{1,0:T(8,128)S(1)} %get-tuple-element.30), channel_id=1, source_target_pairs={{0,4},{4,0},{1,5},{5,1},{2,6},{6,2},{3,7},{7,3},{8,12},{12,8},{9,1... | collective-permute-start | bytes 24584 | tf_op jit(solution)/shard_map/ppermute | solution.py:329
  9.3 1.3 %collective-permute-start.1 = (f32[2,4,8,128]{3,2,1,0:T(8,128)S(1)}, f32[2,4,8,128]{3,2,1,0:T(8,128)S(1)}, u32[]{:S(2)}, u32[]{:S(2)}) collective-permute-start(f32[2,4,8,128]{3,2,1,0:T(8,128)S(1)} %get-tuple-element.35.own_ref), channel_id=1, source_target_pairs={{0,8},{8,0},{16,24},{24,16},{1,9},{9,1},{17,25},{25,17},{2,10},{10... | collective-permute-start | bytes 98312 | tf_op jit(solution)/shard_map/ppermute | solution.py:329
  10.6 4.0 %collective-permute-start.2 = (f32[2,4,8,128]{3,2,1,0:T(8,128)S(1)}, f32[2,4,8,128]{3,2,1,0:T(8,128)S(1)}, u32[]{:S(2)}, u32[]{:S(2)}) collective-permute-start(f32[2,4,8,128]{3,2,1,0:T(8,128)S(1)} %get-tuple-element.36.own_ref), channel_id=1, source_target_pairs={{0,16},{8,24},{16,0},{24,8},{1,17},{9,25},{17,1},{25,9},{2,18},{10... | collective-permute-start | bytes 98312 | tf_op jit(solution)/shard_map/ppermute | solution.py:329
  12.2 8.8 %copy-start = (f32[4,256,128]{2,1,0:T(8,128)S(1)}, f32[4,256,128]{2,1,0:T(8,128)}, u32[]{:S(2)}) copy-start(f32[4,256,128]{2,1,0:T(8,128)} %measured_ref.3) | copy-start | bytes 1572868
  12.2 8.8 %copy-start.4 = (s32[256,4]{0,1:T(4,128)S(1)}, s32[256,4]{0,1:T(4,128)}, u32[]{:S(2)}) copy-start(s32[256,4]{0,1:T(4,128)} %param.12) | copy-start | bytes 12292
  12.2 8.8 %copy-start.5 = (s32[256]{0:T(256)S(1)}, s32[256]{0:T(256)}, u32[]{:S(2)}) copy-start(s32[256]{0:T(256)} %param.11) | copy-start | bytes 3076
  13.7 12.2 %copy-start.3 = (f32[4]{0:T(128)S(1)}, f32[4]{0:T(128)}, u32[]{:S(2)}) copy-start(f32[4]{0:T(128)} %line_ref.3) | copy-start | bytes 52
  14.6 3.8 %collective-permute-start.3 = (f32[1,4,8,128]{3,2,1,0:T(8,128)S(1)}, f32[1,4,8,128]{3,2,1,0:T(8,128)S(1)}, u32[]{:S(2)}, u32[]{:S(2)}) collective-permute-start(f32[1,4,8,128]{3,2,1,0:T(8,128)S(1)} %get-tuple-element.47.refs_0_), channel_id=1, source_target_pairs={{0,1},{1,0},{2,3},{3,2},{4,5},{5,4},{6,7},{7,6},{8,9},{9,8},{10,11... | collective-permute-start | bytes 49160 | tf_op jit(solution)/shard_map/ppermute | solution.py:329
  18.4 4.8 %collective-permute-start.4 = (f32[2,4,8,128]{3,2,1,0:T(8,128)S(1)}, f32[2,4,8,128]{3,2,1,0:T(8,128)S(1)}, u32[]{:S(2)}, u32[]{:S(2)}) collective-permute-start(f32[2,4,8,128]{3,2,1,0:T(8,128)S(1)} %pad_maximum_fusion), channel_id=1, source_target_pairs={{0,2},{1,3},{2,0},{3,1},{4,6},{5,7},{6,4},{7,5},{8,10},{9,11},{10,... | collective-permute-start | bytes 98312 | tf_op jit(solution)/shard_map/ppermute | solution.py:329
  24.5 3.9 %collective-permute-start.5 = (f32[8,256]{1,0:T(8,128)S(1)}, f32[8,256]{1,0:T(8,128)S(1)}, u32[]{:S(2)}, u32[]{:S(2)}) collective-permute-start(f32[8,256]{1,0:T(8,128)S(1)} %get-tuple-element.48), channel_id=1, source_target_pairs={{0,4},{4,0},{1,5},{5,1},{2,6},{6,2},{3,7},{7,3},{8,12},{12,8},{9,1... | collective-permute-start | bytes 24584 | tf_op jit(solution)/shard_map/ppermute | solution.py:329

commit v4 on v3

--- a/solution.py
+++ b/solution.py
@@ -62,8 +62,12 @@
     return total
 
 
-def load_body(scale, line_hbm, conc_hbm, conc_ref, beyond_ref, total_ref, line_ref, line_sem, sems):
+def load_body(
+    scale, scale_x, line_hbm, cross_hbm, index_hbm, conc_hbm, emit_ref, beyond_ref, total_ref,
+    conc_ref, line_ref, cross_ref, index_ref, small_sems, sems,
+):
     n_species, depth, rows, width = conc_hbm.shape
+    n_energy = emit_ref.shape[0]
 
     def copies(chunk):
         span = pl.ds(chunk * CHUNK, CHUNK)
@@ -72,51 +76,54 @@
             for z in range(depth)
         ]
 
-    line_copy = pltpu.make_async_copy(line_hbm, line_ref, line_sem)
-    line_copy.start()
-
+    small = [
+        pltpu.make_async_copy(source, target, small_sems.at[i])
+        for i, (source, target) in enumerate(
+            [(line_hbm, line_ref), (cross_hbm, cross_ref), (index_hbm, index_ref)]
+        )
+    ]
+    for copy in small:
+        copy.start()
     for chunk in range(rows // CHUNK):
         for copy in copies(chunk):
             copy.start()
     table = lane_sums(width, True)
     lane = lax.broadcasted_iota(jnp.int32, (depth, LANES), 1)
-    line_copy.wait()
+    for copy in small:
+        copy.wait()
     line = [line_ref[s] * scale for s in range(n_species)]
+    sigma = [[v * scale_x for v in row] for row in selected(cross_ref, index_ref)]
     for part in range(rows // LANES):
-
-        def step(piece, total):
+        total = jnp.zeros((depth, LANES), F32)
+        for piece in range(LANES // CHUNK):
             chunk = part * (LANES // CHUNK) + piece
             for copy in copies(chunk):
                 copy.wait()
             absorber = []
             for q in range(CHUNK):
                 x = chunk * CHUNK + q
-                absorber.append(weighted(line, [conc_ref[s, x] for s in range(n_species)]))
+                conc = [conc_ref[s, x] for s in range(n_species)]
+                absorber.append(weighted(line, conc))
+                for e in range(n_energy):
+                    emit_ref[e, x] = weighted([sigma[s][e] for s in range(n_species)], conc)
             sums = jnp.dot(split(jnp.concatenate(absorber, axis=0)), table, preferred_element_type=F32)
             for q in range(CHUNK):
                 here = sums[q * depth : (q + 1) * depth]
                 beyond_ref[chunk * CHUNK + q] = here[:, :width]
                 total = jnp.where(lane == piece * CHUNK + q, here[:, width : width + LANES], total)
-            return total
-
-        total_ref[:, part * LANES : (part + 1) * LANES] = lax.fori_loop(
-            0, LANES // CHUNK, step, jnp.zeros((depth, LANES), F32)
-        )
-
-
-def local_body(scale, cross_ref, index_ref, conc_ref, beyond_ref, trans_ref, emit_ref, depth_ref):
-    n_species, rows, depth, width = conc_ref.shape
-    n_energy = trans_ref.shape[0]
-    sigma = [[v * scale for v in row] for row in selected(cross_ref, index_ref)]
+        total_ref[:, part * LANES : (part + 1) * LANES] = total
+
+
+def local_body(source_ref, beyond_ref, trans_ref, emit_ref, depth_ref):
+    n_energy, rows, depth, width = trans_ref.shape
 
     def step(block, path):
         path = list(path)
         for q in range(STEP):
             x = block * STEP + q
-            conc = [conc_ref[s, x] for s in range(n_species)]
             beyond = beyond_ref[x]
             for e in range(n_energy):
-                emission = weighted([sigma[s][e] for s in range(n_species)], conc)
+                emission = source_ref[e, x]
                 trans = jnp.exp2(path[e] + beyond)
                 trans_ref[e, x] = trans
                 emit_ref[e, x] = emission * trans
@@ -222,28 +229,24 @@
         )
 
 
-def slices_of(refs):
-    return [(ref, i) for ref in refs for i in range(ref.shape[0])]
-
-
 def weigh(weights, lines, depth, n_energy, width):
     height = weights.shape[0]
     sums = [[None, None] for _ in range(n_energy)]
-    for r, (lines_ref, i) in enumerate(lines):
+    for order, (r, lines_ref) in enumerate(lines):
         for z in range(depth):
             place = r * depth + z
             weight = jnp.broadcast_to(weights[:, place : place + 1], (height, width))
             for e in range(n_energy):
-                value = weight * lines_ref[i, e, z : z + 1, :]
-                sums[e][z % 2] = value if place < 2 else sums[e][z % 2] + value
+                value = weight * lines_ref[0, e, z : z + 1, :]
+                sums[e][z % 2] = value if order == 0 and z < 2 else sums[e][z % 2] + value
     return [a + b for a, b in sums]
 
 
-def back_body(scale, cross_ref, index_ref, gram_ref, pull_ref, up_ref, further_ref, fluor_ref, *refs):
-    lines, (near_ref, total_ref, gain_ref, shift_ref) = slices_of(refs[:-4]), refs[-4:]
+def back_body(scale, close, cross_ref, index_ref, gram_ref, pull_ref, up_ref, further_ref, fluor_ref, *refs):
+    lines, (near_ref, total_ref, gain_ref, shift_ref) = refs[:-4], refs[-4:]
     n_energy, rows, depth, width = fluor_ref.shape
     n_species = shift_ref.shape[0]
-    sums = weigh(gram_ref[...], lines, depth, n_energy, width)
+    sums = weigh(gram_ref[...], list(zip(close, lines)), depth, n_energy, width)
     back = [sums[e] * scale - pull_ref[e] for e in range(n_energy)]
     gain = [back[e] * jnp.exp2(up_ref[e]) for e in range(n_energy)]
     sigma = selected(cross_ref, index_ref)
@@ -267,29 +270,28 @@
         total_ref[:, part * LANES : (part + 1) * LANES] = total
 
 
-def mix_body(scale, cross_ref, index_ref, line_ref, gain_ref, shift_ref, near_ref, rest_ref, out_ref):
+def mix_body(cross_ref, index_ref, gain_ref, shift_ref, rest_ref, out_ref):
     n_energy, rows, depth, width = rest_ref.shape
     n_species = out_ref.shape[0]
     sigma = selected(cross_ref, index_ref)
-    line = [line_ref[s] * scale for s in range(n_species)]
+    mixed = [[sigma[s][e] * gain_ref[e] for e in range(n_energy)] for s in range(n_species)]
+    shift = [shift_ref[s] for s in range(n_species)]
 
     def step(block, carry):
-        for s in range(n_species):
-            mixed = [sigma[s][e] * gain_ref[e] for e in range(n_energy)]
-            shift = shift_ref[s]
-            for q in range(STEP):
-                x = block * STEP + q
-                rest = weighted(mixed, [rest_ref[e, x] for e in range(n_energy)])
-                out_ref[s, x] = rest + (shift + line[s] * near_ref[x])
+        for q in range(STEP):
+            x = block * STEP + q
+            rest = [rest_ref[e, x] for e in range(n_energy)]
+            for s in range(n_species):
+                out_ref[s, x] = weighted(mixed[s], rest) + shift[s]
         return carry
 
     lax.fori_loop(0, rows // STEP, step, 0)
 
 
 def finish_body(
-    scale, scale_line, count, line_ref, nearer_ref, mix_ref, fan_ref, measured_ref, *refs
+    scale, scale_line, count, line_ref, nearer_ref, near_ref, mix_ref, fan_ref, measured_ref, *refs
 ):
-    lines, (grad_hbm, residual_hbm, grad_ref, residual_ref, sems, residual_sem) = slices_of(refs[:-6]), refs[-6:]
+    lines, (grad_hbm, residual_hbm, grad_ref, residual_ref, sems, residual_sem) = refs[:-6], refs[-6:]
     n_species, rows, depth, width = mix_ref.shape
     n_energy, share, _ = residual_ref.shape
     line = [line_ref[s] * scale_line for s in range(n_species)]
@@ -303,14 +305,15 @@
         ]
 
     for x, column in columns(nearer_ref, lambda v: v * keep, width):
+        before = near_ref[x] + column
         for s in range(n_species):
-            grad_ref[s, x] = mix_ref[s, x] + line[s] * column
+            grad_ref[s, x] = mix_ref[s, x] + line[s] * before
         if x % CHUNK == CHUNK - 1:
             for copy in copies(x // CHUNK):
                 copy.start()
 
     start = pl.multiple_of(lax.axis_index(("beam", "slab")) * share, share)
-    sums = weigh(fan_ref[pl.ds(start, share), :], lines, depth, n_energy, width)
+    sums = weigh(fan_ref[pl.ds(start, share), :], list(enumerate(lines)), depth, n_energy, width)
     for e in range(n_energy):
         residual_ref[e] = sums[e] * scale - measured_ref[e, pl.ds(start, share), :]
     copy = pltpu.make_async_copy(residual_ref, residual_hbm, residual_sem)
@@ -345,6 +348,7 @@
     n_energy = index.shape[0]
     n_beam, n_det, n_slab = (lax.axis_size(a) for a in ("beam", "det", "slab"))
     assert n_beam & (n_beam - 1) == 0 and n_slab & (n_slab - 1) == 0
+    assert fan_weight.shape[1] <= depth + 1
     assert rows % LANES == 0 and width % LANES == 0 and depth % 8 == 0
     full_x, full_y = rows * n_beam, width * n_det
     scale_x = -(1.5 / full_x) * LOG2E
@@ -353,26 +357,33 @@
     cube = VMEM((n_energy, rows, depth, width), F32)
     plane = VMEM((rows, depth, width), F32)
 
-    conc_x, far_local, row_total = call(
-        functools.partial(load_body, scale_y),
+    emission, far_local, row_total = call(
+        functools.partial(load_body, scale_y, scale_x),
         "load",
-        (VMEM((n_species, rows, depth, width), F32), plane, plain(depth, rows)),
+        (cube, plane, plain(depth, rows)),
         (VMEM, VMEM, VMEM),
-        (HBM, HBM),
-        [SMEM((n_species,), F32), pltpu.SemaphoreType.DMA, pltpu.SemaphoreType.DMA((rows // CHUNK,))],
-        cost=(8 * voxels, 0, 16 * voxels),
-    )(pltpu.with_memory_space_constraint(line, HBM), pltpu.with_memory_space_constraint(conc, HBM))
+        (HBM,) * 4,
+        [
+            VMEM((n_species, rows, depth, width), F32),
+            SMEM(line.shape, F32),
+            SMEM(cross.shape, F32),
+            SMEM(index.shape, index.dtype),
+            pltpu.SemaphoreType.DMA((3,)),
+            pltpu.SemaphoreType.DMA((rows // CHUNK,)),
+        ],
+        cost=(40 * voxels, 0, 16 * voxels),
+    )(*(pltpu.with_memory_space_constraint(v, HBM) for v in (line, cross, index, conc)))
 
     far = beyond(row_total, "det", False)
 
     trans, emit, own_depth = call(
-        functools.partial(local_body, scale_x),
+        local_body,
         "local",
         (cube, cube, plain(n_energy, depth, width)),
         (VMEM, VMEM, VMEM),
-        (SMEM, SMEM, VMEM, VMEM),
-        cost=(40 * voxels, 4 * voxels, 1024),
-    )(cross, index, conc_x, far_local)
+        (VMEM, VMEM),
+        cost=(20 * voxels, 4 * voxels, 1024),
+    )(emission, far_local)
 
     wide = (n_energy, depth, width)
     far_wide, pair = call(
@@ -399,12 +410,8 @@
         )(pair, other, up, further)
         distance *= 2
 
-    lines = [pair]
-    distance = 1
-    while distance < n_slab:
-        whole = lines[0] if distance == 1 else jnp.concatenate(lines, axis=0)
-        lines.append(swap(whole, "slab", distance))
-        distance *= 2
+    lines = [pair] + [swap(pair, "slab", r) for r in range(1, n_slab)]
+    close = [r for r in range(n_slab) if r & (r + 1) == 0]
 
     pixels = fan_offset.shape[0]
     gram, pull, fan_turned = call(
@@ -413,21 +420,22 @@
     )(fan_offset[None, :], fan_weight.T, measured)
 
     near, column_total, gain, shift = call(
-        functools.partial(back_body, 1.0 / (scale_x * full_x)),
+        functools.partial(back_body, 1.0 / (scale_x * full_x), close),
         "back",
         (plane, plain(depth, rows), plain(*wide), plain(n_species, depth, width)),
         (VMEM,) * 4,
-        (SMEM, SMEM) + (VMEM,) * (5 + len(lines)),
+        (SMEM, SMEM) + (VMEM,) * (5 + len(close)),
         cost=(10 * voxels, 0, 1024),
-    )(cross, index, gram, pull, up, further, fluor, *lines)
+    )(cross, index, gram, pull, up, further, fluor, *(lines[r] for r in close))
 
     nearer = beyond(column_total, "det", True)
 
     scale_line = scale_y * LN2 / scale_x
+    turned = (n_species, rows, depth, width)
     mixed = call(
-        functools.partial(mix_body, scale_line), "mix", (VMEM(conc_x.shape, F32),), (VMEM,), (SMEM,) * 3 + (VMEM,) * 4,
+        mix_body, "mix", (VMEM(turned, F32),), (VMEM,), (SMEM,) * 2 + (VMEM,) * 3,
         cost=(40 * voxels, 0, 1024),
-    )(cross, index, line, gain, shift, near, rest)[0]
+    )(cross, index, gain, shift, rest)[0]
 
     share = pixels // (n_beam * n_slab)
     return tuple(
@@ -436,16 +444,16 @@
             "finish",
             (plain(*conc.shape), plain(n_energy, share, width)),
             (HBM, HBM),
-            (SMEM,) + (VMEM,) * (4 + len(lines)),
+            (SMEM,) + (VMEM,) * (5 + len(lines)),
             [
-                VMEM(conc_x.shape, F32),
+                VMEM(turned, F32),
                 VMEM((n_energy, share, width), F32),
                 pltpu.SemaphoreType.DMA((rows // CHUNK,)),
                 pltpu.SemaphoreType.DMA,
             ],
             limit=16,
             cost=(10 * voxels, 0, 16 * voxels),
-        )(line, nearer, mixed, fan_turned, measured, *lines)
+        )(line, nearer, near, mixed, fan_turned, measured, *lines)
     )
 
 

time: 31.3 us -> 30.2 us (0.965)
  Pallas kernels: 13.9 us -> 12.4 us
  starting transfers between devices: 10.4 us -> 11.5 us
  waiting for transfers between devices: 6.13 us -> 5.46 us
    pallas_call x4, Pallas kernels: 8.66 us -> 7.12 us  [the longest x1 3.46 us: shards(): call(functools.partial(load_body, scale_y, scale_x), 'load', (cube, plane...]
    ppermute x6 -> x7, starting transfers between devices: 10.4 us -> 11.5 us  [swap(): lax.ppermute(value, axis, [(i, i ^ distance) for i in range(lax.axis_size...]
    ppermute x6 -> x7, waiting for transfers between devices: 6.13 us -> 5.46 us  [swap(): lax.ppermute(value, axis, [(i, i ^ distance) for i in range(lax.axis_size...]
  transfers between devices with their start and end apart: 6 -> 7, of which waited for: 4 -> 5; matrix products, arithmetic and copies ran while one was open for 0% -> 0% of each run, Pallas kernels for 21% -> 18%
where the time goes in v4:
time: 30.2 us; the launch traced here: 30.1 us
  Pallas kernels  12.4 us (41%)
  starting transfers between devices  11.5 us (38%)
  waiting for transfers between devices  5.46 us (18%)
  between operations  0.71 us (2%)
    ppermute x7, starting transfers between devices, swap(): lax.ppermute(value, axis, [(i, i ^ distance) for i in range(lax.axis_size...  11.5 us
    ppermute x7, waiting for transfers between devices, swap(): lax.ppermute(value, axis, [(i, i ^ distance) for i in range(lax.axis_size...  5.46 us
    pallas_call x1, Pallas kernels, shards(): call(functools.partial(load_body, scale_y, scale_x), 'load', (cube, plane...  3.46 us
    pallas_call x1, Pallas kernels, shards(): call(functools.partial(finish_body, 1.0 / (scale_x * full_x), scale_line,...  2.79 us
    pallas_call x1, Pallas kernels, shards(): call(mix_body, 'mix', (VMEM(turned, F32),), (VMEM,), (SMEM,) * 2 + (VMEM,...  1.75 us
    pallas_call x1, Pallas kernels, shards(): call(ahead_body, 'ahead', (cube, cube), (VMEM, VMEM), (VMEM, VMEM, VMEM),...  1.52 us
    pallas_call x1, Pallas kernels, shards(): call(functools.partial(back_body, 1.0 / (scale_x * full_x), close), 'back...  1.22 us
    pallas_call x1, Pallas kernels, shards(): call(local_body, 'local', (cube, cube, plain(n_energy, depth, width)), (V...  0.69 us
  transfers between devices with their start and end apart: 7, of which 5 were waited for; matrix products, arithmetic and copies ran while one was open for 0% of the time, Pallas kernels for 18%

profile of v4, /device:TPU:0, one launch (start us, length us, event | category | flops | bytes accessed | tf_op | source)
XLA Modules:
  0.0 30.1 jit_solution(3744709366976738958)
XLA Ops:
  0.6 3.5 %load.1 = (f32[4,256,8,128]{3,2,1,0:T(8,128)S(1)}, f32[256,8,128]{2,1,0:T(8,128)S(1)}, f32[8,256]{1,0:T(8,128)S(1)}) custom-call(f32[4]{0:T(128)} %line_ref.1, f32[4,16]{1,0:T(4,128)} %cross_ref.3, s32[4]{0:T(128)} %index_ref.3, f32[4,8,256,128]{3,2,1,0:T(8,128)} %conc_hbm.1), custom_call_target="tpu_custom_call" | custom-call | flops 10485760 | bytes 4194304 | tf_op jit(solution)/shard_map/load/pallas_call | solution.py:360
  4.1 3.1 %collective-permute-start = (f32[8,256]{1,0:T(8,128)S(1)}, f32[8,256]{1,0:T(8,128)S(1)}, u32[]{:S(2)}, u32[]{:S(2)}) collective-permute-start(f32[8,256]{1,0:T(8,128)S(1)} %get-tuple-element.30), channel_id=1, source_target_pairs={{0,4},{4,0},{1,5},{5,1},{2,6},{6,2},{3,7},{7,3},{8,12},{12,8},{9,1... | collective-permute-start | bytes 24584 | tf_op jit(solution)/shard_map/ppermute | solution.py:332
  7.2 0.7 %local.1 = (f32[4,256,8,128]{3,2,1,0:T(8,128)S(1)}, f32[4,256,8,128]{3,2,1,0:T(8,128)S(1)}, f32[4,8,128]{2,1,0:T(8,128)S(1)}) custom-call(f32[4,256,8,128]{3,2,1,0:T(8,128)S(1)} %get-tuple-element.31.source_ref, f32[256,8,128]{2,1,0:T(8,128)S(1)} %get-tuple-element.32.beyond_ref), custom_call_target="tpu_custom_call" | custom-call | flops 5242880 | bytes 1024 | tf_op jit(solution)/shard_map/local/pallas_call | solution.py:379
  7.9 0.9 %collective-permute-done.far_ref = f32[8,256]{1,0:T(8,128)S(1)} collective-permute-done((f32[8,256]{1,0:T(8,128)S(1)}, f32[8,256]{1,0:T(8,128)S(1)}, u32[]{:S(2)}, u32[]{:S(2)}) %collective-permute-start) | collective-permute-done | bytes 8224 | tf_op jit(solution)/shard_map/ppermute | solution.py:332
  8.8 0.6 %line.1 = (f32[256,8,128]{2,1,0:T(8,128)S(1)}, f32[2,4,8,128]{3,2,1,0:T(8,128)S(1)}) custom-call(f32[8,256]{1,0:T(8,128)S(1)} %collective-permute-done.far_ref, f32[4,256,8,128]{3,2,1,0:T(8,128)S(1)} %get-tuple-element.33.emit_ref, f32[4,8,128]{2,1,0:T(8,128)S(1)} %get-tuple-element.34.depth_ref.up_ref.further_ref), custom_call_target="tpu_custom_call" | custom-call | flops 2097152 | bytes 1024 | tf_op jit(solution)/shard_map/line/pallas_call | solution.py:389
  9.4 0.1 collective-permute-start.1
  9.4 1.2 %collective-permute-done.1.other_ref = f32[2,4,8,128]{3,2,1,0:T(8,128)S(1)} collective-permute-done((f32[2,4,8,128]{3,2,1,0:T(8,128)S(1)}, f32[2,4,8,128]{3,2,1,0:T(8,128)S(1)}, u32[]{:S(2)}, u32[]{:S(2)}) %collective-permute-start.1) | collective-permute-done | bytes 32800 | tf_op jit(solution)/shard_map/ppermute | solution.py:332
  10.6 2.1 %collective-permute-start.2 = (f32[2,4,8,128]{3,2,1,0:T(8,128)S(1)}, f32[2,4,8,128]{3,2,1,0:T(8,128)S(1)}, u32[]{:S(2)}, u32[]{:S(2)}) collective-permute-start(f32[2,4,8,128]{3,2,1,0:T(8,128)S(1)} %get-tuple-element.36.own_ref), channel_id=1, source_target_pairs={{0,16},{8,24},{16,0},{24,8},{1,17},{9,25},{17,1},{25,9},{2,18},{10... | collective-permute-start | bytes 98312 | tf_op jit(solution)/shard_map/ppermute | solution.py:332
  12.7 0.0 copy-start
  12.7 0.0 copy-start.3
  12.7 0.0 copy-start.5
  12.7 0.0 copy-start.1
  12.7 0.0 copy-start.2
  12.7 1.5 %ahead.1 = (f32[4,256,8,128]{3,2,1,0:T(8,128)S(1)}, f32[4,256,8,128]{3,2,1,0:T(8,128)S(1)}) custom-call(f32[256,8,128]{2,1,0:T(8,128)S(1)} %get-tuple-element.37.far_ref, f32[4,256,8,128]{3,2,1,0:T(8,128)S(1)} %get-tuple-element.38.trans_ref, f32[4,256,8,128]{3,2,1,0:T(8,128)S(1)} %get-tuple-element.33.emit_ref), custom_call_target="tpu_custom_call" | custom-call | flops 5242880 | bytes 1024 | tf_op jit(solution)/shard_map/ahead/pallas_call | solution.py:394
  14.2 0.4 %collective-permute-done.2.other_ref = f32[2,4,8,128]{3,2,1,0:T(8,128)S(1)} collective-permute-done((f32[2,4,8,128]{3,2,1,0:T(8,128)S(1)}, f32[2,4,8,128]{3,2,1,0:T(8,128)S(1)}, u32[]{:S(2)}, u32[]{:S(2)}) %collective-permute-start.2) | collective-permute-done | bytes 32800 | tf_op jit(solution)/shard_map/ppermute | solution.py:332
  14.6 2.1 %collective-permute-start.3 = (f32[1,4,8,128]{3,2,1,0:T(8,128)S(1)}, f32[1,4,8,128]{3,2,1,0:T(8,128)S(1)}, u32[]{:S(2)}, u32[]{:S(2)}) collective-permute-start(f32[1,4,8,128]{3,2,1,0:T(8,128)S(1)} %get-tuple-element.47.refs_0_), channel_id=1, source_target_pairs={{0,1},{1,0},{2,3},{3,2},{4,5},{5,4},{6,7},{7,6},{8,9},{9,8},{10,11... | collective-permute-start | bytes 49160 | tf_op jit(solution)/shard_map/ppermute | solution.py:332
  16.8 2.5 %collective-permute-start.4 = (f32[1,4,8,128]{3,2,1,0:T(8,128)S(1)}, f32[1,4,8,128]{3,2,1,0:T(8,128)S(1)}, u32[]{:S(2)}, u32[]{:S(2)}) collective-permute-start(f32[1,4,8,128]{3,2,1,0:T(8,128)S(1)} %get-tuple-element.47.refs_0_), channel_id=1, source_target_pairs={{0,3},{1,2},{2,1},{3,0},{4,7},{5,6},{6,5},{7,4},{8,11},{9,10},{10,... | collective-permute-start | bytes 49160 | tf_op jit(solution)/shard_map/ppermute | solution.py:332
  19.3 0.1 collective-permute-start.6
  19.4 0.0 copy-done
  19.4 0.0 copy-done.3
  19.4 0.0 copy-done.5
  19.4 0.3 %fan.1 = (f32[8,32]{1,0:T(8,128)S(1)}, f32[4,8,128]{2,1,0:T(8,128)S(1)}, f32[256,32]{1,0:T(8,128)S(1)}) custom-call(s32[1,256]{1,0:T(1,128)S(1)} %bitcast.3, s32[4,256]{1,0:T(4,128)S(1)} %bitcast.2, f32[4,256,128]{2,1,0:T(8,128)S(1)} %copy-done), custom_call_target="tpu_custom_call" | custom-call | flops 8388608 | bytes 524288 | tf_op jit(solution)/shard_map/fan/pallas_call | solution.py:417
  19.7 0.0 collective-permute-done.3.refs_1_
  19.7 2.6 %collective-permute-done.4.refs_2_.refs_3_ = f32[1,4,8,128]{3,2,1,0:T(8,128)S(1)} collective-permute-done((f32[1,4,8,128]{3,2,1,0:T(8,128)S(1)}, f32[1,4,8,128]{3,2,1,0:T(8,128)S(1)}, u32[]{:S(2)}, u32[]{:S(2)}) %collective-permute-start.4) | collective-permute-done | bytes 16416 | tf_op jit(solution)/shard_map/ppermute | solution.py:332
  22.3 0.0 copy-done.1
  22.3 0.0 copy-done.2
  22.3 1.2 %back.1 = (f32[256,8,128]{2,1,0:T(8,128)S(1)}, f32[8,256]{1,0:T(8,128)S(1)}, f32[4,8,128]{2,1,0:T(8,128)S(1)}, f32[4,8,128]{2,1,0:T(8,128)S(1)}) custom-call(f32[4,16]{1,0:T(4,128)S(1)} %copy-done.1, s32[4]{0:T(128)S(1)} %copy-done.2, f32[8,32]{1,0:T(8,128)S(1)} %get-tuple-element.28.gram_ref, f32[4,8,128]{2,1,0:T(8,128)S(1)} %get-tuple-element.29.pull_ref, ...), custom_call_target="tpu_custom_call" | custom-call | flops 2621440 | bytes 1024 | tf_op jit(solution)/shard_map/back/pallas_call | solution.py:422
  23.6 1.6 %collective-permute-start.5 = (f32[8,256]{1,0:T(8,128)S(1)}, f32[8,256]{1,0:T(8,128)S(1)}, u32[]{:S(2)}, u32[]{:S(2)}) collective-permute-start(f32[8,256]{1,0:T(8,128)S(1)} %get-tuple-element.48), channel_id=1, source_target_pairs={{0,4},{4,0},{1,5},{5,1},{2,6},{6,2},{3,7},{7,3},{8,12},{12,8},{9,1... | collective-permute-start | bytes 24584 | tf_op jit(solution)/shard_map/ppermute | solution.py:332
  25.1 0.0 copy-start.4
  25.1 1.8 %mix.1.mix_ref = f32[4,256,8,128]{3,2,1,0:T(8,128)S(1)} custom-call(f32[4,16]{1,0:T(4,128)S(1)} %copy-done.1, s32[4]{0:T(128)S(1)} %copy-done.2, f32[4,8,128]{2,1,0:T(8,128)S(1)} %get-tuple-element.50.gain_ref, f32[4,8,128]{2,1,0:T(8,128)S(1)} %get-tuple-element.51.shift_ref, f32[4,256,8,128]{3,2,1,0:T(8,128)S(1)} %get-tuple-element.52.rest_ref), custom_call_target="tpu_custom_call" | custom-call | flops 10485760 | bytes 1024 | tf_op jit(solution)/shard_map/mix/pallas_call | solution.py:435
  26.9 0.0 collective-permute-done.6.refs_2_
  26.9 0.4 %collective-permute-done.5.nearer_ref = f32[8,256]{1,0:T(8,128)S(1)} collective-permute-done((f32[8,256]{1,0:T(8,128)S(1)}, f32[8,256]{1,0:T(8,128)S(1)}, u32[]{:S(2)}, u32[]{:S(2)}) %collective-permute-start.5) | collective-permute-done | bytes 8224 | tf_op jit(solution)/shard_map/ppermute | solution.py:332
  27.3 0.0 copy-done.4
  27.3 2.8 %finish.1 = (f32[4,8,256,128]{3,2,1,0:T(8,128)}, f32[4,16,128]{2,1,0:T(8,128)}) custom-call(f32[4]{0:T(128)S(1)} %copy-done.4, f32[8,256]{1,0:T(8,128)S(1)} %collective-permute-done.5.nearer_ref, f32[256,8,128]{2,1,0:T(8,128)S(1)} %get-tuple-element.49.near_ref, f32[4,256,8,128]{3,2,1,0:T(8,128)S(1)} %mix.1.mix_ref, ...), custom_call_target="tpu_custom_call" | custom-call | flops 2621440 | bytes 4194304 | tf_op jit(solution)/shard_map/finish/pallas_call | solution.py:442
  (2 shorter events, 0.0 us)
Async XLA Ops:
  4.1 4.7 %collective-permute-start = (f32[8,256]{1,0:T(8,128)S(1)}, f32[8,256]{1,0:T(8,128)S(1)}, u32[]{:S(2)}, u32[]{:S(2)}) collective-permute-start(f32[8,256]{1,0:T(8,128)S(1)} %get-tuple-element.30), channel_id=1, source_target_pairs={{0,4},{4,0},{1,5},{5,1},{2,6},{6,2},{3,7},{7,3},{8,12},{12,8},{9,1... | collective-permute-start | bytes 24584 | tf_op jit(solution)/shard_map/ppermute | solution.py:332
  9.4 1.3 %collective-permute-start.1 = (f32[2,4,8,128]{3,2,1,0:T(8,128)S(1)}, f32[2,4,8,128]{3,2,1,0:T(8,128)S(1)}, u32[]{:S(2)}, u32[]{:S(2)}) collective-permute-start(f32[2,4,8,128]{3,2,1,0:T(8,128)S(1)} %get-tuple-element.35.own_ref), channel_id=1, source_target_pairs={{0,8},{8,0},{16,24},{24,16},{1,9},{9,1},{17,25},{25,17},{2,10},{10... | collective-permute-start | bytes 98312 | tf_op jit(solution)/shard_map/ppermute | solution.py:332
  10.6 4.0 %collective-permute-start.2 = (f32[2,4,8,128]{3,2,1,0:T(8,128)S(1)}, f32[2,4,8,128]{3,2,1,0:T(8,128)S(1)}, u32[]{:S(2)}, u32[]{:S(2)}) collective-permute-start(f32[2,4,8,128]{3,2,1,0:T(8,128)S(1)} %get-tuple-element.36.own_ref), channel_id=1, source_target_pairs={{0,16},{8,24},{16,0},{24,8},{1,17},{9,25},{17,1},{25,9},{2,18},{10... | collective-permute-start | bytes 98312 | tf_op jit(solution)/shard_map/ppermute | solution.py:332
  12.7 6.7 %copy-start = (f32[4,256,128]{2,1,0:T(8,128)S(1)}, f32[4,256,128]{2,1,0:T(8,128)}, u32[]{:S(2)}) copy-start(f32[4,256,128]{2,1,0:T(8,128)} %measured_ref.3) | copy-start | bytes 1572868
  12.7 6.7 %copy-start.3 = (s32[256,4]{0,1:T(4,128)S(1)}, s32[256,4]{0,1:T(4,128)}, u32[]{:S(2)}) copy-start(s32[256,4]{0,1:T(4,128)} %param.12) | copy-start | bytes 12292
  12.7 6.7 %copy-start.5 = (s32[256]{0:T(256)S(1)}, s32[256]{0:T(256)}, u32[]{:S(2)}) copy-start(s32[256]{0:T(256)} %param.11) | copy-start | bytes 3076
  12.7 9.6 %copy-start.1 = (f32[4,16]{1,0:T(4,128)S(1)}, f32[4,16]{1,0:T(4,128)}, u32[]{:S(2)}) copy-start(f32[4,16]{1,0:T(4,128)} %cross_ref.3) | copy-start | bytes 772
  12.7 9.6 %copy-start.2 = (s32[4]{0:T(128)S(1)}, s32[4]{0:T(128)}, u32[]{:S(2)}) copy-start(s32[4]{0:T(128)} %index_ref.3) | copy-start | bytes 52
  14.6 5.1 %collective-permute-start.3 = (f32[1,4,8,128]{3,2,1,0:T(8,128)S(1)}, f32[1,4,8,128]{3,2,1,0:T(8,128)S(1)}, u32[]{:S(2)}, u32[]{:S(2)}) collective-permute-start(f32[1,4,8,128]{3,2,1,0:T(8,128)S(1)} %get-tuple-element.47.refs_0_), channel_id=1, source_target_pairs={{0,1},{1,0},{2,3},{3,2},{4,5},{5,4},{6,7},{7,6},{8,9},{9,8},{10,11... | collective-permute-start | bytes 49160 | tf_op jit(solution)/shard_map/ppermute | solution.py:332
  16.8 5.5 %collective-permute-start.4 = (f32[1,4,8,128]{3,2,1,0:T(8,128)S(1)}, f32[1,4,8,128]{3,2,1,0:T(8,128)S(1)}, u32[]{:S(2)}, u32[]{:S(2)}) collective-permute-start(f32[1,4,8,128]{3,2,1,0:T(8,128)S(1)} %get-tuple-element.47.refs_0_), channel_id=1, source_target_pairs={{0,3},{1,2},{2,1},{3,0},{4,7},{5,6},{6,5},{7,4},{8,11},{9,10},{10,... | collective-permute-start | bytes 49160 | tf_op jit(solution)/shard_map/ppermute | solution.py:332
  19.3 7.6 %collective-permute-start.6 = (f32[1,4,8,128]{3,2,1,0:T(8,128)S(1)}, f32[1,4,8,128]{3,2,1,0:T(8,128)S(1)}, u32[]{:S(2)}, u32[]{:S(2)}) collective-permute-start(f32[1,4,8,128]{3,2,1,0:T(8,128)S(1)} %get-tuple-element.47.refs_0_), channel_id=1, source_target_pairs={{0,2},{1,3},{2,0},{3,1},{4,6},{5,7},{6,4},{7,5},{8,10},{9,11},{10,... | collective-permute-start | bytes 49160 | tf_op jit(solution)/shard_map/ppermute | solution.py:332
  23.6 3.7 %collective-permute-start.5 = (f32[8,256]{1,0:T(8,128)S(1)}, f32[8,256]{1,0:T(8,128)S(1)}, u32[]{:S(2)}, u32[]{:S(2)}) collective-permute-start(f32[8,256]{1,0:T(8,128)S(1)} %get-tuple-element.48), channel_id=1, source_target_pairs={{0,4},{4,0},{1,5},{5,1},{2,6},{6,2},{3,7},{7,3},{8,12},{12,8},{9,1... | collective-permute-start | bytes 24584 | tf_op jit(solution)/shard_map/ppermute | solution.py:332
  25.1 2.1 %copy-start.4 = (f32[4]{0:T(128)S(1)}, f32[4]{0:T(128)}, u32[]{:S(2)}) copy-start(f32[4]{0:T(128)} %line_ref.1) | copy-start | bytes 52

commit v5 on v4

--- a/solution.py
+++ b/solution.py
@@ -63,11 +63,11 @@
 
 
 def load_body(
-    scale, scale_x, line_hbm, cross_hbm, index_hbm, conc_hbm, emit_ref, beyond_ref, total_ref,
-    conc_ref, line_ref, cross_ref, index_ref, small_sems, sems,
+    scale, scale_x, line_hbm, cross_hbm, index_hbm, conc_hbm, conc_ref, emit_ref, beyond_ref, total_ref,
+    line_ref, cross_ref, index_ref, small_sems, sems,
 ):
     n_species, depth, rows, width = conc_hbm.shape
-    n_energy = emit_ref.shape[0]
+    n_early = emit_ref.shape[0]
 
     def copies(chunk):
         span = pl.ds(chunk * CHUNK, CHUNK)
@@ -104,7 +104,7 @@
                 x = chunk * CHUNK + q
                 conc = [conc_ref[s, x] for s in range(n_species)]
                 absorber.append(weighted(line, conc))
-                for e in range(n_energy):
+                for e in range(n_early):
                     emit_ref[e, x] = weighted([sigma[s][e] for s in range(n_species)], conc)
             sums = jnp.dot(split(jnp.concatenate(absorber, axis=0)), table, preferred_element_type=F32)
             for q in range(CHUNK):
@@ -114,16 +114,22 @@
         total_ref[:, part * LANES : (part + 1) * LANES] = total
 
 
-def local_body(source_ref, beyond_ref, trans_ref, emit_ref, depth_ref):
+def local_body(scale, cross_ref, index_ref, conc_ref, early_ref, beyond_ref, trans_ref, emit_ref, depth_ref):
     n_energy, rows, depth, width = trans_ref.shape
+    n_species, n_early = conc_ref.shape[0], early_ref.shape[0]
+    sigma = [[v * scale for v in row] for row in selected(cross_ref, index_ref)]
 
     def step(block, path):
         path = list(path)
         for q in range(STEP):
             x = block * STEP + q
             beyond = beyond_ref[x]
+            conc = [conc_ref[s, x] for s in range(n_species)]
             for e in range(n_energy):
-                emission = source_ref[e, x]
+                if e < n_early:
+                    emission = early_ref[e, x]
+                else:
+                    emission = weighted([sigma[s][e] for s in range(n_species)], conc)
                 trans = jnp.exp2(path[e] + beyond)
                 trans_ref[e, x] = trans
                 emit_ref[e, x] = emission * trans
@@ -204,7 +210,7 @@
     lax.fori_loop(0, rows // STEP, step, (zero,) * n_energy)
 
 
-def fan_body(offset_ref, weight_ref, measured_ref, gram_ref, pull_ref, turned_ref):
+def fan_body(scale, offset_ref, weight_ref, measured_ref, own_ref, gram_ref, pull_ref, turned_ref):
     depth, n_slices = gram_ref.shape
     taps, pixels = weight_ref.shape
     slab = lax.axis_index("slab")
@@ -220,11 +226,14 @@
         blocks.append(block)
     every = jnp.concatenate(blocks, axis=0)
     turned_ref[...] = every.T
-    gram_ref[...] = lax.dot_general(
+    gram = lax.dot_general(
         blocks[0].astype(BF16), every.astype(BF16), (((1,), (1,)), ((), ())), preferred_element_type=F32
     )
-    for e in range(pull_ref.shape[0]):
-        pull_ref[e] = jnp.dot(
+    gram_ref[...] = gram
+    n_energy, _, width = pull_ref.shape
+    sums = weigh(gram, [(0, own_ref)], depth, n_energy, width)
+    for e in range(n_energy):
+        pull_ref[e] = sums[e] * scale - jnp.dot(
             blocks[0], measured_ref[e], precision=lax.Precision.HIGHEST, preferred_element_type=F32
         )
 
@@ -247,7 +256,7 @@
     n_energy, rows, depth, width = fluor_ref.shape
     n_species = shift_ref.shape[0]
     sums = weigh(gram_ref[...], list(zip(close, lines)), depth, n_energy, width)
-    back = [sums[e] * scale - pull_ref[e] for e in range(n_energy)]
+    back = [sums[e] * scale + pull_ref[e] for e in range(n_energy)]
     gain = [back[e] * jnp.exp2(up_ref[e]) for e in range(n_energy)]
     sigma = selected(cross_ref, index_ref)
     pushed = [LN2 * back[e] * further_ref[e] for e in range(n_energy)]
@@ -297,8 +306,11 @@
     line = [line_ref[s] * scale_line for s in range(n_species)]
     keep = jnp.where(reached("det", count, True), 1.0, 0.0)
 
+    ends = [8, 16] + list(range(CHUNK, rows + 1, CHUNK))
+
     def copies(chunk):
-        span = pl.ds(chunk * CHUNK, CHUNK)
+        first = ends[chunk - 1] if chunk else 0
+        span = pl.ds(first, ends[chunk] - first)
         return [
             pltpu.make_async_copy(grad_ref.at[:, span, z, :], grad_hbm.at[:, z, span, :], sems.at[chunk])
             for z in range(depth)
@@ -308,8 +320,8 @@
         before = near_ref[x] + column
         for s in range(n_species):
             grad_ref[s, x] = mix_ref[s, x] + line[s] * before
-        if x % CHUNK == CHUNK - 1:
-            for copy in copies(x // CHUNK):
+        if x + 1 in ends:
+            for copy in copies(ends.index(x + 1)):
                 copy.start()
 
     start = pl.multiple_of(lax.axis_index(("beam", "slab")) * share, share)
@@ -319,12 +331,9 @@
     copy = pltpu.make_async_copy(residual_ref, residual_hbm, residual_sem)
     copy.start()
 
-    def finish(chunk, carry):
+    for chunk in range(len(ends)):
         for done in copies(chunk):
             done.wait()
-        return carry
-
-    lax.fori_loop(0, rows // CHUNK, finish, 0)
     copy.wait()
 
 
@@ -353,18 +362,20 @@
     full_x, full_y = rows * n_beam, width * n_det
     scale_x = -(1.5 / full_x) * LOG2E
     scale_y = -(1.5 / full_y) * LOG2E
+    scale_sum = 1.0 / (scale_x * full_x)
     voxels = depth * rows * width
+    turned = (n_species, rows, depth, width)
     cube = VMEM((n_energy, rows, depth, width), F32)
     plane = VMEM((rows, depth, width), F32)
 
-    emission, far_local, row_total = call(
+    n_early = n_energy // 2
+    conc_x, emission, far_local, row_total = call(
         functools.partial(load_body, scale_y, scale_x),
         "load",
-        (cube, plane, plain(depth, rows)),
-        (VMEM, VMEM, VMEM),
+        (VMEM(turned, F32), VMEM((n_early, rows, depth, width), F32), plane, plain(depth, rows)),
+        (VMEM,) * 4,
         (HBM,) * 4,
         [
-            VMEM((n_species, rows, depth, width), F32),
             SMEM(line.shape, F32),
             SMEM(cross.shape, F32),
             SMEM(index.shape, index.dtype),
@@ -377,13 +388,13 @@
     far = beyond(row_total, "det", False)
 
     trans, emit, own_depth = call(
-        local_body,
+        functools.partial(local_body, scale_x),
         "local",
         (cube, cube, plain(n_energy, depth, width)),
         (VMEM, VMEM, VMEM),
-        (VMEM, VMEM),
+        (SMEM, SMEM) + (VMEM,) * 3,
         cost=(20 * voxels, 4 * voxels, 1024),
-    )(emission, far_local)
+    )(cross, index, conc_x, emission, far_local)
 
     wide = (n_energy, depth, width)
     far_wide, pair = call(
@@ -411,16 +422,16 @@
         distance *= 2
 
     lines = [pair] + [swap(pair, "slab", r) for r in range(1, n_slab)]
-    close = [r for r in range(n_slab) if r & (r + 1) == 0]
+    close = [r for r in range(1, n_slab) if r & (r + 1) == 0]
 
     pixels = fan_offset.shape[0]
     gram, pull, fan_turned = call(
-        fan_body, "fan", (plain(depth, depth * n_slab), plain(*wide), plain(pixels, depth * n_slab)),
-        (VMEM,) * 3, (VMEM,) * 3, cost=(8 * depth * measured.size, 0, 4 * measured.size),
-    )(fan_offset[None, :], fan_weight.T, measured)
+        functools.partial(fan_body, scale_sum), "fan", (plain(depth, depth * n_slab), plain(*wide), plain(pixels, depth * n_slab)),
+        (VMEM,) * 3, (VMEM,) * 4, cost=(8 * depth * measured.size, 0, 4 * measured.size),
+    )(fan_offset[None, :], fan_weight.T, measured, pair)
 
     near, column_total, gain, shift = call(
-        functools.partial(back_body, 1.0 / (scale_x * full_x), close),
+        functools.partial(back_body, scale_sum, close),
         "back",
         (plane, plain(depth, rows), plain(*wide), plain(n_species, depth, width)),
         (VMEM,) * 4,
@@ -431,7 +442,6 @@
     nearer = beyond(column_total, "det", True)
 
     scale_line = scale_y * LN2 / scale_x
-    turned = (n_species, rows, depth, width)
     mixed = call(
         mix_body, "mix", (VMEM(turned, F32),), (VMEM,), (SMEM,) * 2 + (VMEM,) * 3,
         cost=(40 * voxels, 0, 1024),
@@ -440,7 +450,7 @@
     share = pixels // (n_beam * n_slab)
     return tuple(
         call(
-            functools.partial(finish_body, 1.0 / (scale_x * full_x), scale_line, n_det),
+            functools.partial(finish_body, scale_sum, scale_line, n_det),
             "finish",
             (plain(*conc.shape), plain(n_energy, share, width)),
             (HBM, HBM),
@@ -448,7 +458,7 @@
             [
                 VMEM(turned, F32),
                 VMEM((n_energy, share, width), F32),
-                pltpu.SemaphoreType.DMA((rows // CHUNK,)),
+                pltpu.SemaphoreType.DMA((rows // CHUNK + 2,)),
                 pltpu.SemaphoreType.DMA,
             ],
             limit=16,

time: 30.2 us -> 30 us (level)
  Pallas kernels: 12.4 us -> 13 us
  waiting for transfers between devices: 5.46 us -> 4.9 us
    pallas_call x5, Pallas kernels: 8.5 us -> 9.16 us  [the longest x1 3.01 us: shards(): call(functools.partial(load_body, scale_y, scale_x), 'load', (VMEM(turned...]
    ppermute x7, waiting for transfers between devices: 5.46 us -> 4.9 us  [swap(): lax.ppermute(value, axis, [(i, i ^ distance) for i in range(lax.axis_size...]
    ppermute x7, starting transfers between devices: 11.5 us -> 11.2 us  [swap(): lax.ppermute(value, axis, [(i, i ^ distance) for i in range(lax.axis_size...]
  transfers between devices with their start and end apart: 7 -> 7, of which waited for: 5 -> 5; matrix products, arithmetic and copies ran while one was open for 0% -> 0% of each run, Pallas kernels for 18% -> 22%
where the time goes in v5:
time: 30 us; the launch traced here: 29.9 us
  Pallas kernels  13 us (43%)
  starting transfers between devices  11.2 us (37%)
  waiting for transfers between devices  4.9 us (16%)
  between operations  0.73 us (2%)
    ppermute x7, starting transfers between devices, swap(): lax.ppermute(value, axis, [(i, i ^ distance) for i in range(lax.axis_size...  11.2 us
    ppermute x7, waiting for transfers between devices, swap(): lax.ppermute(value, axis, [(i, i ^ distance) for i in range(lax.axis_size...  4.9 us
    pallas_call x1, Pallas kernels, shards(): call(functools.partial(load_body, scale_y, scale_x), 'load', (VMEM(turned...  3.01 us
    pallas_call x1, Pallas kernels, shards(): call(functools.partial(finish_body, scale_sum, scale_line, n_det), 'finis...  2.81 us
    pallas_call x1, Pallas kernels, shards(): call(functools.partial(local_body, scale_x), 'local', (cube, cube, plain(...  1.8 us
    pallas_call x1, Pallas kernels, shards(): call(mix_body, 'mix', (VMEM(turned, F32),), (VMEM,), (SMEM,) * 2 + (VMEM,...  1.75 us
    pallas_call x1, Pallas kernels, shards(): call(ahead_body, 'ahead', (cube, cube), (VMEM, VMEM), (VMEM, VMEM, VMEM),...  1.51 us
    pallas_call x1, Pallas kernels, shards(): call(functools.partial(back_body, scale_sum, close), 'back', (plane, plai...  1.2 us
  transfers between devices with their start and end apart: 7, of which 5 were waited for; matrix products, arithmetic and copies ran while one was open for 0% of the time, Pallas kernels for 22%

profile of v5, /device:TPU:0, one launch (start us, length us, event | category | flops | bytes accessed | tf_op | source)
XLA Modules:
  0.0 29.9 jit_solution(6677066488335440720)
XLA Ops:
  0.6 0.0 copy-start.2
  0.6 0.0 copy-start.1
  0.6 3.0 %load.1 = (f32[4,256,8,128]{3,2,1,0:T(8,128)S(1)}, f32[2,256,8,128]{3,2,1,0:T(8,128)S(1)}, f32[256,8,128]{2,1,0:T(8,128)S(1)}, f32[8,256]{1,0:T(8,128)S(1)}) custom-call(f32[4]{0:T(128)} %line_ref.1, f32[4,16]{1,0:T(4,128)} %cross_ref.5, s32[4]{0:T(128)} %index_ref.5, f32[4,8,256,128]{3,2,1,0:T(8,128)} %conc_hbm.1), custom_call_target="tpu_custom_call" | custom-call | flops 10485760 | bytes 4194304 | tf_op jit(solution)/shard_map/load/pallas_call | solution.py:372
  3.7 3.1 %collective-permute-start = (f32[8,256]{1,0:T(8,128)S(1)}, f32[8,256]{1,0:T(8,128)S(1)}, u32[]{:S(2)}, u32[]{:S(2)}) collective-permute-start(f32[8,256]{1,0:T(8,128)S(1)} %get-tuple-element.29), channel_id=1, source_target_pairs={{0,4},{4,0},{1,5},{5,1},{2,6},{6,2},{3,7},{7,3},{8,12},{12,8},{9,1... | collective-permute-start | bytes 24584 | tf_op jit(solution)/shard_map/ppermute | solution.py:341
  6.7 0.0 copy-done.2
  6.7 0.0 copy-done.1
  6.7 1.8 %local.1 = (f32[4,256,8,128]{3,2,1,0:T(8,128)S(1)}, f32[4,256,8,128]{3,2,1,0:T(8,128)S(1)}, f32[4,8,128]{2,1,0:T(8,128)S(1)}) custom-call(f32[4,16]{1,0:T(4,128)S(1)} %copy-done.1, s32[4]{0:T(128)S(1)} %copy-done.2, f32[4,256,8,128]{3,2,1,0:T(8,128)S(1)} %get-tuple-element.30.conc_ref, f32[2,256,8,128]{3,2,1,0:T(8,128)S(1)} %get-tuple-element.31.early_ref, ...), custom_call_target="tpu_custom_call" | custom-call | flops 5242880 | bytes 1024 | tf_op jit(solution)/shard_map/local/pallas_call | solution.py:390
  8.5 0.0 collective-permute-done.far_ref
  8.5 0.6 %line.1 = (f32[256,8,128]{2,1,0:T(8,128)S(1)}, f32[2,4,8,128]{3,2,1,0:T(8,128)S(1)}) custom-call(f32[8,256]{1,0:T(8,128)S(1)} %collective-permute-done.far_ref, f32[4,256,8,128]{3,2,1,0:T(8,128)S(1)} %get-tuple-element.33.emit_ref, f32[4,8,128]{2,1,0:T(8,128)S(1)} %get-tuple-element.34.depth_ref.up_ref.further_ref), custom_call_target="tpu_custom_call" | custom-call | flops 2097152 | bytes 1024 | tf_op jit(solution)/shard_map/line/pallas_call | solution.py:400
  9.1 0.1 collective-permute-start.1
  9.2 1.2 %collective-permute-done.1.other_ref = f32[2,4,8,128]{3,2,1,0:T(8,128)S(1)} collective-permute-done((f32[2,4,8,128]{3,2,1,0:T(8,128)S(1)}, f32[2,4,8,128]{3,2,1,0:T(8,128)S(1)}, u32[]{:S(2)}, u32[]{:S(2)}) %collective-permute-start.1) | collective-permute-done | bytes 32800 | tf_op jit(solution)/shard_map/ppermute | solution.py:341
  10.4 1.9 %collective-permute-start.2 = (f32[2,4,8,128]{3,2,1,0:T(8,128)S(1)}, f32[2,4,8,128]{3,2,1,0:T(8,128)S(1)}, u32[]{:S(2)}, u32[]{:S(2)}) collective-permute-start(f32[2,4,8,128]{3,2,1,0:T(8,128)S(1)} %get-tuple-element.36.own_ref), channel_id=1, source_target_pairs={{0,16},{8,24},{16,0},{24,8},{1,17},{9,25},{17,1},{25,9},{2,18},{10... | collective-permute-start | bytes 98312 | tf_op jit(solution)/shard_map/ppermute | solution.py:341
  12.3 0.0 copy-start
  12.3 0.0 copy-start.3
  12.3 0.0 copy-start.5
  12.3 1.5 %ahead.1 = (f32[4,256,8,128]{3,2,1,0:T(8,128)S(1)}, f32[4,256,8,128]{3,2,1,0:T(8,128)S(1)}) custom-call(f32[256,8,128]{2,1,0:T(8,128)S(1)} %get-tuple-element.37.far_ref, f32[4,256,8,128]{3,2,1,0:T(8,128)S(1)} %get-tuple-element.38.trans_ref, f32[4,256,8,128]{3,2,1,0:T(8,128)S(1)} %get-tuple-element.33.emit_ref), custom_call_target="tpu_custom_call" | custom-call | flops 5242880 | bytes 1024 | tf_op jit(solution)/shard_map/ahead/pallas_call | solution.py:405
  13.8 0.6 %collective-permute-done.2.other_ref = f32[2,4,8,128]{3,2,1,0:T(8,128)S(1)} collective-permute-done((f32[2,4,8,128]{3,2,1,0:T(8,128)S(1)}, f32[2,4,8,128]{3,2,1,0:T(8,128)S(1)}, u32[]{:S(2)}, u32[]{:S(2)}) %collective-permute-start.2) | collective-permute-done | bytes 32800 | tf_op jit(solution)/shard_map/ppermute | solution.py:341
  14.4 4.0 %collective-permute-start.4 = (f32[1,4,8,128]{3,2,1,0:T(8,128)S(1)}, f32[1,4,8,128]{3,2,1,0:T(8,128)S(1)}, u32[]{:S(2)}, u32[]{:S(2)}) collective-permute-start(f32[1,4,8,128]{3,2,1,0:T(8,128)S(1)} %get-tuple-element.44.own_ref.refs_0_), channel_id=1, source_target_pairs={{0,3},{1,2},{2,1},{3,0},{4,7},{5,6},{6,5},{7,4},{8,11},{9,10},{10,... | collective-permute-start | bytes 49160 | tf_op jit(solution)/shard_map/ppermute | solution.py:341
  18.4 0.0 collective-permute-start.3
  18.4 0.6 %collective-permute-start.6 = (f32[1,4,8,128]{3,2,1,0:T(8,128)S(1)}, f32[1,4,8,128]{3,2,1,0:T(8,128)S(1)}, u32[]{:S(2)}, u32[]{:S(2)}) collective-permute-start(f32[1,4,8,128]{3,2,1,0:T(8,128)S(1)} %get-tuple-element.44.own_ref.refs_0_), channel_id=1, source_target_pairs={{0,2},{1,3},{2,0},{3,1},{4,6},{5,7},{6,4},{7,5},{8,10},{9,11},{10,... | collective-permute-start | bytes 49160 | tf_op jit(solution)/shard_map/ppermute | solution.py:341
  19.0 0.0 copy-done
  19.0 0.0 copy-done.3
  19.0 0.0 copy-done.5
  19.0 0.3 %fan.1 = (f32[8,32]{1,0:T(8,128)S(1)}, f32[4,8,128]{2,1,0:T(8,128)S(1)}, f32[256,32]{1,0:T(8,128)S(1)}) custom-call(s32[1,256]{1,0:T(1,128)S(1)} %bitcast.3, s32[4,256]{1,0:T(4,128)S(1)} %bitcast.2, f32[4,256,128]{2,1,0:T(8,128)S(1)} %copy-done, f32[1,4,8,128]{3,2,1,0:T(8,128)S(1)} %get-tuple-element.44.own_ref.refs_0_), custom_call_target="tpu_custom_call" | custom-call | flops 8388608 | bytes 524288 | tf_op jit(solution)/shard_map/fan/pallas_call | solution.py:428
  19.4 0.7 %collective-permute-done.4.refs_1_.refs_3_ = f32[1,4,8,128]{3,2,1,0:T(8,128)S(1)} collective-permute-done((f32[1,4,8,128]{3,2,1,0:T(8,128)S(1)}, f32[1,4,8,128]{3,2,1,0:T(8,128)S(1)}, u32[]{:S(2)}, u32[]{:S(2)}) %collective-permute-start.4) | collective-permute-done | bytes 16416 | tf_op jit(solution)/shard_map/ppermute | solution.py:341
  20.1 2.0 %collective-permute-done.3.refs_0_.refs_1_ = f32[1,4,8,128]{3,2,1,0:T(8,128)S(1)} collective-permute-done((f32[1,4,8,128]{3,2,1,0:T(8,128)S(1)}, f32[1,4,8,128]{3,2,1,0:T(8,128)S(1)}, u32[]{:S(2)}, u32[]{:S(2)}) %collective-permute-start.3) | collective-permute-done | bytes 16416 | tf_op jit(solution)/shard_map/ppermute | solution.py:341
  22.1 1.2 %back.1 = (f32[256,8,128]{2,1,0:T(8,128)S(1)}, f32[8,256]{1,0:T(8,128)S(1)}, f32[4,8,128]{2,1,0:T(8,128)S(1)}, f32[4,8,128]{2,1,0:T(8,128)S(1)}) custom-call(f32[4,16]{1,0:T(4,128)S(1)} %copy-done.1, s32[4]{0:T(128)S(1)} %copy-done.2, f32[8,32]{1,0:T(8,128)S(1)} %get-tuple-element.45.gram_ref, f32[4,8,128]{2,1,0:T(8,128)S(1)} %get-tuple-element.46.pull_ref, ...), custom_call_target="tpu_custom_call" | custom-call | flops 2621440 | bytes 1024 | tf_op jit(solution)/shard_map/back/pallas_call | solution.py:433
  23.3 1.6 %collective-permute-start.5 = (f32[8,256]{1,0:T(8,128)S(1)}, f32[8,256]{1,0:T(8,128)S(1)}, u32[]{:S(2)}, u32[]{:S(2)}) collective-permute-start(f32[8,256]{1,0:T(8,128)S(1)} %get-tuple-element.50), channel_id=1, source_target_pairs={{0,4},{4,0},{1,5},{5,1},{2,6},{6,2},{3,7},{7,3},{8,12},{12,8},{9,1... | collective-permute-start | bytes 24584 | tf_op jit(solution)/shard_map/ppermute | solution.py:341
  24.9 0.0 copy-start.4
  24.9 1.8 %mix.1.mix_ref = f32[4,256,8,128]{3,2,1,0:T(8,128)S(1)} custom-call(f32[4,16]{1,0:T(4,128)S(1)} %copy-done.1, s32[4]{0:T(128)S(1)} %copy-done.2, f32[4,8,128]{2,1,0:T(8,128)S(1)} %get-tuple-element.52.gain_ref, f32[4,8,128]{2,1,0:T(8,128)S(1)} %get-tuple-element.53.shift_ref, f32[4,256,8,128]{3,2,1,0:T(8,128)S(1)} %get-tuple-element.54.rest_ref), custom_call_target="tpu_custom_call" | custom-call | flops 10485760 | bytes 1024 | tf_op jit(solution)/shard_map/mix/pallas_call | solution.py:445
  26.7 0.0 collective-permute-done.6.refs_2_
  26.7 0.4 %collective-permute-done.5.nearer_ref = f32[8,256]{1,0:T(8,128)S(1)} collective-permute-done((f32[8,256]{1,0:T(8,128)S(1)}, f32[8,256]{1,0:T(8,128)S(1)}, u32[]{:S(2)}, u32[]{:S(2)}) %collective-permute-start.5) | collective-permute-done | bytes 8224 | tf_op jit(solution)/shard_map/ppermute | solution.py:341
  27.0 0.0 copy-done.4
  27.0 2.8 %finish.1 = (f32[4,8,256,128]{3,2,1,0:T(8,128)}, f32[4,16,128]{2,1,0:T(8,128)}) custom-call(f32[4]{0:T(128)S(1)} %copy-done.4, f32[8,256]{1,0:T(8,128)S(1)} %collective-permute-done.5.nearer_ref, f32[256,8,128]{2,1,0:T(8,128)S(1)} %get-tuple-element.51.near_ref, f32[4,256,8,128]{3,2,1,0:T(8,128)S(1)} %mix.1.mix_ref, ...), custom_call_target="tpu_custom_call" | custom-call | flops 2621440 | bytes 4194304 | tf_op jit(solution)/shard_map/finish/pallas_call | solution.py:452
  (2 shorter events, 0.0 us)
Async XLA Ops:
  0.6 6.1 %copy-start.2 = (s32[4]{0:T(128)S(1)}, s32[4]{0:T(128)}, u32[]{:S(2)}) copy-start(s32[4]{0:T(128)} %index_ref.5) | copy-start | bytes 52
  0.6 6.1 %copy-start.1 = (f32[4,16]{1,0:T(4,128)S(1)}, f32[4,16]{1,0:T(4,128)}, u32[]{:S(2)}) copy-start(f32[4,16]{1,0:T(4,128)} %cross_ref.5) | copy-start | bytes 772
  3.7 4.9 %collective-permute-start = (f32[8,256]{1,0:T(8,128)S(1)}, f32[8,256]{1,0:T(8,128)S(1)}, u32[]{:S(2)}, u32[]{:S(2)}) collective-permute-start(f32[8,256]{1,0:T(8,128)S(1)} %get-tuple-element.29), channel_id=1, source_target_pairs={{0,4},{4,0},{1,5},{5,1},{2,6},{6,2},{3,7},{7,3},{8,12},{12,8},{9,1... | collective-permute-start | bytes 24584 | tf_op jit(solution)/shard_map/ppermute | solution.py:341
  9.1 1.3 %collective-permute-start.1 = (f32[2,4,8,128]{3,2,1,0:T(8,128)S(1)}, f32[2,4,8,128]{3,2,1,0:T(8,128)S(1)}, u32[]{:S(2)}, u32[]{:S(2)}) collective-permute-start(f32[2,4,8,128]{3,2,1,0:T(8,128)S(1)} %get-tuple-element.35.own_ref), channel_id=1, source_target_pairs={{0,8},{8,0},{16,24},{24,16},{1,9},{9,1},{17,25},{25,17},{2,10},{10... | collective-permute-start | bytes 98312 | tf_op jit(solution)/shard_map/ppermute | solution.py:341
  10.4 4.0 %collective-permute-start.2 = (f32[2,4,8,128]{3,2,1,0:T(8,128)S(1)}, f32[2,4,8,128]{3,2,1,0:T(8,128)S(1)}, u32[]{:S(2)}, u32[]{:S(2)}) collective-permute-start(f32[2,4,8,128]{3,2,1,0:T(8,128)S(1)} %get-tuple-element.36.own_ref), channel_id=1, source_target_pairs={{0,16},{8,24},{16,0},{24,8},{1,17},{9,25},{17,1},{25,9},{2,18},{10... | collective-permute-start | bytes 98312 | tf_op jit(solution)/shard_map/ppermute | solution.py:341
  12.3 6.8 %copy-start = (f32[4,256,128]{2,1,0:T(8,128)S(1)}, f32[4,256,128]{2,1,0:T(8,128)}, u32[]{:S(2)}) copy-start(f32[4,256,128]{2,1,0:T(8,128)} %measured_ref.3) | copy-start | bytes 1572868
  12.3 6.8 %copy-start.3 = (s32[256,4]{0,1:T(4,128)S(1)}, s32[256,4]{0,1:T(4,128)}, u32[]{:S(2)}) copy-start(s32[256,4]{0,1:T(4,128)} %param.12) | copy-start | bytes 12292
  12.3 6.8 %copy-start.5 = (s32[256]{0:T(256)S(1)}, s32[256]{0:T(256)}, u32[]{:S(2)}) copy-start(s32[256]{0:T(256)} %param.11) | copy-start | bytes 3076
  14.4 5.7 %collective-permute-start.4 = (f32[1,4,8,128]{3,2,1,0:T(8,128)S(1)}, f32[1,4,8,128]{3,2,1,0:T(8,128)S(1)}, u32[]{:S(2)}, u32[]{:S(2)}) collective-permute-start(f32[1,4,8,128]{3,2,1,0:T(8,128)S(1)} %get-tuple-element.44.own_ref.refs_0_), channel_id=1, source_target_pairs={{0,3},{1,2},{2,1},{3,0},{4,7},{5,6},{6,5},{7,4},{8,11},{9,10},{10,... | collective-permute-start | bytes 49160 | tf_op jit(solution)/shard_map/ppermute | solution.py:341
  18.4 3.7 %collective-permute-start.3 = (f32[1,4,8,128]{3,2,1,0:T(8,128)S(1)}, f32[1,4,8,128]{3,2,1,0:T(8,128)S(1)}, u32[]{:S(2)}, u32[]{:S(2)}) collective-permute-start(f32[1,4,8,128]{3,2,1,0:T(8,128)S(1)} %get-tuple-element.44.own_ref.refs_0_), channel_id=1, source_target_pairs={{0,1},{1,0},{2,3},{3,2},{4,5},{5,4},{6,7},{7,6},{8,9},{9,8},{10,11... | collective-permute-start | bytes 49160 | tf_op jit(solution)/shard_map/ppermute | solution.py:341
  18.4 8.3 %collective-permute-start.6 = (f32[1,4,8,128]{3,2,1,0:T(8,128)S(1)}, f32[1,4,8,128]{3,2,1,0:T(8,128)S(1)}, u32[]{:S(2)}, u32[]{:S(2)}) collective-permute-start(f32[1,4,8,128]{3,2,1,0:T(8,128)S(1)} %get-tuple-element.44.own_ref.refs_0_), channel_id=1, source_target_pairs={{0,2},{1,3},{2,0},{3,1},{4,6},{5,7},{6,4},{7,5},{8,10},{9,11},{10,... | collective-permute-start | bytes 49160 | tf_op jit(solution)/shard_map/ppermute | solution.py:341
  23.3 3.7 %collective-permute-start.5 = (f32[8,256]{1,0:T(8,128)S(1)}, f32[8,256]{1,0:T(8,128)S(1)}, u32[]{:S(2)}, u32[]{:S(2)}) collective-permute-start(f32[8,256]{1,0:T(8,128)S(1)} %get-tuple-element.50), channel_id=1, source_target_pairs={{0,4},{4,0},{1,5},{5,1},{2,6},{6,2},{3,7},{7,3},{8,12},{12,8},{9,1... | collective-permute-start | bytes 24584 | tf_op jit(solution)/shard_map/ppermute | solution.py:341
  24.9 2.1 %copy-start.4 = (f32[4]{0:T(128)S(1)}, f32[4]{0:T(128)}, u32[]{:S(2)}) copy-start(f32[4]{0:T(128)} %line_ref.1) | copy-start | bytes 52

commit v6 on v5

--- a/solution.py
+++ b/solution.py
@@ -7,6 +7,7 @@
 from jax.experimental import pallas as pl
 from jax.experimental.pallas import tpu as pltpu
 from jax.sharding import PartitionSpec as P
+
 
 VMEM, SMEM, HBM = pltpu.VMEM, pltpu.SMEM, pltpu.HBM
 F32, BF16 = jnp.float32, jnp.bfloat16
@@ -17,7 +18,7 @@
 LOG2E = 1.0 / LN2
 
 
-def call(body, name, out_shape, out_spaces, in_spaces, scratch=(), limit=8, cost=None):
+def call(body, out_shape, out_spaces, in_spaces, scratch=(), limit=8, cost=None):
     flops, exps, size = cost
     return pl.pallas_call(
         body,
@@ -27,7 +28,6 @@
         scratch_shapes=list(scratch),
         compiler_params=pltpu.CompilerParams(vmem_limit_bytes=limit << 20),
         cost_estimate=pl.CostEstimate(flops=flops, transcendentals=exps, bytes_accessed=size),
-        name=name,
     )
 
 
@@ -157,7 +157,7 @@
 
 
 def line_body(count, far_ref, emit_ref, depth_ref, far_out, pair_ref):
-    n_energy, rows, depth, width = emit_ref.shape
+    n_energy, _, _, width = emit_ref.shape
     keep = jnp.where(reached("det", count, False), 1.0, 0.0)
     sums = [[None, None] for _ in range(n_energy)]
     for x, factor in columns(far_ref, lambda v: jnp.exp2(v * keep), width):
@@ -170,25 +170,28 @@
         pair_ref[1, e] = sums[e][0] + sums[e][1]
 
 
-def merge_body(distance, first_round, own_ref, other_ref, up_ref, further_ref, out_ref, up_out, further_out):
-    lower = (lax.axis_index("beam") & distance) == 0
-    span, sums = own_ref[0], own_ref[1]
-    first = jnp.where(lower, span, other_ref[0])
-    fade = jnp.exp2(first)
-    late = fade * jnp.where(lower, other_ref[1], sums)
-    zero = jnp.zeros_like(late)
-    if first_round:
-        further_out[...] = jnp.where(lower, late, zero)
-        up_out[...] = jnp.where(lower, zero, first)
-    else:
-        further_out[...] = jnp.where(lower, further_ref[...] + late, fade * further_ref[...])
-        up_out[...] = up_ref[...] + jnp.where(lower, zero, first)
-    total = jnp.where(lower, sums, other_ref[1]) + late
-    if out_ref.shape[0] == 2:
-        out_ref[0] = span + other_ref[0]
-        out_ref[1] = total
-    else:
-        out_ref[0] = total
+def merge_body(*refs):
+    pairs, (total_ref, up_ref, further_ref) = refs[:-3], refs[-3:]
+    beam = lax.axis_index("beam")
+    state = [(ref[0], ref[1]) for ref in pairs]
+    up, further = jnp.zeros_like(state[0][0]), jnp.zeros_like(state[0][0])
+    distance = 1
+    while len(state) > 1:
+        lower = (beam & distance) == 0
+        merged = []
+        for i in range(0, len(state), 2):
+            (span, sums), (other_span, other_sums) = state[i], state[i + 1]
+            fade = jnp.exp2(jnp.where(lower, span, other_span))
+            late = fade * jnp.where(lower, other_sums, sums)
+            if i == 0:
+                further = jnp.where(lower, further + late, fade * further)
+                up = jnp.where(lower, up, up + other_span)
+            merged.append((span + other_span, jnp.where(lower, sums, other_sums) + late))
+        state = merged
+        distance *= 2
+    total_ref[0] = state[0][1]
+    up_ref[...] = up
+    further_ref[...] = further
 
 
 def ahead_body(far_ref, trans_ref, emit_ref, fluor_ref, rest_ref):
@@ -210,28 +213,31 @@
     lax.fori_loop(0, rows // STEP, step, (zero,) * n_energy)
 
 
-def fan_body(scale, offset_ref, weight_ref, measured_ref, own_ref, gram_ref, pull_ref, turned_ref):
-    depth, n_slices = gram_ref.shape
+def fan_body(scale, near_slabs, offset_ref, weight_ref, measured_ref, own_ref, gram_ref, pull_ref, turned_ref):
+    depth, n_slab = gram_ref.shape[0], turned_ref.shape[1] // gram_ref.shape[0]
     taps, pixels = weight_ref.shape
-    slab = lax.axis_index("slab")
+    own = lax.axis_index("slab")
     offset = jnp.broadcast_to(offset_ref[...], (depth, pixels))
-    level = lax.broadcasted_iota(jnp.int32, (depth, pixels), 0)
-    blocks = []
-    for r in range(n_slices // depth):
-        place = level + (slab ^ r) * depth - offset
-        block = jnp.zeros((depth, pixels), F32)
-        for j in range(taps):
-            tap = jnp.broadcast_to(weight_ref[j : j + 1, :], (depth, pixels)).astype(F32)
-            block = block + jnp.where(place == j, tap, 0.0)
-        blocks.append(block)
-    every = jnp.concatenate(blocks, axis=0)
-    turned_ref[...] = every.T
+    level = lax.broadcasted_iota(jnp.int32, (depth, pixels), 0) - offset
+    taps = [jnp.broadcast_to(weight_ref[j : j + 1, :], (depth, pixels)).astype(F32) for j in range(taps)]
+
+    def block(slab):
+        place = level + slab * depth
+        found = jnp.zeros((depth, pixels), F32)
+        for j, tap in enumerate(taps):
+            found = found + jnp.where(place == j, tap, 0.0)
+        return found
+
+    blocks = [block(own ^ r) for r in range(n_slab)]
+    turned_ref[...] = jnp.concatenate(blocks, axis=0).T
+    odd = own + jnp.where((own & 1) == 1, 1, -1)
+    near = jnp.concatenate([block(odd) if r is None else blocks[r] for r in near_slabs], axis=0)
     gram = lax.dot_general(
-        blocks[0].astype(BF16), every.astype(BF16), (((1,), (1,)), ((), ())), preferred_element_type=F32
+        blocks[0].astype(BF16), near.astype(BF16), (((1,), (1,)), ((), ())), preferred_element_type=F32
     )
     gram_ref[...] = gram
     n_energy, _, width = pull_ref.shape
-    sums = weigh(gram, [(0, own_ref)], depth, n_energy, width)
+    sums = weigh(gram, [(0, own_ref, 0)], depth, n_energy, width)
     for e in range(n_energy):
         pull_ref[e] = sums[e] * scale - jnp.dot(
             blocks[0], measured_ref[e], precision=lax.Precision.HIGHEST, preferred_element_type=F32
@@ -241,21 +247,21 @@
 def weigh(weights, lines, depth, n_energy, width):
     height = weights.shape[0]
     sums = [[None, None] for _ in range(n_energy)]
-    for order, (r, lines_ref) in enumerate(lines):
+    for order, (r, lines_ref, i) in enumerate(lines):
         for z in range(depth):
             place = r * depth + z
             weight = jnp.broadcast_to(weights[:, place : place + 1], (height, width))
             for e in range(n_energy):
-                value = weight * lines_ref[0, e, z : z + 1, :]
+                value = weight * lines_ref[i, e, z : z + 1, :]
                 sums[e][z % 2] = value if order == 0 and z < 2 else sums[e][z % 2] + value
     return [a + b for a, b in sums]
 
 
-def back_body(scale, close, cross_ref, index_ref, gram_ref, pull_ref, up_ref, further_ref, fluor_ref, *refs):
+def back_body(scale, cross_ref, index_ref, gram_ref, pull_ref, up_ref, further_ref, fluor_ref, *refs):
     lines, (near_ref, total_ref, gain_ref, shift_ref) = refs[:-4], refs[-4:]
     n_energy, rows, depth, width = fluor_ref.shape
     n_species = shift_ref.shape[0]
-    sums = weigh(gram_ref[...], list(zip(close, lines)), depth, n_energy, width)
+    sums = weigh(gram_ref[...], [(r + 1, ref, 0) for r, ref in enumerate(lines)], depth, n_energy, width)
     back = [sums[e] * scale + pull_ref[e] for e in range(n_energy)]
     gain = [back[e] * jnp.exp2(up_ref[e]) for e in range(n_energy)]
     sigma = selected(cross_ref, index_ref)
@@ -280,7 +286,7 @@
 
 
 def mix_body(cross_ref, index_ref, gain_ref, shift_ref, rest_ref, out_ref):
-    n_energy, rows, depth, width = rest_ref.shape
+    n_energy, rows, _, _ = rest_ref.shape
     n_species = out_ref.shape[0]
     sigma = selected(cross_ref, index_ref)
     mixed = [[sigma[s][e] * gain_ref[e] for e in range(n_energy)] for s in range(n_species)]
@@ -325,7 +331,9 @@
                 copy.start()
 
     start = pl.multiple_of(lax.axis_index(("beam", "slab")) * share, share)
-    sums = weigh(fan_ref[pl.ds(start, share), :], list(enumerate(lines)), depth, n_energy, width)
+    pieces = [(ref, i) for ref in lines for i in range(ref.shape[0])]
+    pieces = [(r, ref, i) for r, (ref, i) in enumerate(pieces)]
+    sums = weigh(fan_ref[pl.ds(start, share), :], pieces, depth, n_energy, width)
     for e in range(n_energy):
         residual_ref[e] = sums[e] * scale - measured_ref[e, pl.ds(start, share), :]
     copy = pltpu.make_async_copy(residual_ref, residual_hbm, residual_sem)
@@ -335,6 +343,19 @@
         for done in copies(chunk):
             done.wait()
     copy.wait()
+
+
+def odd_pairs(n_beam, n_slab):
+    pairs = []
+    for beam in range(n_beam):
+        for slab in range(n_slab):
+            other = slab + 1 if slab % 2 else slab - 1
+            if 0 <= other < n_slab:
+                target = beam * n_slab + other
+            else:
+                target = (beam ^ (n_beam // 2)) * n_slab + slab
+            pairs.append((beam * n_slab + slab, target))
+    return pairs
 
 
 def swap(value, axis, distance):
@@ -371,7 +392,6 @@
     n_early = n_energy // 2
     conc_x, emission, far_local, row_total = call(
         functools.partial(load_body, scale_y, scale_x),
-        "load",
         (VMEM(turned, F32), VMEM((n_early, rows, depth, width), F32), plane, plain(depth, rows)),
         (VMEM,) * 4,
         (HBM,) * 4,
@@ -389,7 +409,6 @@
 
     trans, emit, own_depth = call(
         functools.partial(local_body, scale_x),
-        "local",
         (cube, cube, plain(n_energy, depth, width)),
         (VMEM, VMEM, VMEM),
         (SMEM, SMEM) + (VMEM,) * 3,
@@ -398,52 +417,54 @@
 
     wide = (n_energy, depth, width)
     far_wide, pair = call(
-        functools.partial(line_body, n_det), "line", (plane, plain(2, *wide)), (VMEM,) * 2, (VMEM,) * 3,
+        functools.partial(line_body, n_det), (plane, plain(2, *wide)), (VMEM,) * 2, (VMEM,) * 3,
         cost=(8 * voxels, 0, 1024),
     )(far, emit, own_depth)
 
     fluor, rest = call(
-        ahead_body, "ahead", (cube, cube), (VMEM, VMEM), (VMEM, VMEM, VMEM),
+        ahead_body, (cube, cube), (VMEM, VMEM), (VMEM, VMEM, VMEM),
         cost=(20 * voxels, 0, 1024),
     )(far_wide, trans, emit)
 
-    up = further = own_depth
-    distance = 1
-    while distance < n_beam:
-        other = swap(pair, "beam", distance)
-        kept = 1 if 2 * distance == n_beam else 2
-        if kept == 1:
-            other, fluor, rest = lax.optimization_barrier((other, fluor, rest))
-        pair, up, further = call(
-            functools.partial(merge_body, distance, distance == 1),
-            "merge", (plain(kept, *wide), plain(*wide), plain(*wide)), (VMEM,) * 3, (VMEM,) * 4,
-            cost=(1 << 14, 1 << 12, 1024),
-        )(pair, other, up, further)
-        distance *= 2
-
-    lines = [pair] + [swap(pair, "slab", r) for r in range(1, n_slab)]
-    close = [r for r in range(1, n_slab) if r & (r + 1) == 0]
+    others = [swap(pair, "beam", r) for r in range(1, n_beam)]
+    if others:
+        others[-1], fluor, rest = lax.optimization_barrier((others[-1], fluor, rest))
+    total, up, further = call(
+        merge_body, (plain(1, *wide), plain(*wide), plain(*wide)), (VMEM,) * 3, (VMEM,) * n_beam,
+        cost=(1 << 15, 1 << 13, 1024),
+    )(pair, *others)
+
+    if n_slab == 4 and n_beam > 1:
+        even = swap(total, "slab", 1)
+        odd = lax.ppermute(total, ("beam", "slab"), odd_pairs(n_beam, n_slab))
+        near_lines = [total, even, odd]
+        near_slabs = [0, 1, None]
+        half = jnp.concatenate([total, even], axis=0)
+        lines = [total, even, swap(half, "slab", 2)]
+    else:
+        lines = [total] + [swap(total, "slab", r) for r in range(1, n_slab)]
+        near_slabs = [r for r in range(n_slab) if r & (r + 1) == 0]
+        near_lines = [lines[r] for r in near_slabs]
 
     pixels = fan_offset.shape[0]
     gram, pull, fan_turned = call(
-        functools.partial(fan_body, scale_sum), "fan", (plain(depth, depth * n_slab), plain(*wide), plain(pixels, depth * n_slab)),
+        functools.partial(fan_body, scale_sum, near_slabs), (plain(depth, depth * len(near_slabs)), plain(*wide), plain(pixels, depth * n_slab)),
         (VMEM,) * 3, (VMEM,) * 4, cost=(8 * depth * measured.size, 0, 4 * measured.size),
-    )(fan_offset[None, :], fan_weight.T, measured, pair)
+    )(fan_offset[None, :], fan_weight.T, measured, total)
 
     near, column_total, gain, shift = call(
-        functools.partial(back_body, scale_sum, close),
-        "back",
+        functools.partial(back_body, scale_sum),
         (plane, plain(depth, rows), plain(*wide), plain(n_species, depth, width)),
         (VMEM,) * 4,
-        (SMEM, SMEM) + (VMEM,) * (5 + len(close)),
+        (SMEM, SMEM) + (VMEM,) * (4 + len(near_lines)),
         cost=(10 * voxels, 0, 1024),
-    )(cross, index, gram, pull, up, further, fluor, *(lines[r] for r in close))
+    )(cross, index, gram, pull, up, further, fluor, *near_lines[1:])
 
     nearer = beyond(column_total, "det", True)
 
     scale_line = scale_y * LN2 / scale_x
     mixed = call(
-        mix_body, "mix", (VMEM(turned, F32),), (VMEM,), (SMEM,) * 2 + (VMEM,) * 3,
+        mix_body, (VMEM(turned, F32),), (VMEM,), (SMEM,) * 2 + (VMEM,) * 3,
         cost=(40 * voxels, 0, 1024),
     )(cross, index, gain, shift, rest)[0]
 
@@ -451,7 +472,6 @@
     return tuple(
         call(
             functools.partial(finish_body, scale_sum, scale_line, n_det),
-            "finish",
             (plain(*conc.shape), plain(n_energy, share, width)),
             (HBM, HBM),
             (SMEM,) + (VMEM,) * (5 + len(lines)),

time: 30 us -> 31.9 us (1.063)
  waiting for transfers between devices: 4.9 us -> 6.16 us
  starting transfers between devices: 11.2 us -> 11.8 us
    ppermute x0 -> x1, waiting for transfers between devices: none -> 2.15 us  [shards(): odd = lax.ppermute(total, ('beam', 'slab'), odd_pairs(n_beam, n_slab))]
    ppermute x0 -> x1, starting transfers between devices: none -> 1.21 us  [shards(): odd = lax.ppermute(total, ('beam', 'slab'), odd_pairs(n_beam, n_slab))]
    ppermute x7, waiting for transfers between devices: 4.9 us -> 4 us  [swap(): lax.ppermute(value, axis, [(i, i ^ distance) for i in range(lax.axis_size...]
    ppermute x7, starting transfers between devices: 11.2 us -> 10.6 us  [swap(): lax.ppermute(value, axis, [(i, i ^ distance) for i in range(lax.axis_size...]
    pallas_call x10 -> x9, Pallas kernels: 13 us -> 13 us  [the longest x1 3.01 us: shards(): call(functools.partial(load_body, scale_y, scale_x), (VMEM(turned, F32),...]
  transfers between devices with their start and end apart: 7 -> 8, of which waited for: 5 -> 4; matrix products, arithmetic and copies ran while one was open for 0% -> 0% of each run, Pallas kernels for 22% -> 21%
where the time goes in v6:
time: 31.9 us; the launch traced here: 31.7 us
  Pallas kernels  13 us (41%)
  starting transfers between devices  11.8 us (37%)
  waiting for transfers between devices  6.16 us (19%)
  between operations  0.72 us (2%)
    ppermute x7, starting transfers between devices, swap(): lax.ppermute(value, axis, [(i, i ^ distance) for i in range(lax.axis_size...  10.6 us
    ppermute x7, waiting for transfers between devices, swap(): lax.ppermute(value, axis, [(i, i ^ distance) for i in range(lax.axis_size...  4 us
    pallas_call x1, Pallas kernels, shards(): call(functools.partial(load_body, scale_y, scale_x), (VMEM(turned, F32),...  3.01 us
    pallas_call x1, Pallas kernels, shards(): call(functools.partial(finish_body, scale_sum, scale_line, n_det), (plain...  2.81 us
    ppermute x1, waiting for transfers between devices, shards(): odd = lax.ppermute(total, ('beam', 'slab'), odd_pairs(n_beam, n_slab))  2.15 us
    pallas_call x1, Pallas kernels, shards(): call(functools.partial(local_body, scale_x), (cube, cube, plain(n_energy,...  1.8 us
    pallas_call x1, Pallas kernels, shards(): call(mix_body, (VMEM(turned, F32),), (VMEM,), (SMEM,) * 2 + (VMEM,) * 3,...  1.75 us
    pallas_call x1, Pallas kernels, shards(): call(ahead_body, (cube, cube), (VMEM, VMEM), (VMEM, VMEM, VMEM), cost=(20...  1.51 us
  transfers between devices with their start and end apart: 8, of which 4 were waited for; matrix products, arithmetic and copies ran while one was open for 0% of the time, Pallas kernels for 21%

profile of v6, /device:TPU:0, one launch (start us, length us, event | category | flops | bytes accessed | tf_op | source)
XLA Modules:
  0.0 31.7 jit_solution(993442800898547814)
XLA Ops:
  0.6 0.0 copy-start.2
  0.6 0.0 copy-start.1
  0.6 3.0 %shard_map.86 = (f32[4,256,8,128]{3,2,1,0:T(8,128)S(1)}, f32[2,256,8,128]{3,2,1,0:T(8,128)S(1)}, f32[256,8,128]{2,1,0:T(8,128)S(1)}, f32[8,256]{1,0:T(8,128)S(1)}) custom-call(f32[4]{0:T(128)} %line_ref.1, f32[4,16]{1,0:T(4,128)} %cross_ref.5, s32[4]{0:T(128)} %index_ref.5, f32[4,8,256,128]{3,2,1,0:T(8,128)} %conc_hbm.1), custom_call_target="tpu_custom_call" | custom-call | flops 10485760 | bytes 4194304 | tf_op jit(solution)/shard_map/pallas_call | solution.py:393
  3.7 3.1 %collective-permute-start = (f32[8,256]{1,0:T(8,128)S(1)}, f32[8,256]{1,0:T(8,128)S(1)}, u32[]{:S(2)}, u32[]{:S(2)}) collective-permute-start(f32[8,256]{1,0:T(8,128)S(1)} %get-tuple-element.26), channel_id=1, source_target_pairs={{0,4},{4,0},{1,5},{5,1},{2,6},{6,2},{3,7},{7,3},{8,12},{12,8},{9,1... | collective-permute-start | bytes 24584 | tf_op jit(solution)/shard_map/ppermute | solution.py:362
  6.7 0.0 copy-done.2
  6.7 0.0 copy-done.1
  6.7 1.8 %shard_map.87 = (f32[4,256,8,128]{3,2,1,0:T(8,128)S(1)}, f32[4,256,8,128]{3,2,1,0:T(8,128)S(1)}, f32[4,8,128]{2,1,0:T(8,128)S(1)}) custom-call(f32[4,16]{1,0:T(4,128)S(1)} %copy-done.1, s32[4]{0:T(128)S(1)} %copy-done.2, f32[4,256,8,128]{3,2,1,0:T(8,128)S(1)} %get-tuple-element.27.conc_ref, f32[2,256,8,128]{3,2,1,0:T(8,128)S(1)} %get-tuple-element.28.early_ref, ...), custom_call_target="tpu_custom_call" | custom-call | flops 5242880 | bytes 1024 | tf_op jit(solution)/shard_map/pallas_call | solution.py:410
  8.5 0.0 collective-permute-done.far_ref
  8.5 0.6 %shard_map.88 = (f32[256,8,128]{2,1,0:T(8,128)S(1)}, f32[2,4,8,128]{3,2,1,0:T(8,128)S(1)}) custom-call(f32[8,256]{1,0:T(8,128)S(1)} %collective-permute-done.far_ref, f32[4,256,8,128]{3,2,1,0:T(8,128)S(1)} %get-tuple-element.30.emit_ref, f32[4,8,128]{2,1,0:T(8,128)S(1)} %get-tuple-element.31.depth_ref), custom_call_target="tpu_custom_call" | custom-call | flops 2097152 | bytes 1024 | tf_op jit(solution)/shard_map/pallas_call | solution.py:419
  9.1 0.7 %collective-permute-start.3 = (f32[2,4,8,128]{3,2,1,0:T(8,128)S(1)}, f32[2,4,8,128]{3,2,1,0:T(8,128)S(1)}, u32[]{:S(2)}, u32[]{:S(2)}) collective-permute-start(f32[2,4,8,128]{3,2,1,0:T(8,128)S(1)} %get-tuple-element.32.refs_0_), channel_id=1, source_target_pairs={{0,24},{8,16},{16,8},{24,0},{1,25},{9,17},{17,9},{25,1},{2,26},{10... | collective-permute-start | bytes 98312 | tf_op jit(solution)/shard_map/ppermute | solution.py:362
  9.8 1.2 %collective-permute-start.2 = (f32[2,4,8,128]{3,2,1,0:T(8,128)S(1)}, f32[2,4,8,128]{3,2,1,0:T(8,128)S(1)}, u32[]{:S(2)}, u32[]{:S(2)}) collective-permute-start(f32[2,4,8,128]{3,2,1,0:T(8,128)S(1)} %get-tuple-element.32.refs_0_), channel_id=1, source_target_pairs={{0,16},{8,24},{16,0},{24,8},{1,17},{9,25},{17,1},{25,9},{2,18},{10... | collective-permute-start | bytes 98312 | tf_op jit(solution)/shard_map/ppermute | solution.py:362
  11.1 0.0 collective-permute-start.1
  11.1 0.0 copy-start
  11.1 0.0 copy-start.3
  11.1 0.0 copy-start.5
  11.1 1.5 %shard_map.89 = (f32[4,256,8,128]{3,2,1,0:T(8,128)S(1)}, f32[4,256,8,128]{3,2,1,0:T(8,128)S(1)}) custom-call(f32[256,8,128]{2,1,0:T(8,128)S(1)} %get-tuple-element.33.far_ref, f32[4,256,8,128]{3,2,1,0:T(8,128)S(1)} %get-tuple-element.34.trans_ref, f32[4,256,8,128]{3,2,1,0:T(8,128)S(1)} %get-tuple-element.30.emit_ref), custom_call_target="tpu_custom_call" | custom-call | flops 5242880 | bytes 1024 | tf_op jit(solution)/shard_map/pallas_call | solution.py:424
  12.6 0.0 collective-permute-done.3.refs_3_
  12.6 1.2 %collective-permute-done.2.refs_2_ = f32[2,4,8,128]{3,2,1,0:T(8,128)S(1)} collective-permute-done((f32[2,4,8,128]{3,2,1,0:T(8,128)S(1)}, f32[2,4,8,128]{3,2,1,0:T(8,128)S(1)}, u32[]{:S(2)}, u32[]{:S(2)}) %collective-permute-start.2) | collective-permute-done | bytes 32800 | tf_op jit(solution)/shard_map/ppermute | solution.py:362
  13.8 0.0 collective-permute-done.1.refs_1_
  13.8 1.6 %collective-permute-start.4 = (f32[1,4,8,128]{3,2,1,0:T(8,128)S(1)}, f32[1,4,8,128]{3,2,1,0:T(8,128)S(1)}, u32[]{:S(2)}, u32[]{:S(2)}) collective-permute-start(f32[1,4,8,128]{3,2,1,0:T(8,128)S(1)} %get-tuple-element.38.own_ref.refs_0_), channel_id=1, source_target_pairs={{0,1},{1,0},{2,3},{3,2},{4,5},{5,4},{6,7},{7,6},{8,9},{9,8},{10,11... | collective-permute-start | bytes 49160 | tf_op jit(solution)/shard_map/ppermute | solution.py:362
  15.5 2.2 %collective-permute-done.4.refs_0_.refs_1_ = f32[1,4,8,128]{3,2,1,0:T(8,128)S(1)} collective-permute-done((f32[1,4,8,128]{3,2,1,0:T(8,128)S(1)}, f32[1,4,8,128]{3,2,1,0:T(8,128)S(1)}, u32[]{:S(2)}, u32[]{:S(2)}) %collective-permute-start.4) | collective-permute-done | bytes 16416 | tf_op jit(solution)/shard_map/ppermute | solution.py:362
  17.6 2.6 %collective-permute-start.7 = (f32[2,4,8,128]{3,2,1,0:T(8,128)S(1)}, f32[2,4,8,128]{3,2,1,0:T(8,128)S(1)}, u32[]{:S(2)}, u32[]{:S(2)}) collective-permute-start(f32[2,4,8,128]{3,2,1,0:T(8,128)S(1)} %pad_maximum_fusion), channel_id=1, source_target_pairs={{0,2},{1,3},{2,0},{3,1},{4,6},{5,7},{6,4},{7,5},{8,10},{9,11},{10,... | collective-permute-start | bytes 98312 | tf_op jit(solution)/shard_map/ppermute | solution.py:362
  20.2 1.2 %collective-permute-start.5 = (f32[1,4,8,128]{3,2,1,0:T(8,128)S(1)}, f32[1,4,8,128]{3,2,1,0:T(8,128)S(1)}, u32[]{:S(2)}, u32[]{:S(2)}) collective-permute-start(f32[1,4,8,128]{3,2,1,0:T(8,128)S(1)} %get-tuple-element.38.own_ref.refs_0_), channel_id=1, source_target_pairs={{0,16},{1,2},{2,1},{3,19},{8,24},{9,10},{10,9},{11,27},{16,0},{17,... | collective-permute-start | bytes 49160 | tf_op jit(solution)/shard_map/ppermute | solution.py:439
  21.5 0.0 copy-done
  21.5 0.0 copy-done.3
  21.5 0.0 copy-done.5
  21.5 0.4 %shard_map.91 = (f32[8,24]{1,0:T(8,128)S(1)}, f32[4,8,128]{2,1,0:T(8,128)S(1)}, f32[256,32]{1,0:T(8,128)S(1)}) custom-call(s32[1,256]{1,0:T(1,128)S(1)} %bitcast.3, s32[4,256]{1,0:T(4,128)S(1)} %bitcast.2, f32[4,256,128]{2,1,0:T(8,128)S(1)} %copy-done, f32[1,4,8,128]{3,2,1,0:T(8,128)S(1)} %get-tuple-element.38.own_ref.refs_0_), custom_call_target="tpu_custom_call" | custom-call | flops 8388608 | bytes 524288 | tf_op jit(solution)/shard_map/pallas_call | solution.py:450
  21.8 2.2 %collective-permute-done.5.refs_1_ = f32[1,4,8,128]{3,2,1,0:T(8,128)S(1)} collective-permute-done((f32[1,4,8,128]{3,2,1,0:T(8,128)S(1)}, f32[1,4,8,128]{3,2,1,0:T(8,128)S(1)}, u32[]{:S(2)}, u32[]{:S(2)}) %collective-permute-start.5) | collective-permute-done | bytes 16416 | tf_op jit(solution)/shard_map/ppermute | solution.py:439
  24.0 1.2 %shard_map.92 = (f32[256,8,128]{2,1,0:T(8,128)S(1)}, f32[8,256]{1,0:T(8,128)S(1)}, f32[4,8,128]{2,1,0:T(8,128)S(1)}, f32[4,8,128]{2,1,0:T(8,128)S(1)}) custom-call(f32[4,16]{1,0:T(4,128)S(1)} %copy-done.1, s32[4]{0:T(128)S(1)} %copy-done.2, f32[8,24]{1,0:T(8,128)S(1)} %get-tuple-element.39.gram_ref, f32[4,8,128]{2,1,0:T(8,128)S(1)} %get-tuple-element.40.pull_ref, ...), custom_call_target="tpu_custom_call" | custom-call | flops 2621440 | bytes 1024 | tf_op jit(solution)/shard_map/pallas_call | solution.py:455
  25.2 1.3 %collective-permute-start.6 = (f32[8,256]{1,0:T(8,128)S(1)}, f32[8,256]{1,0:T(8,128)S(1)}, u32[]{:S(2)}, u32[]{:S(2)}) collective-permute-start(f32[8,256]{1,0:T(8,128)S(1)} %get-tuple-element.44), channel_id=1, source_target_pairs={{0,4},{4,0},{1,5},{5,1},{2,6},{6,2},{3,7},{7,3},{8,12},{12,8},{9,1... | collective-permute-start | bytes 24584 | tf_op jit(solution)/shard_map/ppermute | solution.py:362
  26.5 0.0 copy-start.4
  26.5 1.8 %shard_map.93.mix_ref = f32[4,256,8,128]{3,2,1,0:T(8,128)S(1)} custom-call(f32[4,16]{1,0:T(4,128)S(1)} %copy-done.1, s32[4]{0:T(128)S(1)} %copy-done.2, f32[4,8,128]{2,1,0:T(8,128)S(1)} %get-tuple-element.46.gain_ref, f32[4,8,128]{2,1,0:T(8,128)S(1)} %get-tuple-element.47.shift_ref, f32[4,256,8,128]{3,2,1,0:T(8,128)S(1)} %get-tuple-element.48.rest_ref), custom_call_target="tpu_custom_call" | custom-call | flops 10485760 | bytes 1024 | tf_op jit(solution)/shard_map/pallas_call | solution.py:466
  28.3 0.6 %collective-permute-done.6.nearer_ref = f32[8,256]{1,0:T(8,128)S(1)} collective-permute-done((f32[8,256]{1,0:T(8,128)S(1)}, f32[8,256]{1,0:T(8,128)S(1)}, u32[]{:S(2)}, u32[]{:S(2)}) %collective-permute-start.6) | collective-permute-done | bytes 8224 | tf_op jit(solution)/shard_map/ppermute | solution.py:362
  28.9 0.0 collective-permute-done.7.refs_2_
  28.9 0.0 copy-done.4
  28.9 2.8 %shard_map.94 = (f32[4,8,256,128]{3,2,1,0:T(8,128)}, f32[4,16,128]{2,1,0:T(8,128)}) custom-call(f32[4]{0:T(128)S(1)} %copy-done.4, f32[8,256]{1,0:T(8,128)S(1)} %collective-permute-done.6.nearer_ref, f32[256,8,128]{2,1,0:T(8,128)S(1)} %get-tuple-element.45.near_ref, f32[4,256,8,128]{3,2,1,0:T(8,128)S(1)} %shard_map.93.mix_ref, ...), custom_call_target="tpu_custom_call" | custom-call | flops 2621440 | bytes 4194304 | tf_op jit(solution)/shard_map/pallas_call | solution.py:473
  (2 shorter events, 0.0 us)
Async XLA Ops:
  0.6 6.1 %copy-start.2 = (s32[4]{0:T(128)S(1)}, s32[4]{0:T(128)}, u32[]{:S(2)}) copy-start(s32[4]{0:T(128)} %index_ref.5) | copy-start | bytes 52
  0.6 6.1 %copy-start.1 = (f32[4,16]{1,0:T(4,128)S(1)}, f32[4,16]{1,0:T(4,128)}, u32[]{:S(2)}) copy-start(f32[4,16]{1,0:T(4,128)} %cross_ref.5) | copy-start | bytes 772
  3.7 4.9 %collective-permute-start = (f32[8,256]{1,0:T(8,128)S(1)}, f32[8,256]{1,0:T(8,128)S(1)}, u32[]{:S(2)}, u32[]{:S(2)}) collective-permute-start(f32[8,256]{1,0:T(8,128)S(1)} %get-tuple-element.26), channel_id=1, source_target_pairs={{0,4},{4,0},{1,5},{5,1},{2,6},{6,2},{3,7},{7,3},{8,12},{12,8},{9,1... | collective-permute-start | bytes 24584 | tf_op jit(solution)/shard_map/ppermute | solution.py:362
  9.1 3.5 %collective-permute-start.3 = (f32[2,4,8,128]{3,2,1,0:T(8,128)S(1)}, f32[2,4,8,128]{3,2,1,0:T(8,128)S(1)}, u32[]{:S(2)}, u32[]{:S(2)}) collective-permute-start(f32[2,4,8,128]{3,2,1,0:T(8,128)S(1)} %get-tuple-element.32.refs_0_), channel_id=1, source_target_pairs={{0,24},{8,16},{16,8},{24,0},{1,25},{9,17},{17,9},{25,1},{2,26},{10... | collective-permute-start | bytes 98312 | tf_op jit(solution)/shard_map/ppermute | solution.py:362
  9.8 4.0 %collective-permute-start.2 = (f32[2,4,8,128]{3,2,1,0:T(8,128)S(1)}, f32[2,4,8,128]{3,2,1,0:T(8,128)S(1)}, u32[]{:S(2)}, u32[]{:S(2)}) collective-permute-start(f32[2,4,8,128]{3,2,1,0:T(8,128)S(1)} %get-tuple-element.32.refs_0_), channel_id=1, source_target_pairs={{0,16},{8,24},{16,0},{24,8},{1,17},{9,25},{17,1},{25,9},{2,18},{10... | collective-permute-start | bytes 98312 | tf_op jit(solution)/shard_map/ppermute | solution.py:362
  11.1 2.8 %collective-permute-start.1 = (f32[2,4,8,128]{3,2,1,0:T(8,128)S(1)}, f32[2,4,8,128]{3,2,1,0:T(8,128)S(1)}, u32[]{:S(2)}, u32[]{:S(2)}) collective-permute-start(f32[2,4,8,128]{3,2,1,0:T(8,128)S(1)} %get-tuple-element.32.refs_0_), channel_id=1, source_target_pairs={{0,8},{8,0},{16,24},{24,16},{1,9},{9,1},{17,25},{25,17},{2,10},{10... | collective-permute-start | bytes 98312 | tf_op jit(solution)/shard_map/ppermute | solution.py:362
  11.1 10.4 %copy-start = (f32[4,256,128]{2,1,0:T(8,128)S(1)}, f32[4,256,128]{2,1,0:T(8,128)}, u32[]{:S(2)}) copy-start(f32[4,256,128]{2,1,0:T(8,128)} %measured_ref.3) | copy-start | bytes 1572868
  11.1 10.4 %copy-start.3 = (s32[256,4]{0,1:T(4,128)S(1)}, s32[256,4]{0,1:T(4,128)}, u32[]{:S(2)}) copy-start(s32[256,4]{0,1:T(4,128)} %param.12) | copy-start | bytes 12292
  11.1 10.4 %copy-start.5 = (s32[256]{0:T(256)S(1)}, s32[256]{0:T(256)}, u32[]{:S(2)}) copy-start(s32[256]{0:T(256)} %param.11) | copy-start | bytes 3076
  13.8 3.8 %collective-permute-start.4 = (f32[1,4,8,128]{3,2,1,0:T(8,128)S(1)}, f32[1,4,8,128]{3,2,1,0:T(8,128)S(1)}, u32[]{:S(2)}, u32[]{:S(2)}) collective-permute-start(f32[1,4,8,128]{3,2,1,0:T(8,128)S(1)} %get-tuple-element.38.own_ref.refs_0_), channel_id=1, source_target_pairs={{0,1},{1,0},{2,3},{3,2},{4,5},{5,4},{6,7},{7,6},{8,9},{9,8},{10,11... | collective-permute-start | bytes 49160 | tf_op jit(solution)/shard_map/ppermute | solution.py:362
  17.6 11.3 %collective-permute-start.7 = (f32[2,4,8,128]{3,2,1,0:T(8,128)S(1)}, f32[2,4,8,128]{3,2,1,0:T(8,128)S(1)}, u32[]{:S(2)}, u32[]{:S(2)}) collective-permute-start(f32[2,4,8,128]{3,2,1,0:T(8,128)S(1)} %pad_maximum_fusion), channel_id=1, source_target_pairs={{0,2},{1,3},{2,0},{3,1},{4,6},{5,7},{6,4},{7,5},{8,10},{9,11},{10,... | collective-permute-start | bytes 98312 | tf_op jit(solution)/shard_map/ppermute | solution.py:362
  20.2 3.7 %collective-permute-start.5 = (f32[1,4,8,128]{3,2,1,0:T(8,128)S(1)}, f32[1,4,8,128]{3,2,1,0:T(8,128)S(1)}, u32[]{:S(2)}, u32[]{:S(2)}) collective-permute-start(f32[1,4,8,128]{3,2,1,0:T(8,128)S(1)} %get-tuple-element.38.own_ref.refs_0_), channel_id=1, source_target_pairs={{0,16},{1,2},{2,1},{3,19},{8,24},{9,10},{10,9},{11,27},{16,0},{17,... | collective-permute-start | bytes 49160 | tf_op jit(solution)/shard_map/ppermute | solution.py:439
  25.2 3.7 %collective-permute-start.6 = (f32[8,256]{1,0:T(8,128)S(1)}, f32[8,256]{1,0:T(8,128)S(1)}, u32[]{:S(2)}, u32[]{:S(2)}) collective-permute-start(f32[8,256]{1,0:T(8,128)S(1)} %get-tuple-element.44), channel_id=1, source_target_pairs={{0,4},{4,0},{1,5},{5,1},{2,6},{6,2},{3,7},{7,3},{8,12},{12,8},{9,1... | collective-permute-start | bytes 24584 | tf_op jit(solution)/shard_map/ppermute | solution.py:362
  26.5 2.4 %copy-start.4 = (f32[4]{0:T(128)S(1)}, f32[4]{0:T(128)}, u32[]{:S(2)}) copy-start(f32[4]{0:T(128)} %line_ref.1) | copy-start | bytes 52

commit v7 on v6

--- a/solution.py
+++ b/solution.py
@@ -55,6 +55,11 @@
     return [[cross_ref[s, columns[e]] for e in range(n_energy)] for s in range(cross_ref.shape[0])]
 
 
+def planes(plane_ref, n_species, n_energy):
+    cross = [[plane_ref[s * n_energy + e] for e in range(n_energy)] for s in range(n_species)]
+    return cross, [plane_ref[n_species * n_energy + s] for s in range(n_species)]
+
+
 def weighted(weights, values):
     total = weights[0] * values[0]
     for weight, value in zip(weights[1:], values[1:]):
@@ -63,7 +68,7 @@
 
 
 def load_body(
-    scale, scale_x, line_hbm, cross_hbm, index_hbm, conc_hbm, conc_ref, emit_ref, beyond_ref, total_ref,
+    scale, scale_x, line_hbm, cross_hbm, index_hbm, conc_hbm, conc_ref, emit_ref, beyond_ref, total_ref, plane_ref,
     line_ref, cross_ref, index_ref, small_sems, sems,
 ):
     n_species, depth, rows, width = conc_hbm.shape
@@ -92,7 +97,11 @@
     for copy in small:
         copy.wait()
     line = [line_ref[s] * scale for s in range(n_species)]
-    sigma = [[v * scale_x for v in row] for row in selected(cross_ref, index_ref)]
+    sigma = selected(cross_ref, index_ref)
+    scalars = [v for row in sigma for v in row] + [line_ref[s] for s in range(n_species)]
+    for i, value in enumerate(scalars):
+        plane_ref[i] = jnp.full((depth, width), value)
+    sigma = [[v * scale_x for v in row] for row in sigma]
     for part in range(rows // LANES):
         total = jnp.zeros((depth, LANES), F32)
         for piece in range(LANES // CHUNK):
@@ -114,10 +123,10 @@
         total_ref[:, part * LANES : (part + 1) * LANES] = total
 
 
-def local_body(scale, cross_ref, index_ref, conc_ref, early_ref, beyond_ref, trans_ref, emit_ref, depth_ref):
+def local_body(scale, plane_ref, conc_ref, early_ref, beyond_ref, trans_ref, emit_ref, depth_ref):
     n_energy, rows, depth, width = trans_ref.shape
     n_species, n_early = conc_ref.shape[0], early_ref.shape[0]
-    sigma = [[v * scale for v in row] for row in selected(cross_ref, index_ref)]
+    sigma = [[v * scale for v in row] for row in planes(plane_ref, n_species, n_energy)[0]]
 
     def step(block, path):
         path = list(path)
@@ -257,14 +266,14 @@
     return [a + b for a, b in sums]
 
 
-def back_body(scale, cross_ref, index_ref, gram_ref, pull_ref, up_ref, further_ref, fluor_ref, *refs):
+def back_body(scale, plane_ref, gram_ref, pull_ref, up_ref, further_ref, fluor_ref, *refs):
     lines, (near_ref, total_ref, gain_ref, shift_ref) = refs[:-4], refs[-4:]
     n_energy, rows, depth, width = fluor_ref.shape
     n_species = shift_ref.shape[0]
     sums = weigh(gram_ref[...], [(r + 1, ref, 0) for r, ref in enumerate(lines)], depth, n_energy, width)
     back = [sums[e] * scale + pull_ref[e] for e in range(n_energy)]
     gain = [back[e] * jnp.exp2(up_ref[e]) for e in range(n_energy)]
-    sigma = selected(cross_ref, index_ref)
+    sigma, _ = planes(plane_ref, n_species, n_energy)
     pushed = [LN2 * back[e] * further_ref[e] for e in range(n_energy)]
     for e in range(n_energy):
         gain_ref[e] = gain[e]
@@ -285,10 +294,10 @@
         total_ref[:, part * LANES : (part + 1) * LANES] = total
 
 
-def mix_body(cross_ref, index_ref, gain_ref, shift_ref, rest_ref, out_ref):
+def mix_body(plane_ref, gain_ref, shift_ref, rest_ref, out_ref):
     n_energy, rows, _, _ = rest_ref.shape
     n_species = out_ref.shape[0]
-    sigma = selected(cross_ref, index_ref)
+    sigma, _ = planes(plane_ref, n_species, n_energy)
     mixed = [[sigma[s][e] * gain_ref[e] for e in range(n_energy)] for s in range(n_species)]
     shift = [shift_ref[s] for s in range(n_species)]
 
@@ -304,12 +313,12 @@
 
 
 def finish_body(
-    scale, scale_line, count, line_ref, nearer_ref, near_ref, mix_ref, fan_ref, measured_ref, *refs
+    scale, scale_line, count, plane_ref, nearer_ref, near_ref, mix_ref, fan_ref, measured_ref, *refs
 ):
     lines, (grad_hbm, residual_hbm, grad_ref, residual_ref, sems, residual_sem) = refs[:-6], refs[-6:]
     n_species, rows, depth, width = mix_ref.shape
     n_energy, share, _ = residual_ref.shape
-    line = [line_ref[s] * scale_line for s in range(n_species)]
+    line = [v * scale_line for v in planes(plane_ref, n_species, n_energy)[1]]
     keep = jnp.where(reached("det", count, True), 1.0, 0.0)
 
     ends = [8, 16] + list(range(CHUNK, rows + 1, CHUNK))
@@ -390,10 +399,11 @@
     plane = VMEM((rows, depth, width), F32)
 
     n_early = n_energy // 2
-    conc_x, emission, far_local, row_total = call(
+    conc_x, emission, far_local, row_total, fixed = call(
         functools.partial(load_body, scale_y, scale_x),
-        (VMEM(turned, F32), VMEM((n_early, rows, depth, width), F32), plane, plain(depth, rows)),
-        (VMEM,) * 4,
+        (VMEM(turned, F32), VMEM((n_early, rows, depth, width), F32), plane, plain(depth, rows),
+         VMEM((n_species * n_energy + n_species, depth, width), F32)),
+        (VMEM,) * 5,
         (HBM,) * 4,
         [
             SMEM(line.shape, F32),
@@ -411,9 +421,9 @@
         functools.partial(local_body, scale_x),
         (cube, cube, plain(n_energy, depth, width)),
         (VMEM, VMEM, VMEM),
-        (SMEM, SMEM) + (VMEM,) * 3,
+        (VMEM,) * 4,
         cost=(20 * voxels, 4 * voxels, 1024),
-    )(cross, index, conc_x, emission, far_local)
+    )(fixed, conc_x, emission, far_local)
 
     wide = (n_energy, depth, width)
     far_wide, pair = call(
@@ -456,17 +466,17 @@
         functools.partial(back_body, scale_sum),
         (plane, plain(depth, rows), plain(*wide), plain(n_species, depth, width)),
         (VMEM,) * 4,
-        (SMEM, SMEM) + (VMEM,) * (4 + len(near_lines)),
+        (VMEM,) * (5 + len(near_lines)),
         cost=(10 * voxels, 0, 1024),
-    )(cross, index, gram, pull, up, further, fluor, *near_lines[1:])
+    )(fixed, gram, pull, up, further, fluor, *near_lines[1:])
 
     nearer = beyond(column_total, "det", True)
 
     scale_line = scale_y * LN2 / scale_x
     mixed = call(
-        mix_body, (VMEM(turned, F32),), (VMEM,), (SMEM,) * 2 + (VMEM,) * 3,
+        mix_body, (VMEM(turned, F32),), (VMEM,), (VMEM,) * 4,
         cost=(40 * voxels, 0, 1024),
-    )(cross, index, gain, shift, rest)[0]
+    )(fixed, gain, shift, rest)[0]
 
     share = pixels // (n_beam * n_slab)
     return tuple(
@@ -474,7 +484,7 @@
             functools.partial(finish_body, scale_sum, scale_line, n_det),
             (plain(*conc.shape), plain(n_energy, share, width)),
             (HBM, HBM),
-            (SMEM,) + (VMEM,) * (5 + len(lines)),
+            (VMEM,) * (6 + len(lines)),
             [
                 VMEM(turned, F32),
                 VMEM((n_energy, share, width), F32),
@@ -483,7 +493,7 @@
             ],
             limit=16,
             cost=(10 * voxels, 0, 16 * voxels),
-        )(line, nearer, near, mixed, fan_turned, measured, *lines)
+        )(fixed, nearer, near, mixed, fan_turned, measured, *lines)
     )
 
 

time: 31.9 us -> 30.5 us (0.956)
  Pallas kernels: 13 us -> 10.7 us
  starting transfers between devices: 11.8 us -> 13.2 us
  waiting for transfers between devices: 6.16 us -> 5.75 us
    ppermute x7, starting transfers between devices: 10.6 us -> 11.7 us  [swap(): lax.ppermute(value, axis, [(i, i ^ distance) for i in range(lax.axis_size...]
    pallas_call x1, Pallas kernels: 1.8 us -> 1.18 us  [shards(): call(functools.partial(local_body, scale_x), (cube, cube, plain(n_energy,...]
    pallas_call x1, Pallas kernels: 1.75 us -> 1.16 us  [shards(): call(mix_body, (VMEM(turned, F32),), (VMEM,), (VMEM,) * 4, cost=(40 * vox...]
    pallas_call x1, Pallas kernels: 1.21 us -> 0.64 us  [shards(): call(functools.partial(back_body, scale_sum), (plane, plain(depth, rows),...]
    pallas_call x1, Pallas kernels: 2.81 us -> 2.28 us  [shards(): call(functools.partial(finish_body, scale_sum, scale_line, n_det), (plain...]
  transfers between devices with their start and end apart: 8 -> 8, of which waited for: 4 -> 5; matrix products, arithmetic and copies ran while one was open for 0% -> 0% of each run, Pallas kernels for 21% -> 16%
where the time goes in v7:
time: 30.5 us; the launch traced here: 30.3 us
  starting transfers between devices  13.2 us (43%)
  Pallas kernels  10.7 us (35%)
  waiting for transfers between devices  5.75 us (19%)
  between operations  0.7 us (2%)
    ppermute x7, starting transfers between devices, swap(): lax.ppermute(value, axis, [(i, i ^ distance) for i in range(lax.axis_size...  11.7 us
    ppermute x7, waiting for transfers between devices, swap(): lax.ppermute(value, axis, [(i, i ^ distance) for i in range(lax.axis_size...  3.87 us
    pallas_call x1, Pallas kernels, shards(): call(functools.partial(load_body, scale_y, scale_x), (VMEM(turned, F32),...  3 us
    pallas_call x1, Pallas kernels, shards(): call(functools.partial(finish_body, scale_sum, scale_line, n_det), (plain...  2.28 us
    ppermute x1, waiting for transfers between devices, shards(): odd = lax.ppermute(total, ('beam', 'slab'), odd_pairs(n_beam, n_slab))  1.87 us
    pallas_call x1, Pallas kernels, shards(): call(ahead_body, (cube, cube), (VMEM, VMEM), (VMEM, VMEM, VMEM), cost=(20...  1.51 us
    ppermute x1, starting transfers between devices, shards(): odd = lax.ppermute(total, ('beam', 'slab'), odd_pairs(n_beam, n_slab))  1.49 us
    pallas_call x1, Pallas kernels, shards(): call(functools.partial(local_body, scale_x), (cube, cube, plain(n_energy,...  1.18 us
  transfers between devices with their start and end apart: 8, of which 5 were waited for; matrix products, arithmetic and copies ran while one was open for 0% of the time, Pallas kernels for 16%

profile of v7, /device:TPU:0, one launch (start us, length us, event | category | flops | bytes accessed | tf_op | source)
XLA Modules:
  0.0 30.3 jit_solution(2555319889570032932)
XLA Ops:
  0.6 3.0 %shard_map.86 = (f32[4,256,8,128]{3,2,1,0:T(8,128)S(1)}, f32[2,256,8,128]{3,2,1,0:T(8,128)S(1)}, f32[256,8,128]{2,1,0:T(8,128)S(1)}, f32[8,256]{1,0:T(8,128)S(1)}, f32[20,8,128]{2,1,0:T(8,128)S(1)}) custom-call(f32[4]{0:T(128)} %line_hbm.1, f32[4,16]{1,0:T(4,128)} %cross_hbm.1, s32[4]{0:T(128)} %index_hbm.1, f32[4,8,256,128]{3,2,1,0:T(8,128)} %conc_hbm.1), custom_call_target="tpu_custom_call" | custom-call | flops 10485760 | bytes 4194304 | tf_op jit(solution)/shard_map/pallas_call | solution.py:402
  3.6 3.1 %collective-permute-start = (f32[8,256]{1,0:T(8,128)S(1)}, f32[8,256]{1,0:T(8,128)S(1)}, u32[]{:S(2)}, u32[]{:S(2)}) collective-permute-start(f32[8,256]{1,0:T(8,128)S(1)} %get-tuple-element.28), channel_id=1, source_target_pairs={{0,4},{4,0},{1,5},{5,1},{2,6},{6,2},{3,7},{7,3},{8,12},{12,8},{9,1... | collective-permute-start | bytes 24584 | tf_op jit(solution)/shard_map/ppermute | solution.py:371
  6.7 1.2 %shard_map.87 = (f32[4,256,8,128]{3,2,1,0:T(8,128)S(1)}, f32[4,256,8,128]{3,2,1,0:T(8,128)S(1)}, f32[4,8,128]{2,1,0:T(8,128)S(1)}) custom-call(f32[20,8,128]{2,1,0:T(8,128)S(1)} %get-tuple-element.27.plane_ref, f32[4,256,8,128]{3,2,1,0:T(8,128)S(1)} %get-tuple-element.29.conc_ref, f32[2,256,8,128]{3,2,1,0:T(8,128)S(1)} %get-tuple-element.30.early_ref, ...), custom_call_target="tpu_custom_call" | custom-call | flops 5242880 | bytes 1024 | tf_op jit(solution)/shard_map/pallas_call | solution.py:420
  7.9 0.4 %collective-permute-done.far_ref = f32[8,256]{1,0:T(8,128)S(1)} collective-permute-done((f32[8,256]{1,0:T(8,128)S(1)}, f32[8,256]{1,0:T(8,128)S(1)}, u32[]{:S(2)}, u32[]{:S(2)}) %collective-permute-start) | collective-permute-done | bytes 8224 | tf_op jit(solution)/shard_map/ppermute | solution.py:371
  8.3 0.6 %shard_map.88 = (f32[256,8,128]{2,1,0:T(8,128)S(1)}, f32[2,4,8,128]{3,2,1,0:T(8,128)S(1)}) custom-call(f32[8,256]{1,0:T(8,128)S(1)} %collective-permute-done.far_ref, f32[4,256,8,128]{3,2,1,0:T(8,128)S(1)} %get-tuple-element.32.emit_ref, f32[4,8,128]{2,1,0:T(8,128)S(1)} %get-tuple-element.33.depth_ref), custom_call_target="tpu_custom_call" | custom-call | flops 2097152 | bytes 1024 | tf_op jit(solution)/shard_map/pallas_call | solution.py:429
  8.9 0.3 %collective-permute-start.3 = (f32[2,4,8,128]{3,2,1,0:T(8,128)S(1)}, f32[2,4,8,128]{3,2,1,0:T(8,128)S(1)}, u32[]{:S(2)}, u32[]{:S(2)}) collective-permute-start(f32[2,4,8,128]{3,2,1,0:T(8,128)S(1)} %get-tuple-element.34.refs_0_), channel_id=1, source_target_pairs={{0,24},{8,16},{16,8},{24,0},{1,25},{9,17},{17,9},{25,1},{2,26},{10... | collective-permute-start | bytes 98312 | tf_op jit(solution)/shard_map/ppermute | solution.py:371
  9.2 1.8 %collective-permute-start.2 = (f32[2,4,8,128]{3,2,1,0:T(8,128)S(1)}, f32[2,4,8,128]{3,2,1,0:T(8,128)S(1)}, u32[]{:S(2)}, u32[]{:S(2)}) collective-permute-start(f32[2,4,8,128]{3,2,1,0:T(8,128)S(1)} %get-tuple-element.34.refs_0_), channel_id=1, source_target_pairs={{0,16},{8,24},{16,0},{24,8},{1,17},{9,25},{17,1},{25,9},{2,18},{10... | collective-permute-start | bytes 98312 | tf_op jit(solution)/shard_map/ppermute | solution.py:371
  11.0 0.0 collective-permute-start.1
  11.1 0.0 copy-start
  11.1 0.0 copy-start.1
  11.1 0.0 copy-start.2
  11.1 1.5 %shard_map.89 = (f32[4,256,8,128]{3,2,1,0:T(8,128)S(1)}, f32[4,256,8,128]{3,2,1,0:T(8,128)S(1)}) custom-call(f32[256,8,128]{2,1,0:T(8,128)S(1)} %get-tuple-element.35.far_ref, f32[4,256,8,128]{3,2,1,0:T(8,128)S(1)} %get-tuple-element.36.trans_ref, f32[4,256,8,128]{3,2,1,0:T(8,128)S(1)} %get-tuple-element.32.emit_ref), custom_call_target="tpu_custom_call" | custom-call | flops 5242880 | bytes 1024 | tf_op jit(solution)/shard_map/pallas_call | solution.py:434
  12.6 0.0 collective-permute-done.3.refs_3_
  12.6 0.6 %collective-permute-done.2.refs_2_ = f32[2,4,8,128]{3,2,1,0:T(8,128)S(1)} collective-permute-done((f32[2,4,8,128]{3,2,1,0:T(8,128)S(1)}, f32[2,4,8,128]{3,2,1,0:T(8,128)S(1)}, u32[]{:S(2)}, u32[]{:S(2)}) %collective-permute-start.2) | collective-permute-done | bytes 32800 | tf_op jit(solution)/shard_map/ppermute | solution.py:371
  13.2 0.0 collective-permute-done.1.refs_1_
  13.2 1.9 %collective-permute-start.4 = (f32[1,4,8,128]{3,2,1,0:T(8,128)S(1)}, f32[1,4,8,128]{3,2,1,0:T(8,128)S(1)}, u32[]{:S(2)}, u32[]{:S(2)}) collective-permute-start(f32[1,4,8,128]{3,2,1,0:T(8,128)S(1)} %get-tuple-element.40.own_ref.refs_0_), channel_id=1, source_target_pairs={{0,1},{1,0},{2,3},{3,2},{4,5},{5,4},{6,7},{7,6},{8,9},{9,8},{10,11... | collective-permute-start | bytes 49160 | tf_op jit(solution)/shard_map/ppermute | solution.py:371
  15.2 1.9 %collective-permute-done.4.refs_0_.refs_1_ = f32[1,4,8,128]{3,2,1,0:T(8,128)S(1)} collective-permute-done((f32[1,4,8,128]{3,2,1,0:T(8,128)S(1)}, f32[1,4,8,128]{3,2,1,0:T(8,128)S(1)}, u32[]{:S(2)}, u32[]{:S(2)}) %collective-permute-start.4) | collective-permute-done | bytes 16416 | tf_op jit(solution)/shard_map/ppermute | solution.py:371
  17.0 2.9 %collective-permute-start.7 = (f32[2,4,8,128]{3,2,1,0:T(8,128)S(1)}, f32[2,4,8,128]{3,2,1,0:T(8,128)S(1)}, u32[]{:S(2)}, u32[]{:S(2)}) collective-permute-start(f32[2,4,8,128]{3,2,1,0:T(8,128)S(1)} %pad_maximum_fusion), channel_id=1, source_target_pairs={{0,2},{1,3},{2,0},{3,1},{4,6},{5,7},{6,4},{7,5},{8,10},{9,11},{10,... | collective-permute-start | bytes 98312 | tf_op jit(solution)/shard_map/ppermute | solution.py:371
  19.9 1.5 %collective-permute-start.5 = (f32[1,4,8,128]{3,2,1,0:T(8,128)S(1)}, f32[1,4,8,128]{3,2,1,0:T(8,128)S(1)}, u32[]{:S(2)}, u32[]{:S(2)}) collective-permute-start(f32[1,4,8,128]{3,2,1,0:T(8,128)S(1)} %get-tuple-element.40.own_ref.refs_0_), channel_id=1, source_target_pairs={{0,16},{1,2},{2,1},{3,19},{8,24},{9,10},{10,9},{11,27},{16,0},{17,... | collective-permute-start | bytes 49160 | tf_op jit(solution)/shard_map/ppermute | solution.py:449
  21.4 0.0 copy-done
  21.4 0.0 copy-done.1
  21.4 0.0 copy-done.2
  21.4 0.4 %shard_map.91 = (f32[8,24]{1,0:T(8,128)S(1)}, f32[4,8,128]{2,1,0:T(8,128)S(1)}, f32[256,32]{1,0:T(8,128)S(1)}) custom-call(s32[1,256]{1,0:T(1,128)S(1)} %bitcast.3, s32[4,256]{1,0:T(4,128)S(1)} %bitcast.2, f32[4,256,128]{2,1,0:T(8,128)S(1)} %copy-done, f32[1,4,8,128]{3,2,1,0:T(8,128)S(1)} %get-tuple-element.40.own_ref.refs_0_), custom_call_target="tpu_custom_call" | custom-call | flops 8388608 | bytes 524288 | tf_op jit(solution)/shard_map/pallas_call | solution.py:460
  21.8 1.9 %collective-permute-done.5.refs_1_ = f32[1,4,8,128]{3,2,1,0:T(8,128)S(1)} collective-permute-done((f32[1,4,8,128]{3,2,1,0:T(8,128)S(1)}, f32[1,4,8,128]{3,2,1,0:T(8,128)S(1)}, u32[]{:S(2)}, u32[]{:S(2)}) %collective-permute-start.5) | collective-permute-done | bytes 16416 | tf_op jit(solution)/shard_map/ppermute | solution.py:449
  23.7 0.6 %shard_map.92 = (f32[256,8,128]{2,1,0:T(8,128)S(1)}, f32[8,256]{1,0:T(8,128)S(1)}, f32[4,8,128]{2,1,0:T(8,128)S(1)}, f32[4,8,128]{2,1,0:T(8,128)S(1)}) custom-call(f32[20,8,128]{2,1,0:T(8,128)S(1)} %get-tuple-element.27.plane_ref, f32[8,24]{1,0:T(8,128)S(1)} %get-tuple-element.41.gram_ref, f32[4,8,128]{2,1,0:T(8,128)S(1)} %get-tuple-element.42.pull_ref, ...), custom_call_target="tpu_custom_call" | custom-call | flops 2621440 | bytes 1024 | tf_op jit(solution)/shard_map/pallas_call | solution.py:465
  24.3 1.6 %collective-permute-start.6 = (f32[8,256]{1,0:T(8,128)S(1)}, f32[8,256]{1,0:T(8,128)S(1)}, u32[]{:S(2)}, u32[]{:S(2)}) collective-permute-start(f32[8,256]{1,0:T(8,128)S(1)} %get-tuple-element.46), channel_id=1, source_target_pairs={{0,4},{4,0},{1,5},{5,1},{2,6},{6,2},{3,7},{7,3},{8,12},{12,8},{9,1... | collective-permute-start | bytes 24584 | tf_op jit(solution)/shard_map/ppermute | solution.py:371
  25.9 1.2 %shard_map.93.mix_ref = f32[4,256,8,128]{3,2,1,0:T(8,128)S(1)} custom-call(f32[20,8,128]{2,1,0:T(8,128)S(1)} %get-tuple-element.27.plane_ref, f32[4,8,128]{2,1,0:T(8,128)S(1)} %get-tuple-element.48.gain_ref, f32[4,8,128]{2,1,0:T(8,128)S(1)} %get-tuple-element.49.shift_ref, f32[4,256,8,128]{3,2,1,0:T(8,128)S(1)} %get-tuple-element.50.rest_ref), custom_call_target="tpu_custom_call" | custom-call | flops 10485760 | bytes 1024 | tf_op jit(solution)/shard_map/pallas_call | solution.py:476
  27.1 1.0 %collective-permute-done.6.nearer_ref = f32[8,256]{1,0:T(8,128)S(1)} collective-permute-done((f32[8,256]{1,0:T(8,128)S(1)}, f32[8,256]{1,0:T(8,128)S(1)}, u32[]{:S(2)}, u32[]{:S(2)}) %collective-permute-start.6) | collective-permute-done | bytes 8224 | tf_op jit(solution)/shard_map/ppermute | solution.py:371
  28.0 0.0 collective-permute-done.7.refs_2_
  28.0 2.3 %shard_map.94 = (f32[4,8,256,128]{3,2,1,0:T(8,128)}, f32[4,16,128]{2,1,0:T(8,128)}) custom-call(f32[20,8,128]{2,1,0:T(8,128)S(1)} %get-tuple-element.27.plane_ref, f32[8,256]{1,0:T(8,128)S(1)} %collective-permute-done.6.nearer_ref, f32[256,8,128]{2,1,0:T(8,128)S(1)} %get-tuple-element.47.near_ref, f32[4,256,8,128]{3,2,1,0:T(8,128)S(1)} %shard_map.93.mix_ref, ...), custom_call_target="tpu_custom_call" | custom-call | flops 2621440 | bytes 4194304 | tf_op jit(solution)/shard_map/pallas_call | solution.py:483
  (2 shorter events, 0.0 us)
Async XLA Ops:
  3.6 4.7 %collective-permute-start = (f32[8,256]{1,0:T(8,128)S(1)}, f32[8,256]{1,0:T(8,128)S(1)}, u32[]{:S(2)}, u32[]{:S(2)}) collective-permute-start(f32[8,256]{1,0:T(8,128)S(1)} %get-tuple-element.28), channel_id=1, source_target_pairs={{0,4},{4,0},{1,5},{5,1},{2,6},{6,2},{3,7},{7,3},{8,12},{12,8},{9,1... | collective-permute-start | bytes 24584 | tf_op jit(solution)/shard_map/ppermute | solution.py:371
  8.9 3.7 %collective-permute-start.3 = (f32[2,4,8,128]{3,2,1,0:T(8,128)S(1)}, f32[2,4,8,128]{3,2,1,0:T(8,128)S(1)}, u32[]{:S(2)}, u32[]{:S(2)}) collective-permute-start(f32[2,4,8,128]{3,2,1,0:T(8,128)S(1)} %get-tuple-element.34.refs_0_), channel_id=1, source_target_pairs={{0,24},{8,16},{16,8},{24,0},{1,25},{9,17},{17,9},{25,1},{2,26},{10... | collective-permute-start | bytes 98312 | tf_op jit(solution)/shard_map/ppermute | solution.py:371
  9.2 4.0 %collective-permute-start.2 = (f32[2,4,8,128]{3,2,1,0:T(8,128)S(1)}, f32[2,4,8,128]{3,2,1,0:T(8,128)S(1)}, u32[]{:S(2)}, u32[]{:S(2)}) collective-permute-start(f32[2,4,8,128]{3,2,1,0:T(8,128)S(1)} %get-tuple-element.34.refs_0_), channel_id=1, source_target_pairs={{0,16},{8,24},{16,0},{24,8},{1,17},{9,25},{17,1},{25,9},{2,18},{10... | collective-permute-start | bytes 98312 | tf_op jit(solution)/shard_map/ppermute | solution.py:371
  11.0 2.2 %collective-permute-start.1 = (f32[2,4,8,128]{3,2,1,0:T(8,128)S(1)}, f32[2,4,8,128]{3,2,1,0:T(8,128)S(1)}, u32[]{:S(2)}, u32[]{:S(2)}) collective-permute-start(f32[2,4,8,128]{3,2,1,0:T(8,128)S(1)} %get-tuple-element.34.refs_0_), channel_id=1, source_target_pairs={{0,8},{8,0},{16,24},{24,16},{1,9},{9,1},{17,25},{25,17},{2,10},{10... | collective-permute-start | bytes 98312 | tf_op jit(solution)/shard_map/ppermute | solution.py:371
  11.1 10.4 %copy-start = (f32[4,256,128]{2,1,0:T(8,128)S(1)}, f32[4,256,128]{2,1,0:T(8,128)}, u32[]{:S(2)}) copy-start(f32[4,256,128]{2,1,0:T(8,128)} %measured_ref.3) | copy-start | bytes 1572868
  11.1 10.4 %copy-start.1 = (s32[256,4]{0,1:T(4,128)S(1)}, s32[256,4]{0,1:T(4,128)}, u32[]{:S(2)}) copy-start(s32[256,4]{0,1:T(4,128)} %param.12) | copy-start | bytes 12292
  11.1 10.4 %copy-start.2 = (s32[256]{0:T(256)S(1)}, s32[256]{0:T(256)}, u32[]{:S(2)}) copy-start(s32[256]{0:T(256)} %param.11) | copy-start | bytes 3076
  13.2 3.8 %collective-permute-start.4 = (f32[1,4,8,128]{3,2,1,0:T(8,128)S(1)}, f32[1,4,8,128]{3,2,1,0:T(8,128)S(1)}, u32[]{:S(2)}, u32[]{:S(2)}) collective-permute-start(f32[1,4,8,128]{3,2,1,0:T(8,128)S(1)} %get-tuple-element.40.own_ref.refs_0_), channel_id=1, source_target_pairs={{0,1},{1,0},{2,3},{3,2},{4,5},{5,4},{6,7},{7,6},{8,9},{9,8},{10,11... | collective-permute-start | bytes 49160 | tf_op jit(solution)/shard_map/ppermute | solution.py:371
  17.0 11.0 %collective-permute-start.7 = (f32[2,4,8,128]{3,2,1,0:T(8,128)S(1)}, f32[2,4,8,128]{3,2,1,0:T(8,128)S(1)}, u32[]{:S(2)}, u32[]{:S(2)}) collective-permute-start(f32[2,4,8,128]{3,2,1,0:T(8,128)S(1)} %pad_maximum_fusion), channel_id=1, source_target_pairs={{0,2},{1,3},{2,0},{3,1},{4,6},{5,7},{6,4},{7,5},{8,10},{9,11},{10,... | collective-permute-start | bytes 98312 | tf_op jit(solution)/shard_map/ppermute | solution.py:371
  19.9 3.7 %collective-permute-start.5 = (f32[1,4,8,128]{3,2,1,0:T(8,128)S(1)}, f32[1,4,8,128]{3,2,1,0:T(8,128)S(1)}, u32[]{:S(2)}, u32[]{:S(2)}) collective-permute-start(f32[1,4,8,128]{3,2,1,0:T(8,128)S(1)} %get-tuple-element.40.own_ref.refs_0_), channel_id=1, source_target_pairs={{0,16},{1,2},{2,1},{3,19},{8,24},{9,10},{10,9},{11,27},{16,0},{17,... | collective-permute-start | bytes 49160 | tf_op jit(solution)/shard_map/ppermute | solution.py:449
  24.3 3.7 %collective-permute-start.6 = (f32[8,256]{1,0:T(8,128)S(1)}, f32[8,256]{1,0:T(8,128)S(1)}, u32[]{:S(2)}, u32[]{:S(2)}) collective-permute-start(f32[8,256]{1,0:T(8,128)S(1)} %get-tuple-element.46), channel_id=1, source_target_pairs={{0,4},{4,0},{1,5},{5,1},{2,6},{6,2},{3,7},{7,3},{8,12},{12,8},{9,1... | collective-permute-start | bytes 24584 | tf_op jit(solution)/shard_map/ppermute | solution.py:371

commit v8 on v7

--- a/solution.py
+++ b/solution.py
@@ -73,9 +73,11 @@
 ):
     n_species, depth, rows, width = conc_hbm.shape
     n_early = emit_ref.shape[0]
+    ends = list(range(CHUNK, rows, CHUNK)) + [rows - CHUNK // 2, rows]
+    starts = [0] + ends[:-1]
 
     def copies(chunk):
-        span = pl.ds(chunk * CHUNK, CHUNK)
+        span = pl.ds(starts[chunk], ends[chunk] - starts[chunk])
         return [
             pltpu.make_async_copy(conc_hbm.at[:, z, span, :], conc_ref.at[:, span, z, :], sems.at[chunk])
             for z in range(depth)
@@ -89,7 +91,7 @@
     ]
     for copy in small:
         copy.start()
-    for chunk in range(rows // CHUNK):
+    for chunk in range(len(ends)):
         for copy in copies(chunk):
             copy.start()
     table = lane_sums(width, True)
@@ -102,25 +104,23 @@
     for i, value in enumerate(scalars):
         plane_ref[i] = jnp.full((depth, width), value)
     sigma = [[v * scale_x for v in row] for row in sigma]
-    for part in range(rows // LANES):
-        total = jnp.zeros((depth, LANES), F32)
-        for piece in range(LANES // CHUNK):
-            chunk = part * (LANES // CHUNK) + piece
-            for copy in copies(chunk):
-                copy.wait()
-            absorber = []
-            for q in range(CHUNK):
-                x = chunk * CHUNK + q
-                conc = [conc_ref[s, x] for s in range(n_species)]
-                absorber.append(weighted(line, conc))
-                for e in range(n_early):
-                    emit_ref[e, x] = weighted([sigma[s][e] for s in range(n_species)], conc)
-            sums = jnp.dot(split(jnp.concatenate(absorber, axis=0)), table, preferred_element_type=F32)
-            for q in range(CHUNK):
-                here = sums[q * depth : (q + 1) * depth]
-                beyond_ref[chunk * CHUNK + q] = here[:, :width]
-                total = jnp.where(lane == piece * CHUNK + q, here[:, width : width + LANES], total)
-        total_ref[:, part * LANES : (part + 1) * LANES] = total
+    total = jnp.zeros((depth, LANES), F32)
+    for chunk, (start, end) in enumerate(zip(starts, ends)):
+        for copy in copies(chunk):
+            copy.wait()
+        absorber = []
+        for x in range(start, end):
+            conc = [conc_ref[s, x] for s in range(n_species)]
+            absorber.append(weighted(line, conc))
+            for e in range(n_early):
+                emit_ref[e, x] = weighted([sigma[s][e] for s in range(n_species)], conc)
+        sums = jnp.dot(split(jnp.concatenate(absorber, axis=0)), table, preferred_element_type=F32)
+        for q, x in enumerate(range(start, end)):
+            here = sums[q * depth : (q + 1) * depth]
+            beyond_ref[x] = here[:, :width]
+            total = jnp.where(lane == x % LANES, here[:, width : width + LANES], total)
+        if end % LANES == 0:
+            total_ref[:, end - LANES : end] = total
 
 
 def local_body(scale, plane_ref, conc_ref, early_ref, beyond_ref, trans_ref, emit_ref, depth_ref):
@@ -266,9 +266,9 @@
     return [a + b for a, b in sums]
 
 
-def back_body(scale, plane_ref, gram_ref, pull_ref, up_ref, further_ref, fluor_ref, *refs):
+def back_body(scale, count, plane_ref, gram_ref, pull_ref, up_ref, further_ref, fluor_ref, *refs):
     lines, (near_ref, total_ref, gain_ref, shift_ref) = refs[:-4], refs[-4:]
-    n_energy, rows, depth, width = fluor_ref.shape
+    n_energy, _, depth, width = fluor_ref.shape
     n_species = shift_ref.shape[0]
     sums = weigh(gram_ref[...], [(r + 1, ref, 0) for r, ref in enumerate(lines)], depth, n_energy, width)
     back = [sums[e] * scale + pull_ref[e] for e in range(n_energy)]
@@ -279,22 +279,36 @@
         gain_ref[e] = gain[e]
     for s in range(n_species):
         shift_ref[s] = weighted(sigma[s], pushed)
+    last = lax.axis_index("det") == count - 1
+
+    @pl.when(jnp.logical_not(last))
+    def _():
+        column_sums(gain, fluor_ref, near_ref, total_ref)
+
+    @pl.when(last)
+    def _():
+        total_ref[...] = jnp.zeros_like(total_ref)
+
+
+def column_sums(gain, fluor_ref, near_ref, total_ref):
+    n_energy, rows, depth, width = fluor_ref.shape
     table = lane_sums(width, False)
     lane = lax.broadcasted_iota(jnp.int32, (depth, LANES), 1)
-    for part in range(rows // LANES):
-        total = jnp.zeros((depth, LANES), F32)
-        for piece in range(LANES // CHUNK):
-            first = part * LANES + piece * CHUNK
-            heavy = [weighted(gain, [fluor_ref[e, first + q] for e in range(n_energy)]) for q in range(CHUNK)]
-            found = jnp.dot(split(jnp.concatenate(heavy, axis=0)), table, preferred_element_type=F32)
-            for q in range(CHUNK):
-                here = found[q * depth : (q + 1) * depth]
-                near_ref[first + q] = here[:, :width]
-                total = jnp.where(lane == piece * CHUNK + q, here[:, width : width + LANES], total)
-        total_ref[:, part * LANES : (part + 1) * LANES] = total
-
-
-def mix_body(plane_ref, gain_ref, shift_ref, rest_ref, out_ref):
+    total = jnp.zeros((depth, LANES), F32)
+    for start in range(0, rows, CHUNK):
+        span = range(start, start + CHUNK)
+        heavy = [weighted(gain, [fluor_ref[e, x] for e in range(n_energy)]) for x in span]
+        found = jnp.dot(split(jnp.concatenate(heavy, axis=0)), table, preferred_element_type=F32)
+        for q, x in enumerate(span):
+            here = found[q * depth : (q + 1) * depth]
+            near_ref[x] = here[:, :width]
+            if total_ref is not None:
+                total = jnp.where(lane == x % LANES, here[:, width : width + LANES], total)
+        if total_ref is not None and (start + CHUNK) % LANES == 0:
+            total_ref[:, start + CHUNK - LANES : start + CHUNK] = total
+
+
+def mix_body(count, plane_ref, gain_ref, shift_ref, rest_ref, fluor_ref, out_ref, near_ref):
     n_energy, rows, _, _ = rest_ref.shape
     n_species = out_ref.shape[0]
     sigma, _ = planes(plane_ref, n_species, n_energy)
@@ -311,15 +325,20 @@
 
     lax.fori_loop(0, rows // STEP, step, 0)
 
+    @pl.when(lax.axis_index("det") == count - 1)
+    def _():
+        column_sums([gain_ref[e] for e in range(n_energy)], fluor_ref, near_ref, None)
+
 
 def finish_body(
-    scale, scale_line, count, plane_ref, nearer_ref, near_ref, mix_ref, fan_ref, measured_ref, *refs
+    scale, scale_line, count, plane_ref, nearer_ref, near_ref, last_ref, mix_ref, fan_ref, measured_ref, *refs
 ):
     lines, (grad_hbm, residual_hbm, grad_ref, residual_ref, sems, residual_sem) = refs[:-6], refs[-6:]
     n_species, rows, depth, width = mix_ref.shape
     n_energy, share, _ = residual_ref.shape
     line = [v * scale_line for v in planes(plane_ref, n_species, n_energy)[1]]
     keep = jnp.where(reached("det", count, True), 1.0, 0.0)
+    last = lax.axis_index("det") == count - 1
 
     ends = [8, 16] + list(range(CHUNK, rows + 1, CHUNK))
 
@@ -332,7 +351,7 @@
         ]
 
     for x, column in columns(nearer_ref, lambda v: v * keep, width):
-        before = near_ref[x] + column
+        before = jnp.where(last, last_ref[x], near_ref[x]) + column
         for s in range(n_species):
             grad_ref[s, x] = mix_ref[s, x] + line[s] * before
         if x + 1 in ends:
@@ -362,7 +381,7 @@
             if 0 <= other < n_slab:
                 target = beam * n_slab + other
             else:
-                target = (beam ^ (n_beam // 2)) * n_slab + slab
+                target = (beam ^ 1) * n_slab + slab
             pairs.append((beam * n_slab + slab, target))
     return pairs
 
@@ -398,7 +417,7 @@
     cube = VMEM((n_energy, rows, depth, width), F32)
     plane = VMEM((rows, depth, width), F32)
 
-    n_early = n_energy // 2
+    n_early = (n_energy + 3) // 4
     conc_x, emission, far_local, row_total, fixed = call(
         functools.partial(load_body, scale_y, scale_x),
         (VMEM(turned, F32), VMEM((n_early, rows, depth, width), F32), plane, plain(depth, rows),
@@ -410,7 +429,7 @@
             SMEM(cross.shape, F32),
             SMEM(index.shape, index.dtype),
             pltpu.SemaphoreType.DMA((3,)),
-            pltpu.SemaphoreType.DMA((rows // CHUNK,)),
+            pltpu.SemaphoreType.DMA((rows // CHUNK + 1,)),
         ],
         cost=(40 * voxels, 0, 16 * voxels),
     )(*(pltpu.with_memory_space_constraint(v, HBM) for v in (line, cross, index, conc)))
@@ -463,7 +482,7 @@
     )(fan_offset[None, :], fan_weight.T, measured, total)
 
     near, column_total, gain, shift = call(
-        functools.partial(back_body, scale_sum),
+        functools.partial(back_body, scale_sum, n_det),
         (plane, plain(depth, rows), plain(*wide), plain(n_species, depth, width)),
         (VMEM,) * 4,
         (VMEM,) * (5 + len(near_lines)),
@@ -473,10 +492,10 @@
     nearer = beyond(column_total, "det", True)
 
     scale_line = scale_y * LN2 / scale_x
-    mixed = call(
-        mix_body, (VMEM(turned, F32),), (VMEM,), (VMEM,) * 4,
+    mixed, near_last = call(
+        functools.partial(mix_body, n_det), (VMEM(turned, F32), plane), (VMEM,) * 2, (VMEM,) * 5,
         cost=(40 * voxels, 0, 1024),
-    )(fixed, gain, shift, rest)[0]
+    )(fixed, gain, shift, rest, fluor)
 
     share = pixels // (n_beam * n_slab)
     return tuple(
@@ -484,7 +503,7 @@
             functools.partial(finish_body, scale_sum, scale_line, n_det),
             (plain(*conc.shape), plain(n_energy, share, width)),
             (HBM, HBM),
-            (VMEM,) * (6 + len(lines)),
+            (VMEM,) * (7 + len(lines)),
             [
                 VMEM(turned, F32),
                 VMEM((n_energy, share, width), F32),
@@ -493,7 +512,7 @@
             ],
             limit=16,
             cost=(10 * voxels, 0, 16 * voxels),
-        )(fixed, nearer, near, mixed, fan_turned, measured, *lines)
+        )(fixed, nearer, near, near_last, mixed, fan_turned, measured, *lines)
     )
 
 

time: 30.5 us -> 29.1 us (0.954)
  the two profiles are of different devices: /device:TPU:0 before, /device:TPU:10 now
where the time goes in v8:
time: 29.1 us; the launch traced here: 28.9 us
  Pallas kernels  11 us (38%)
  waiting for transfers between devices  9.52 us (33%)
  starting transfers between devices  7.66 us (26%)
  between operations  0.71 us (2%)
    ppermute x7, starting transfers between devices, swap(): lax.ppermute(value, axis, [(i, i ^ distance) for i in range(lax.axis_size...  7.66 us
    ppermute x7, waiting for transfers between devices, swap(): lax.ppermute(value, axis, [(i, i ^ distance) for i in range(lax.axis_size...  6.16 us
    ppermute x1, waiting for transfers between devices, shards(): odd = lax.ppermute(total, ('beam', 'slab'), odd_pairs(n_beam, n_slab))  3.35 us
    pallas_call x1, Pallas kernels, shards(): call(functools.partial(load_body, scale_y, scale_x), (VMEM(turned, F32),...  3.06 us
    pallas_call x1, Pallas kernels, shards(): call(functools.partial(finish_body, scale_sum, scale_line, n_det), (plain...  2.29 us
    pallas_call x1, Pallas kernels, shards(): call(ahead_body, (cube, cube), (VMEM, VMEM), (VMEM, VMEM, VMEM), cost=(20...  1.51 us
    pallas_call x1, Pallas kernels, shards(): call(functools.partial(local_body, scale_x), (cube, cube, plain(n_energy,...  1.39 us
    pallas_call x1, Pallas kernels, shards(): call(functools.partial(mix_body, n_det), (VMEM(turned, F32), plane), (VME...  1.18 us
  transfers between devices with their start and end apart: 8, of which 5 were waited for; matrix products, arithmetic and copies ran while one was open for 0% of the time, Pallas kernels for 18%

profile of v8, /device:TPU:10, one launch (start us, length us, event | category | flops | bytes accessed | tf_op | source)
XLA Modules:
  0.0 28.9 jit_solution(733787346239349071)
XLA Ops:
  0.6 3.1 %shard_map.86 = (f32[4,256,8,128]{3,2,1,0:T(8,128)S(1)}, f32[1,256,8,128]{3,2,1,0:T(8,128)S(1)}, f32[256,8,128]{2,1,0:T(8,128)S(1)}, f32[8,256]{1,0:T(8,128)S(1)}, f32[20,8,128]{2,1,0:T(8,128)S(1)}) custom-call(f32[4]{0:T(128)} %line_hbm.1, f32[4,16]{1,0:T(4,128)} %cross_hbm.1, s32[4]{0:T(128)} %index_hbm.1, f32[4,8,256,128]{3,2,1,0:T(8,128)} %conc_hbm.1), custom_call_target="tpu_custom_call" | custom-call | flops 10485760 | bytes 4194304 | tf_op jit(solution)/shard_map/pallas_call | solution.py:421
  3.7 1.6 %collective-permute-start = (f32[8,256]{1,0:T(8,128)S(1)}, f32[8,256]{1,0:T(8,128)S(1)}, u32[]{:S(2)}, u32[]{:S(2)}) collective-permute-start(f32[8,256]{1,0:T(8,128)S(1)} %get-tuple-element.30), channel_id=1, source_target_pairs={{0,4},{4,0},{1,5},{5,1},{2,6},{6,2},{3,7},{7,3},{8,12},{12,8},{9,1... | collective-permute-start | bytes 24584 | tf_op jit(solution)/shard_map/ppermute | solution.py:390
  5.3 1.4 %shard_map.87 = (f32[4,256,8,128]{3,2,1,0:T(8,128)S(1)}, f32[4,256,8,128]{3,2,1,0:T(8,128)S(1)}, f32[4,8,128]{2,1,0:T(8,128)S(1)}) custom-call(f32[20,8,128]{2,1,0:T(8,128)S(1)} %get-tuple-element.29.plane_ref, f32[4,256,8,128]{3,2,1,0:T(8,128)S(1)} %get-tuple-element.31.conc_ref, f32[1,256,8,128]{3,2,1,0:T(8,128)S(1)} %get-tuple-element.32.early_ref, ...), custom_call_target="tpu_custom_call" | custom-call | flops 5242880 | bytes 1024 | tf_op jit(solution)/shard_map/pallas_call | solution.py:439
  6.7 0.7 %collective-permute-done.far_ref = f32[8,256]{1,0:T(8,128)S(1)} collective-permute-done((f32[8,256]{1,0:T(8,128)S(1)}, f32[8,256]{1,0:T(8,128)S(1)}, u32[]{:S(2)}, u32[]{:S(2)}) %collective-permute-start) | collective-permute-done | bytes 8224 | tf_op jit(solution)/shard_map/ppermute | solution.py:390
  7.4 0.6 %shard_map.88 = (f32[256,8,128]{2,1,0:T(8,128)S(1)}, f32[2,4,8,128]{3,2,1,0:T(8,128)S(1)}) custom-call(f32[8,256]{1,0:T(8,128)S(1)} %collective-permute-done.far_ref, f32[4,256,8,128]{3,2,1,0:T(8,128)S(1)} %get-tuple-element.34.emit_ref, f32[4,8,128]{2,1,0:T(8,128)S(1)} %get-tuple-element.35.depth_ref), custom_call_target="tpu_custom_call" | custom-call | flops 2097152 | bytes 1024 | tf_op jit(solution)/shard_map/pallas_call | solution.py:448
  8.0 0.1 collective-permute-start.3
  8.1 0.6 %collective-permute-start.2 = (f32[2,4,8,128]{3,2,1,0:T(8,128)S(1)}, f32[2,4,8,128]{3,2,1,0:T(8,128)S(1)}, u32[]{:S(2)}, u32[]{:S(2)}) collective-permute-start(f32[2,4,8,128]{3,2,1,0:T(8,128)S(1)} %get-tuple-element.36.refs_0_), channel_id=1, source_target_pairs={{0,16},{8,24},{16,0},{24,8},{1,17},{9,25},{17,1},{25,9},{2,18},{10... | collective-permute-start | bytes 98312 | tf_op jit(solution)/shard_map/ppermute | solution.py:390
  8.7 1.2 %collective-permute-start.1 = (f32[2,4,8,128]{3,2,1,0:T(8,128)S(1)}, f32[2,4,8,128]{3,2,1,0:T(8,128)S(1)}, u32[]{:S(2)}, u32[]{:S(2)}) collective-permute-start(f32[2,4,8,128]{3,2,1,0:T(8,128)S(1)} %get-tuple-element.36.refs_0_), channel_id=1, source_target_pairs={{0,8},{8,0},{16,24},{24,16},{1,9},{9,1},{17,25},{25,17},{2,10},{10... | collective-permute-start | bytes 98312 | tf_op jit(solution)/shard_map/ppermute | solution.py:390
  9.9 0.0 copy-start
  9.9 0.0 copy-start.1
  9.9 0.0 copy-start.2
  9.9 1.5 %shard_map.89 = (f32[4,256,8,128]{3,2,1,0:T(8,128)S(1)}, f32[4,256,8,128]{3,2,1,0:T(8,128)S(1)}) custom-call(f32[256,8,128]{2,1,0:T(8,128)S(1)} %get-tuple-element.37.far_ref, f32[4,256,8,128]{3,2,1,0:T(8,128)S(1)} %get-tuple-element.38.trans_ref, f32[4,256,8,128]{3,2,1,0:T(8,128)S(1)} %get-tuple-element.34.emit_ref), custom_call_target="tpu_custom_call" | custom-call | flops 5242880 | bytes 1024 | tf_op jit(solution)/shard_map/pallas_call | solution.py:453
  11.4 0.0 collective-permute-done.3.refs_3_
  11.4 0.7 %collective-permute-done.2.refs_2_ = f32[2,4,8,128]{3,2,1,0:T(8,128)S(1)} collective-permute-done((f32[2,4,8,128]{3,2,1,0:T(8,128)S(1)}, f32[2,4,8,128]{3,2,1,0:T(8,128)S(1)}, u32[]{:S(2)}, u32[]{:S(2)}) %collective-permute-start.2) | collective-permute-done | bytes 32800 | tf_op jit(solution)/shard_map/ppermute | solution.py:390
  12.1 0.0 collective-permute-done.1.refs_1_
  12.1 0.5 %collective-permute-start.4 = (f32[1,4,8,128]{3,2,1,0:T(8,128)S(1)}, f32[1,4,8,128]{3,2,1,0:T(8,128)S(1)}, u32[]{:S(2)}, u32[]{:S(2)}) collective-permute-start(f32[1,4,8,128]{3,2,1,0:T(8,128)S(1)} %get-tuple-element.42.own_ref.refs_0_), channel_id=1, source_target_pairs={{0,1},{1,0},{2,3},{3,2},{4,5},{5,4},{6,7},{7,6},{8,9},{9,8},{10,11... | collective-permute-start | bytes 49160 | tf_op jit(solution)/shard_map/ppermute | solution.py:390
  12.6 3.3 %collective-permute-done.4.refs_0_.refs_1_ = f32[1,4,8,128]{3,2,1,0:T(8,128)S(1)} collective-permute-done((f32[1,4,8,128]{3,2,1,0:T(8,128)S(1)}, f32[1,4,8,128]{3,2,1,0:T(8,128)S(1)}, u32[]{:S(2)}, u32[]{:S(2)}) %collective-permute-start.4) | collective-permute-done | bytes 16416 | tf_op jit(solution)/shard_map/ppermute | solution.py:390
  15.9 2.6 %collective-permute-start.7 = (f32[2,4,8,128]{3,2,1,0:T(8,128)S(1)}, f32[2,4,8,128]{3,2,1,0:T(8,128)S(1)}, u32[]{:S(2)}, u32[]{:S(2)}) collective-permute-start(f32[2,4,8,128]{3,2,1,0:T(8,128)S(1)} %pad_maximum_fusion), channel_id=1, source_target_pairs={{0,2},{1,3},{2,0},{3,1},{4,6},{5,7},{6,4},{7,5},{8,10},{9,11},{10,... | collective-permute-start | bytes 98312 | tf_op jit(solution)/shard_map/ppermute | solution.py:390
  18.5 0.0 collective-permute-start.5
  18.5 0.0 copy-done
  18.5 0.0 copy-done.1
  18.5 0.0 copy-done.2
  18.5 0.4 %shard_map.91 = (f32[8,24]{1,0:T(8,128)S(1)}, f32[4,8,128]{2,1,0:T(8,128)S(1)}, f32[256,32]{1,0:T(8,128)S(1)}) custom-call(s32[1,256]{1,0:T(1,128)S(1)} %bitcast.3, s32[4,256]{1,0:T(4,128)S(1)} %bitcast.2, f32[4,256,128]{2,1,0:T(8,128)S(1)} %copy-done, f32[1,4,8,128]{3,2,1,0:T(8,128)S(1)} %get-tuple-element.42.own_ref.refs_0_), custom_call_target="tpu_custom_call" | custom-call | flops 8388608 | bytes 524288 | tf_op jit(solution)/shard_map/pallas_call | solution.py:479
  18.9 3.4 %collective-permute-done.5.refs_1_ = f32[1,4,8,128]{3,2,1,0:T(8,128)S(1)} collective-permute-done((f32[1,4,8,128]{3,2,1,0:T(8,128)S(1)}, f32[1,4,8,128]{3,2,1,0:T(8,128)S(1)}, u32[]{:S(2)}, u32[]{:S(2)}) %collective-permute-start.5) | collective-permute-done | bytes 16416 | tf_op jit(solution)/shard_map/ppermute | solution.py:468
  22.3 0.6 %shard_map.92 = (f32[256,8,128]{2,1,0:T(8,128)S(1)}, f32[8,256]{1,0:T(8,128)S(1)}, f32[4,8,128]{2,1,0:T(8,128)S(1)}, f32[4,8,128]{2,1,0:T(8,128)S(1)}) custom-call(f32[20,8,128]{2,1,0:T(8,128)S(1)} %get-tuple-element.29.plane_ref, f32[8,24]{1,0:T(8,128)S(1)} %get-tuple-element.43.gram_ref, f32[4,8,128]{2,1,0:T(8,128)S(1)} %get-tuple-element.44.pull_ref, ...), custom_call_target="tpu_custom_call" | custom-call | flops 2621440 | bytes 1024 | tf_op jit(solution)/shard_map/pallas_call | solution.py:484
  22.9 1.0 %collective-permute-start.6 = (f32[8,256]{1,0:T(8,128)S(1)}, f32[8,256]{1,0:T(8,128)S(1)}, u32[]{:S(2)}, u32[]{:S(2)}) collective-permute-start(f32[8,256]{1,0:T(8,128)S(1)} %get-tuple-element.48), channel_id=1, source_target_pairs={{0,4},{4,0},{1,5},{5,1},{2,6},{6,2},{3,7},{7,3},{8,12},{12,8},{9,1... | collective-permute-start | bytes 24584 | tf_op jit(solution)/shard_map/ppermute | solution.py:390
  24.0 1.2 %shard_map.93 = (f32[4,256,8,128]{3,2,1,0:T(8,128)S(1)}, f32[256,8,128]{2,1,0:T(8,128)S(1)}) custom-call(f32[20,8,128]{2,1,0:T(8,128)S(1)} %get-tuple-element.29.plane_ref, f32[4,8,128]{2,1,0:T(8,128)S(1)} %get-tuple-element.50.gain_ref, f32[4,8,128]{2,1,0:T(8,128)S(1)} %get-tuple-element.51.shift_ref, f32[4,256,8,128]{3,2,1,0:T(8,128)S(1)} %get-tuple-element.52.rest_ref, ...), custom_call_target="tpu_custom_call" | custom-call | flops 10485760 | bytes 1024 | tf_op jit(solution)/shard_map/pallas_call | solution.py:495
  25.1 1.5 %collective-permute-done.6.nearer_ref = f32[8,256]{1,0:T(8,128)S(1)} collective-permute-done((f32[8,256]{1,0:T(8,128)S(1)}, f32[8,256]{1,0:T(8,128)S(1)}, u32[]{:S(2)}, u32[]{:S(2)}) %collective-permute-start.6) | collective-permute-done | bytes 8224 | tf_op jit(solution)/shard_map/ppermute | solution.py:390
  26.6 0.0 collective-permute-done.7.refs_2_
  26.6 2.3 %shard_map.94 = (f32[4,8,256,128]{3,2,1,0:T(8,128)}, f32[4,16,128]{2,1,0:T(8,128)}) custom-call(f32[20,8,128]{2,1,0:T(8,128)S(1)} %get-tuple-element.29.plane_ref, f32[8,256]{1,0:T(8,128)S(1)} %collective-permute-done.6.nearer_ref, f32[256,8,128]{2,1,0:T(8,128)S(1)} %get-tuple-element.49.near_ref, f32[256,8,128]{2,1,0:T(8,128)S(1)} %get-tuple-element.53.last_ref, ...), custom_call_target="tpu_custom_call" | custom-call | flops 2621440 | bytes 4194304 | tf_op jit(solution)/shard_map/pallas_call | solution.py:502
  (2 shorter events, 0.0 us)
Async XLA Ops:
  3.7 3.7 %collective-permute-start = (f32[8,256]{1,0:T(8,128)S(1)}, f32[8,256]{1,0:T(8,128)S(1)}, u32[]{:S(2)}, u32[]{:S(2)}) collective-permute-start(f32[8,256]{1,0:T(8,128)S(1)} %get-tuple-element.30), channel_id=1, source_target_pairs={{0,4},{4,0},{1,5},{5,1},{2,6},{6,2},{3,7},{7,3},{8,12},{12,8},{9,1... | collective-permute-start | bytes 24584 | tf_op jit(solution)/shard_map/ppermute | solution.py:390
  8.0 3.4 %collective-permute-start.3 = (f32[2,4,8,128]{3,2,1,0:T(8,128)S(1)}, f32[2,4,8,128]{3,2,1,0:T(8,128)S(1)}, u32[]{:S(2)}, u32[]{:S(2)}) collective-permute-start(f32[2,4,8,128]{3,2,1,0:T(8,128)S(1)} %get-tuple-element.36.refs_0_), channel_id=1, source_target_pairs={{0,24},{8,16},{16,8},{24,0},{1,25},{9,17},{17,9},{25,1},{2,26},{10... | collective-permute-start | bytes 98312 | tf_op jit(solution)/shard_map/ppermute | solution.py:390
  8.1 4.0 %collective-permute-start.2 = (f32[2,4,8,128]{3,2,1,0:T(8,128)S(1)}, f32[2,4,8,128]{3,2,1,0:T(8,128)S(1)}, u32[]{:S(2)}, u32[]{:S(2)}) collective-permute-start(f32[2,4,8,128]{3,2,1,0:T(8,128)S(1)} %get-tuple-element.36.refs_0_), channel_id=1, source_target_pairs={{0,16},{8,24},{16,0},{24,8},{1,17},{9,25},{17,1},{25,9},{2,18},{10... | collective-permute-start | bytes 98312 | tf_op jit(solution)/shard_map/ppermute | solution.py:390
  8.7 3.4 %collective-permute-start.1 = (f32[2,4,8,128]{3,2,1,0:T(8,128)S(1)}, f32[2,4,8,128]{3,2,1,0:T(8,128)S(1)}, u32[]{:S(2)}, u32[]{:S(2)}) collective-permute-start(f32[2,4,8,128]{3,2,1,0:T(8,128)S(1)} %get-tuple-element.36.refs_0_), channel_id=1, source_target_pairs={{0,8},{8,0},{16,24},{24,16},{1,9},{9,1},{17,25},{25,17},{2,10},{10... | collective-permute-start | bytes 98312 | tf_op jit(solution)/shard_map/ppermute | solution.py:390
  9.9 8.6 %copy-start = (f32[4,256,128]{2,1,0:T(8,128)S(1)}, f32[4,256,128]{2,1,0:T(8,128)}, u32[]{:S(2)}) copy-start(f32[4,256,128]{2,1,0:T(8,128)} %measured_ref.3) | copy-start | bytes 1572868
  9.9 8.6 %copy-start.1 = (s32[256,4]{0,1:T(4,128)S(1)}, s32[256,4]{0,1:T(4,128)}, u32[]{:S(2)}) copy-start(s32[256,4]{0,1:T(4,128)} %param.12) | copy-start | bytes 12292
  9.9 8.6 %copy-start.2 = (s32[256]{0:T(256)S(1)}, s32[256]{0:T(256)}, u32[]{:S(2)}) copy-start(s32[256]{0:T(256)} %param.11) | copy-start | bytes 3076
  12.1 3.8 %collective-permute-start.4 = (f32[1,4,8,128]{3,2,1,0:T(8,128)S(1)}, f32[1,4,8,128]{3,2,1,0:T(8,128)S(1)}, u32[]{:S(2)}, u32[]{:S(2)}) collective-permute-start(f32[1,4,8,128]{3,2,1,0:T(8,128)S(1)} %get-tuple-element.42.own_ref.refs_0_), channel_id=1, source_target_pairs={{0,1},{1,0},{2,3},{3,2},{4,5},{5,4},{6,7},{7,6},{8,9},{9,8},{10,11... | collective-permute-start | bytes 49160 | tf_op jit(solution)/shard_map/ppermute | solution.py:390
  15.9 10.7 %collective-permute-start.7 = (f32[2,4,8,128]{3,2,1,0:T(8,128)S(1)}, f32[2,4,8,128]{3,2,1,0:T(8,128)S(1)}, u32[]{:S(2)}, u32[]{:S(2)}) collective-permute-start(f32[2,4,8,128]{3,2,1,0:T(8,128)S(1)} %pad_maximum_fusion), channel_id=1, source_target_pairs={{0,2},{1,3},{2,0},{3,1},{4,6},{5,7},{6,4},{7,5},{8,10},{9,11},{10,... | collective-permute-start | bytes 98312 | tf_op jit(solution)/shard_map/ppermute | solution.py:390
  18.5 3.7 %collective-permute-start.5 = (f32[1,4,8,128]{3,2,1,0:T(8,128)S(1)}, f32[1,4,8,128]{3,2,1,0:T(8,128)S(1)}, u32[]{:S(2)}, u32[]{:S(2)}) collective-permute-start(f32[1,4,8,128]{3,2,1,0:T(8,128)S(1)} %get-tuple-element.42.own_ref.refs_0_), channel_id=1, source_target_pairs={{0,8},{1,2},{2,1},{3,11},{8,0},{9,10},{10,9},{11,3},{16,24},{17,18... | collective-permute-start | bytes 49160 | tf_op jit(solution)/shard_map/ppermute | solution.py:468
  22.9 3.7 %collective-permute-start.6 = (f32[8,256]{1,0:T(8,128)S(1)}, f32[8,256]{1,0:T(8,128)S(1)}, u32[]{:S(2)}, u32[]{:S(2)}) collective-permute-start(f32[8,256]{1,0:T(8,128)S(1)} %get-tuple-element.48), channel_id=1, source_target_pairs={{0,4},{4,0},{1,5},{5,1},{2,6},{6,2},{3,7},{7,3},{8,12},{12,8},{9,1... | collective-permute-start | bytes 24584 | tf_op jit(solution)/shard_map/ppermute | solution.py:390
